TPU v7x, 32 devices: a whole 2x2x4 slice. The times are simulated.
32 devices in a mesh: dp: 8 (over y, x, core), seq: 4 (over z).
Axes of the slice: x: 2, y: 2, z: 4, core: 2. Of those that a mesh axis runs over, the one named last changes fastest.
Arguments:
- inputs: bfloat16 [8, 3, 1024, 1024], P('dp', None, 'seq'), may hold values from -6 to 6
- encoded: bfloat16 [8, 1024, 1024], P('dp', 'seq'), may hold values from -6 to 6
- target_lengths: int32 [8, 4], P('dp'), may hold values from 1 to 512, 960 in all within a row
- source_lengths: int32 [8, 4], P('dp'), may hold values from 1 to 512, 960 in all within a row
- query_key_value: bfloat16 [1024, 3072], replicated, may hold values from -0.1875 to 0.1875
- bucket_weight: bfloat16 [1024, 512], replicated, may hold values from -0.1875 to 0.1875
- self_output: bfloat16 [1024, 1024], replicated, may hold values from -1.5 to 1.5
- cross_query: bfloat16 [1024, 1024], replicated, may hold values from -0.1875 to 0.1875
- cross_key_value: bfloat16 [1024, 2048], replicated, may hold values from -0.1875 to 0.1875
- cross_output: bfloat16 [1024, 1024], replicated, may hold values from -1.5 to 1.5
- up_weight: bfloat16 [1024, 4096], replicated, may hold values from -0.1875 to 0.1875
- up_bias: float32 [4096], replicated, may hold values from -3 to 3
- down_weight: bfloat16 [4096, 1024], replicated, may hold values from -0.09375 to 0.09375
- down_bias: float32 [1024], replicated, may hold values from -2 to 2
- norm_gain: float32 [3, 1024], replicated, may hold values from 0.5 to 1.5
- norm_shift: float32 [3, 1024], replicated, may hold values from -2 to 2
- cotangent: bfloat16 [8, 3, 1024, 1024], P('dp', None, 'seq'), may hold values from -6 to 6
Outputs:
- outputs: bfloat16 [8, 3, 1024, 1024], P('dp', None, 'seq')
- inputs_gradient: bfloat16 [8, 3, 1024, 1024], P('dp', None, 'seq')
- encoded_gradient: bfloat16 [8, 1024, 1024], P('dp', 'seq')
- query_key_value_gradient: float32 [1024, 3072], P(('dp', 'seq'))
- bucket_weight_gradient: float32 [1024, 512], P(('dp', 'seq'))
- self_output_gradient: float32 [1024, 1024], P(('dp', 'seq'))
- cross_query_gradient: float32 [1024, 1024], P(('dp', 'seq'))
- cross_key_value_gradient: float32 [1024, 2048], P(('dp', 'seq'))
- cross_output_gradient: float32 [1024, 1024], P(('dp', 'seq'))
- up_weight_gradient: float32 [1024, 4096], P(('dp', 'seq'))
- up_bias_gradient: float32 [4096], P(('dp', 'seq'))
- down_weight_gradient: float32 [4096, 1024], P(('dp', 'seq'))
- down_bias_gradient: float32 [1024], P(('dp', 'seq'))
- norm_gain_gradient: float32 [3, 1024], P(None, ('dp', 'seq'))
- norm_shift_gradient: float32 [3, 1024], P(None, ('dp', 'seq'))
Inputs may be any that keep to these rules, and one draw needn't show every extreme that they name: `target_lengths`: each row's 4 documents fill its first 960 positions; the rest is padding. `source_lengths`: each row's 4 documents fill its first 960 positions; the rest is padding.
All inputs are finite; a program needn't handle non-finite values.
Results may differ from a plain program's by a relative error of at most 0.025.
Values may be sent and summed in bfloat16 or wider, within the bound.
A program may use at most 960 MiB of HBM per device.

v0:
```python
import math

import jax
import jax.numpy as jnp
from jax import lax
from jax.sharding import PartitionSpec as P

HEADS = 16
HEAD_DIM = 64
BUCKETS = 32


bucket_edges = [
    int(math.ceil(16.0 * 8.0 ** (bucket_level / 16.0))) for bucket_level in range(1, 16)
]


def bucket_of(distance):
    forward_gap = jnp.maximum(distance, 0)
    far_bucket = jnp.full_like(forward_gap, 16)
    for bucket_edge in bucket_edges:
        far_bucket = far_bucket + (forward_gap >= bucket_edge).astype(jnp.int32)
    return jnp.where(forward_gap < 16, forward_gap, far_bucket)


def segment_ids(lengths, positions):
    ends = jnp.cumsum(lengths, axis=1)
    return jnp.sum((positions[None, :, None] >= ends[:, None, :]).astype(jnp.int32), axis=2)


def normalize(hidden, gain, shift):
    centre = hidden - jnp.mean(hidden, axis=-1, keepdims=True)
    scale_inv = lax.rsqrt(jnp.mean(centre * centre, axis=-1, keepdims=True) + 1e-05)
    unit = centre * scale_inv
    return (unit * gain + shift, unit, scale_inv)


def normalize_back(upstream, unit, scale_inv, gain):
    along = upstream * gain
    inner = (
        along
        - jnp.mean(along, axis=-1, keepdims=True)
        - unit * jnp.mean(along * unit, axis=-1, keepdims=True)
    )
    return (scale_inv * inner, jnp.sum(upstream * unit, axis=0), jnp.sum(upstream, axis=0))


def weight_grad(left, right):
    return lax.dot_general(
        left, right, (((0,), (0,)), ((), ())), preferred_element_type=jnp.float32
    )


def input_grad(upstream, weight):
    return lax.dot_general(
        upstream, weight, (((1,), (1,)), ((), ())), preferred_element_type=jnp.float32
    )


def self_scores(
    queries, own_keys, key_rows, table, query_seg, key_seg, query_pos, stream_of, key_pos, onehot
):
    scale = HEAD_DIM ** (-0.5)
    mixed = scale * jnp.einsum(
        "qhd,khd->qhk", queries, key_rows, preferred_element_type=jnp.float32
    )
    bias = jnp.einsum(
        "qhb,qkb->qhk",
        table,
        onehot,
        precision=lax.Precision.HIGHEST,
        preferred_element_type=jnp.float32,
    )
    allowed = (query_seg[:, None] == key_seg[None, :]) & (
        key_pos[None, :] <= query_pos[:, None] - (stream_of[:, None] > 0).astype(jnp.int32)
    )
    scores = jnp.where(allowed[:, None, :], mixed + bias, -1000000000.0)
    own_raw = (
        scale * jnp.sum(queries.astype(jnp.float32) * own_keys.astype(jnp.float32), axis=-1)
        + table[:, :, 0]
    )
    own_score = jnp.where((stream_of > 0)[:, None], own_raw, -1000000000.0)
    return (scores, own_score)


def cross_scores(queries, key_rows, query_seg, key_seg):
    mixed = HEAD_DIM ** (-0.5) * jnp.einsum(
        "qhd,khd->qhk", queries, key_rows, preferred_element_type=jnp.float32
    )
    allowed = query_seg[:, None] == key_seg[None, :]
    return jnp.where(allowed[:, None, :], mixed, -1000000000.0)


def cross_forward(item):
    queries, key_rows, value_rows, query_seg, key_seg = item
    scores = cross_scores(queries, key_rows, query_seg, key_seg)
    top = jnp.max(scores, axis=-1)
    weights = jnp.exp(scores - top[..., None])
    total = jnp.sum(weights, axis=-1)
    probs = (weights / total[..., None]).astype(jnp.bfloat16)
    mixed = jnp.einsum("qhk,khd->qhd", probs, value_rows, preferred_element_type=jnp.float32)
    return (mixed.astype(jnp.bfloat16), top + jnp.log(total))


def cross_backward(item):
    queries, key_rows, value_rows, query_seg, key_seg, upstream, log_total = item
    scores = cross_scores(queries, key_rows, query_seg, key_seg)
    probs = jnp.exp(scores - log_total[..., None])
    prob_grad = jnp.einsum("qhd,khd->qhk", upstream, value_rows, preferred_element_type=jnp.float32)
    centre = jnp.sum(probs * prob_grad, axis=-1)
    score_grad = (probs * (prob_grad - centre[..., None])).astype(jnp.bfloat16)
    scale = HEAD_DIM ** (-0.5)
    query_grad = scale * jnp.einsum(
        "qhk,khd->qhd", score_grad, key_rows, preferred_element_type=jnp.float32
    )
    key_grad = scale * jnp.einsum(
        "qhk,qhd->khd", score_grad, queries, preferred_element_type=jnp.float32
    )
    value_grad = jnp.einsum(
        "qhk,qhd->khd", probs.astype(jnp.bfloat16), upstream, preferred_element_type=jnp.float32
    )
    full_len = key_rows.shape[0]
    return (
        query_grad,
        jnp.concatenate(
            [key_grad.reshape(full_len, -1), value_grad.reshape(full_len, -1)], axis=-1
        ),
    )


def shards(
    inputs,
    encoded,
    target_lengths,
    source_lengths,
    query_key_value,
    bucket_weight,
    self_output,
    cross_query,
    cross_key_value,
    cross_output,
    up_weight,
    up_bias,
    down_weight,
    down_bias,
    norm_gain,
    norm_shift,
    cotangent,
):
    row_count, stream_count, local_len, model_width = inputs.shape
    head_count = HEADS
    head_size = model_width // head_count
    full_len = local_len * lax.axis_size("seq")
    start = lax.axis_index("seq") * local_len
    here = start + jnp.arange(local_len, dtype=jnp.int32)
    key_pos = jnp.arange(full_len, dtype=jnp.int32)
    query_pos = jnp.tile(here, stream_count)
    stream_of = jnp.repeat(jnp.arange(stream_count, dtype=jnp.int32), local_len)
    target_here = jnp.tile(segment_ids(target_lengths, here), (1, stream_count))
    target_all = segment_ids(target_lengths, key_pos)
    source_all = segment_ids(source_lengths, key_pos)
    bucket_index = bucket_of(query_pos[:, None] - key_pos[None, :])
    onehot = (
        bucket_index[:, :, None] == jnp.arange(BUCKETS, dtype=jnp.int32)[None, None, :]
    ).astype(jnp.float32)
    token_count = row_count * stream_count * local_len
    heads_shape = (row_count, stream_count * local_len, head_count, head_size)
    flat_in = inputs.reshape(token_count, model_width)
    projected = jnp.dot(flat_in, query_key_value, preferred_element_type=jnp.float32).astype(
        jnp.bfloat16
    )
    relative = jnp.dot(flat_in, bucket_weight, preferred_element_type=jnp.float32)
    by_row = projected.reshape(row_count, stream_count, local_len, 3 * model_width)
    gathered_kv = lax.all_gather(by_row[:, 0, :, model_width:], "seq", axis=1, tiled=True)
    query_self = by_row[..., :model_width].reshape(heads_shape)
    key_self = by_row[..., model_width : 2 * model_width].reshape(heads_shape)
    value_self = by_row[..., 2 * model_width :].reshape(heads_shape)
    key_main = gathered_kv[..., :model_width].reshape(row_count, full_len, head_count, head_size)
    value_main = gathered_kv[..., model_width:].reshape(row_count, full_len, head_count, head_size)
    rel_rows = relative.reshape(row_count, stream_count * local_len, head_count, -1)

    def self_forward(item):
        queries, own_keys, own_values, key_rows, value_rows, table, query_seg, key_seg = item
        scores, own_score = self_scores(
            queries,
            own_keys,
            key_rows,
            table,
            query_seg,
            key_seg,
            query_pos,
            stream_of,
            key_pos,
            onehot,
        )
        top = jnp.maximum(jnp.max(scores, axis=-1), own_score)
        weights = jnp.exp(scores - top[..., None])
        own_weight = jnp.exp(own_score - top)
        total = jnp.sum(weights, axis=-1) + own_weight
        probs = (weights / total[..., None]).astype(jnp.bfloat16)
        own_prob = (own_weight / total).astype(jnp.bfloat16)
        mixed = jnp.einsum("qhk,khd->qhd", probs, value_rows, preferred_element_type=jnp.float32)
        mixed = mixed + own_prob.astype(jnp.float32)[..., None] * own_values.astype(jnp.float32)
        return (mixed.astype(jnp.bfloat16), top + jnp.log(total))

    def self_backward(item):
        (
            queries,
            own_keys,
            own_values,
            key_rows,
            value_rows,
            table,
            query_seg,
            key_seg,
            upstream,
            log_total,
        ) = item
        scores, own_score = self_scores(
            queries,
            own_keys,
            key_rows,
            table,
            query_seg,
            key_seg,
            query_pos,
            stream_of,
            key_pos,
            onehot,
        )
        probs = jnp.exp(scores - log_total[..., None])
        own_prob = jnp.exp(own_score - log_total)
        prob_grad = jnp.einsum(
            "qhd,khd->qhk", upstream, value_rows, preferred_element_type=jnp.float32
        )
        up_float = upstream.astype(jnp.float32)
        own_prob_grad = jnp.sum(up_float * own_values.astype(jnp.float32), axis=-1)
        centre = jnp.sum(probs * prob_grad, axis=-1) + own_prob * own_prob_grad
        score_grad = (probs * (prob_grad - centre[..., None])).astype(jnp.bfloat16)
        own_float = (own_prob * (own_prob_grad - centre)).astype(jnp.bfloat16).astype(jnp.float32)
        scale = HEAD_DIM ** (-0.5)
        query_grad = scale * (
            jnp.einsum("qhk,khd->qhd", score_grad, key_rows, preferred_element_type=jnp.float32)
            + own_float[..., None] * own_keys.astype(jnp.float32)
        )
        key_grad = scale * jnp.einsum(
            "qhk,qhd->khd", score_grad, queries, preferred_element_type=jnp.float32
        )
        value_grad = jnp.einsum(
            "qhk,qhd->khd", probs.astype(jnp.bfloat16), upstream, preferred_element_type=jnp.float32
        )
        own_key_grad = scale * own_float[..., None] * queries.astype(jnp.float32)
        own_value_grad = own_prob.astype(jnp.bfloat16).astype(jnp.float32)[..., None] * up_float
        table_grad = jnp.einsum(
            "qhk,qkb->qhb",
            score_grad.astype(jnp.float32),
            onehot,
            precision=lax.Precision.HIGHEST,
            preferred_element_type=jnp.float32,
        )
        table_grad = table_grad.at[:, :, 0].add(own_float)
        key_len = key_rows.shape[0]
        main_part = jnp.concatenate(
            [key_grad.reshape(key_len, -1), value_grad.reshape(key_len, -1)], axis=-1
        )
        return (query_grad, own_key_grad, own_value_grad, main_part, table_grad)

    self_mix, self_log = lax.map(
        self_forward,
        (query_self, key_self, value_self, key_main, value_main, rel_rows, target_here, target_all),
    )
    self_flat = self_mix.reshape(token_count, model_width)
    branch_one = jnp.dot(self_flat, self_output, preferred_element_type=jnp.float32)
    hidden_one, unit_one, inv_one = normalize(
        flat_in.astype(jnp.float32) + branch_one, norm_gain[0], norm_shift[0]
    )
    low_one = hidden_one.astype(jnp.bfloat16)
    cross_q = jnp.dot(low_one, cross_query, preferred_element_type=jnp.float32).astype(jnp.bfloat16)
    enc_flat = encoded.reshape(row_count * local_len, model_width)
    local_kv = (
        jnp.dot(enc_flat, cross_key_value, preferred_element_type=jnp.float32)
        .astype(jnp.bfloat16)
        .reshape(row_count, local_len, 2 * model_width)
    )
    source_kv = lax.all_gather(local_kv, "seq", axis=1, tiled=True)
    cross_keys = source_kv[..., :model_width].reshape(row_count, full_len, head_count, head_size)
    cross_values = source_kv[..., model_width:].reshape(row_count, full_len, head_count, head_size)
    cross_heads = cross_q.reshape(heads_shape)
    cross_mix, cross_log = lax.map(
        cross_forward, (cross_heads, cross_keys, cross_values, target_here, source_all)
    )
    cross_flat = cross_mix.reshape(token_count, model_width)
    branch_two = jnp.dot(cross_flat, cross_output, preferred_element_type=jnp.float32)
    hidden_two, unit_two, inv_two = normalize(hidden_one + branch_two, norm_gain[1], norm_shift[1])
    low_two = hidden_two.astype(jnp.bfloat16)
    pre_act = jnp.dot(low_two, up_weight, preferred_element_type=jnp.float32) + up_bias
    gelu_value, gelu_back = jax.vjp(lambda held: jax.nn.gelu(held, approximate=False), pre_act)
    activated = gelu_value.astype(jnp.bfloat16)
    branch_three = jnp.dot(activated, down_weight, preferred_element_type=jnp.float32) + down_bias
    result, unit_three, inv_three = normalize(
        hidden_two + branch_three, norm_gain[2], norm_shift[2]
    )
    three_grad, gain_three, shift_three = normalize_back(
        cotangent.reshape(token_count, model_width).astype(jnp.float32),
        unit_three,
        inv_three,
        norm_gain[2],
    )
    three_low = three_grad.astype(jnp.bfloat16)
    down_grad = weight_grad(activated, three_low)
    down_bias_grad = jnp.sum(three_grad, axis=0)
    act_grad = input_grad(three_low, down_weight).astype(jnp.bfloat16)
    pre_grad = gelu_back(act_grad.astype(jnp.float32))[0]
    up_bias_grad = jnp.sum(pre_grad, axis=0)
    pre_low = pre_grad.astype(jnp.bfloat16)
    up_grad = weight_grad(low_two, pre_low)
    hidden_two_grad = three_grad + input_grad(pre_low, up_weight).astype(jnp.bfloat16).astype(
        jnp.float32
    )
    two_grad, gain_two, shift_two = normalize_back(hidden_two_grad, unit_two, inv_two, norm_gain[1])
    two_low = two_grad.astype(jnp.bfloat16)
    cross_out_grad = weight_grad(cross_flat, two_low)
    cross_upstream = input_grad(two_low, cross_output).astype(jnp.bfloat16).reshape(heads_shape)
    cross_q_grad, source_parts = lax.map(
        cross_backward,
        (cross_heads, cross_keys, cross_values, target_here, source_all, cross_upstream, cross_log),
    )
    source_sums = lax.psum_scatter(
        source_parts.astype(jnp.bfloat16), "seq", scatter_dimension=1, tiled=True
    ).astype(jnp.float32)
    source_low = source_sums.reshape(row_count * local_len, 2 * model_width).astype(jnp.bfloat16)
    cross_kv_grad = weight_grad(enc_flat, source_low)
    encoded_grad = (
        input_grad(source_low, cross_key_value).astype(jnp.bfloat16).reshape(encoded.shape)
    )
    query_low = cross_q_grad.reshape(token_count, model_width).astype(jnp.bfloat16)
    cross_query_grad = weight_grad(low_one, query_low)
    hidden_one_grad = two_grad + input_grad(query_low, cross_query).astype(jnp.bfloat16).astype(
        jnp.float32
    )
    one_grad, gain_one, shift_one = normalize_back(hidden_one_grad, unit_one, inv_one, norm_gain[0])
    one_low = one_grad.astype(jnp.bfloat16)
    self_out_grad = weight_grad(self_flat, one_low)
    self_upstream = input_grad(one_low, self_output).astype(jnp.bfloat16).reshape(heads_shape)
    query_grad, own_key_grad, own_value_grad, main_parts, table_grad = lax.map(
        self_backward,
        (
            query_self,
            key_self,
            value_self,
            key_main,
            value_main,
            rel_rows,
            target_here,
            target_all,
            self_upstream,
            self_log,
        ),
    )
    main_sums = lax.psum_scatter(
        main_parts.astype(jnp.bfloat16), "seq", scatter_dimension=1, tiled=True
    ).astype(jnp.float32)
    stream_shape = (row_count, stream_count, local_len, model_width)
    key_total = own_key_grad.reshape(stream_shape)
    key_total = jnp.concatenate(
        [key_total[:, :1] + main_sums[:, None, :, :model_width], key_total[:, 1:]], axis=1
    )
    value_total = own_value_grad.reshape(stream_shape)
    value_total = jnp.concatenate(
        [value_total[:, :1] + main_sums[:, None, :, model_width:], value_total[:, 1:]], axis=1
    )
    projected_grad = (
        jnp.concatenate([query_grad.reshape(stream_shape), key_total, value_total], axis=-1)
        .reshape(token_count, 3 * model_width)
        .astype(jnp.bfloat16)
    )
    table_low = table_grad.reshape(token_count, -1).astype(jnp.bfloat16)
    qkv_grad = weight_grad(flat_in, projected_grad)
    bucket_grad = weight_grad(flat_in, table_low)
    inputs_grad = one_grad + (
        input_grad(projected_grad, query_key_value) + input_grad(table_low, bucket_weight)
    ).astype(jnp.bfloat16).astype(jnp.float32)
    gain_stack = jnp.stack([gain_one, gain_two, gain_three], axis=0)
    shift_stack = jnp.stack([shift_one, shift_two, shift_three], axis=0)
    summed = (
        lax.psum_scatter(qkv_grad, ("dp", "seq"), scatter_dimension=0, tiled=True),
        lax.psum_scatter(bucket_grad, ("dp", "seq"), scatter_dimension=0, tiled=True),
        lax.psum_scatter(self_out_grad, ("dp", "seq"), scatter_dimension=0, tiled=True),
        lax.psum_scatter(cross_query_grad, ("dp", "seq"), scatter_dimension=0, tiled=True),
        lax.psum_scatter(cross_kv_grad, ("dp", "seq"), scatter_dimension=0, tiled=True),
        lax.psum_scatter(cross_out_grad, ("dp", "seq"), scatter_dimension=0, tiled=True),
        lax.psum_scatter(up_grad, ("dp", "seq"), scatter_dimension=0, tiled=True),
        lax.psum_scatter(up_bias_grad, ("dp", "seq"), scatter_dimension=0, tiled=True),
        lax.psum_scatter(down_grad, ("dp", "seq"), scatter_dimension=0, tiled=True),
        lax.psum_scatter(down_bias_grad, ("dp", "seq"), scatter_dimension=0, tiled=True),
        lax.psum_scatter(gain_stack, ("dp", "seq"), scatter_dimension=1, tiled=True),
        lax.psum_scatter(shift_stack, ("dp", "seq"), scatter_dimension=1, tiled=True),
    )
    return (
        result.astype(jnp.bfloat16).reshape(inputs.shape),
        inputs_grad.astype(jnp.bfloat16).reshape(inputs.shape),
        encoded_grad,
        summed[0],
        summed[1],
        summed[2],
        summed[3],
        summed[4],
        summed[5],
        summed[6],
        summed[7],
        summed[8],
        summed[9],
        summed[10],
        summed[11],
    )


def solution(mesh):
    placed = (
        P("dp", None, "seq", None),
        P("dp", "seq", None),
        P("dp", None),
        P("dp", None),
        P(),
        P(),
        P(),
        P(),
        P(),
        P(),
        P(),
        P(),
        P(),
        P(),
        P(),
        P(),
        P("dp", None, "seq", None),
    )
    return jax.shard_map(
        shards,
        mesh=mesh,
        in_specs=placed,
        out_specs=(
            P("dp", None, "seq", None),
            P("dp", None, "seq", None),
            P("dp", "seq", None),
            P(("dp", "seq"), None),
            P(("dp", "seq"), None),
            P(("dp", "seq"), None),
            P(("dp", "seq"), None),
            P(("dp", "seq"), None),
            P(("dp", "seq"), None),
            P(("dp", "seq"), None),
            P(("dp", "seq")),
            P(("dp", "seq"), None),
            P(("dp", "seq")),
            P(None, ("dp", "seq")),
            P(None, ("dp", "seq")),
        ),
        check_vma=False,
    )
```

profile of v0, /device:TPU:0, one launch (start us, length us, event | category | flops | bytes accessed | tf_op | source)
XLA Modules:
  0.0 3287.9 jit_solution(12788581256339365738)
XLA Ops:
  7.2 7.7 convolution_convert_fusion.1
  84.3 36.7 %fusion.1 = f32[768,16,1024]{2,1,0:T(8,128)} fusion(f32[768,16,32]{2,1,0:T(8,128)} %copy.212, s32[768,1024]{1,0:T(8,128)} %compare_select_fusion), kind=kOutput, calls=%fused_computation.4 | convolution fusion | flops 4857004032 | bytes 55050240 | tf_op jit(solution)/shard_map/while/body/eval_jaxpr/qhb,qkb->qhk/dot_general | solution.py:67
  121.0 49.1 %copy.213 = f32[768,16,1024]{0,2,1:T(8,128)} copy(f32[768,16,1024]{2,1,0:T(8,128)} %fusion.1) | data formatting | bytes 100663296 | tf_op jit(solution)/shard_map/while/body/eval_jaxpr/qhb,qkb->qhk/dot_general | solution.py:67
  181.0 32.7 fusion.120
  214.8 19.1 fusion.11
  251.3 21.5 fusion.45
  284.7 21.5 fusion.23
  306.2 20.9 fusion.12
  327.8 22.3 fusion.79
  355.5 39.1 %multiply_convert_fusion = (bf16[768,4096]{1,0:T(8,128)(2,1)S(1)}, f32[768,4096]{1,0:T(8,128)}, f32[768,4096]{1,0:T(8,128)}) fusion(f32[4096]{0:T(1024)S(1)} %copy-done.85, bf16[1024,4096]{1,0:T(8,128)(2,1)} %param.29, f32[768,1024]{1,0:T(8,128)S(1)} %get-tuple-element.335, f32[1024]{0:T(1024)S(1)} %bitcast.312, f32[1024]{0:T(1024)S(1)} %bitcast.307, ...), kind=kOutput, calls=%fused_computation.47 | convolution fusion | flops 6654001152 | bytes 43022336 | tf_op jit(solution)/shard_map/dot_general | solution.py:296
  394.7 7.0 fusion.123
  409.0 22.1 fusion.124
  431.1 14.3 multiply_reduce_fusion
  454.0 22.2 fusion.70
  476.1 34.5 %fusion.5 = (f32[768,16]{0,1:T(8,128)S(1)}, f32[16,1024,768]{2,1,0:T(8,128)}) fusion(f32[768,16]{0,1:T(8,128)S(1)} %copy-done.36, f32[16,1024,768]{2,1,0:T(8,128)} %get-tuple-element.333, pred[768,1024]{0,1:T(8,128)(4,1)S(1)} %copy-done.3, bf16[1024,16,64]{0,2,1:T(8,128)(2,1)} %bitcast.279, bf16[768,16,64]{0,2,1:T(8,128)(2,1)} %bitcast.281), kind=kOutput, calls=%fused_computation.12 | convolution fusion | flops 1673515008 | bytes 105218048 | tf_op jit(solution)/shard_map/while/body/eval_jaxpr/qhd,khd->qhk/dot_general | solution.py:109
  510.7 41.1 %fusion.7 = bf16[768,16,1024]{0,2,1:T(8,128)(2,1)} fusion(f32[16,1024,768]{2,1,0:T(8,128)} %get-tuple-element.341, f32[768,16]{0,1:T(8,128)S(1)} %get-tuple-element.340, f32[768,16]{0,1:T(8,128)S(1)} %copy-done.36, f32[16,1024,768]{2,1,0:T(8,128)} %get-tuple-element.333, pred[768,1024]{0,1:T(8,128)(4,1)S(1)} %copy-done.3), kind=kLoop, calls=%fused_computation.14 | loop fusion | flops 75497472 | bytes 126713856 | tf_op jit(solution)/shard_map/while/body/eval_jaxpr/convert_element_type | solution.py:111
  551.8 14.2 multiply_convert_fusion.3
  566.0 13.9 multiply_convert_fusion.1
  579.9 7.2 multiply_reduce_fusion.1
  597.1 20.3 fusion.73
  617.3 32.0 fusion.2
  661.0 42.2 %fusion.4 = bf16[768,16,1024]{0,2,1:T(8,128)(2,1)} fusion(f32[16,1024,768]{2,1,0:T(8,128)} %get-tuple-element.344, f32[768,16,1024]{0,2,1:T(8,128)} %get-tuple-element.329, f32[768,16]{0,1:T(8,128)S(1)} %bitcast.315, f32[768,16]{0,1:T(8,128)S(1)} %bitcast.291), kind=kLoop, calls=%fused_computation.9 | loop fusion | flops 50331648 | bytes 125927424 | tf_op jit(solution)/shard_map/while/body/eval_jaxpr/convert_element_type | solution.py:239
  703.2 13.4 multiply_convert_fusion.2
  716.6 6.9 copy.227
  723.5 24.0 pad_maximum_fusion
  747.5 350.2 %copy.250 = bf16[1,1024,2048]{0,2,1:T(8,128)(2,1)} copy(bf16[1,1024,2048]{1,0,2:T(2,128)(2,1)} %pad_maximum_fusion) | data formatting | bytes 8388608
  1097.6 168.4 %bitcast_reduce_fusion = bf16[1024,2048]{1,0:T(8,128)(2,1)} fusion(bf16[1,1024,2048]{0,2,1:T(8,128)(2,1)} %copy.250), kind=kLoop, calls=%fused_computation | loop fusion | bytes 8388608
  1266.2 33.0 %copy.234 = bf16[768,16,1024]{2,1,0:T(8,128)(2,1)} copy(bf16[768,16,1024]{0,2,1:T(8,128)(2,1)} %fusion.4) | data formatting | bytes 50331648 | tf_op jit(solution)/shard_map/while/body/eval_jaxpr/convert_element_type | solution.py:239
  1300.2 20.6 fusion
  1361.1 9.2 copy.256
  1384.2 7.6 copy_multiply_fusion
  1395.6 13.7 fusion.37
  1426.4 83.2 %reshape_bitcast_fusion = bf16[1,256,2048]{0,2,1:T(8,128)(2,1)} fusion(bf16[256,2048]{1,0:T(8,128)(2,1)} %reduce-scatter.37.cloned.1.call-done), kind=kLoop, calls=%fused_computation.1 | loop fusion | bytes 2097152
  1509.6 117.8 %copy.251 = bf16[1,256,2048]{1,0,2:T(2,128)(2,1)S(1)} copy(bf16[1,256,2048]{0,2,1:T(8,128)(2,1)} %reshape_bitcast_fusion) | data formatting | bytes 2097152
  1639.1 8.3 copy.232
  1655.5 12.5 convolution_bitcast_fusion
  1668.0 12.6 copy.252
  1681.3 13.5 fusion.46
  1694.8 13.8 fusion.95
  1709.4 42.2 %all-reduce.2 = (f32[4096]{0:T(1024)S(1)}, f32[1024]{0:T(1024)S(1)}) all-reduce(f32[4096]{0:T(1024)S(1)} %copy-done.73, f32[1024]{0:T(1024)S(1)} %copy-done.63), channel_id=13, replica_groups=mesh['dp'=8,'seq'=4] {'dp','seq'}, use_global_device_ids=true, to_apply=%region_35.36.clone | all-reduce | flops 5120 | bytes 40960
  1760.0 8.0 fusion.69
  1770.2 132.1 %reduce-scatter.31.cloned.1.call-done = f32[32,1024]{1,0:T(8,128)} async-done(((f32[1024,1024]{1,0:T(8,128)}), f32[32,1024]{1,0:T(8,128)}) %reduce-scatter.31.cloned.1.call-update) | async-done | bytes 131088 | tf_op jit(solution)/shard_map/reduce_scatter | solution.py:391
  1902.2 149.6 %reduce-scatter.29.cloned.1.call-done = f32[32,1024]{1,0:T(8,128)} async-done(((f32[1024,1024]{1,0:T(8,128)}), f32[32,1024]{1,0:T(8,128)}) %reduce-scatter.29.cloned.1.call-update) | async-done | bytes 131088 | tf_op jit(solution)/shard_map/reduce_scatter | solution.py:389
  2051.8 149.6 %reduce-scatter.27.cloned.1.call-done = f32[32,1024]{1,0:T(8,128)} async-done(((f32[1024,1024]{1,0:T(8,128)}), f32[32,1024]{1,0:T(8,128)}) %reduce-scatter.27.cloned.1.call-update) | async-done | bytes 131088 | tf_op jit(solution)/shard_map/reduce_scatter | solution.py:388
  2201.5 187.4 %reduce-scatter.43.cloned.1.call-done = f32[32,2048]{1,0:T(8,128)} async-done(((f32[1024,2048]{1,0:T(8,128)}), f32[32,2048]{1,0:T(8,128)}) %reduce-scatter.43.cloned.1.call-update) | async-done | bytes 262160
  2388.9 161.0 %reduce-scatter.39.cloned.1.call-done = f32[32,3072]{1,0:T(8,128)} async-done(((f32[1024,3072]{1,0:T(8,128)}), f32[32,3072]{1,0:T(8,128)}) %reduce-scatter.39.cloned.1.call-update) | async-done | bytes 393232
  2549.8 366.2 %reduce-scatter.33.cloned.1.call-done = f32[32,4096]{1,0:T(8,128)} async-done(((f32[1024,4096]{1,0:T(8,128)}), f32[32,4096]{1,0:T(8,128)}) %reduce-scatter.33.cloned.1.call-update) | async-done | bytes 524304 | tf_op jit(solution)/shard_map/reduce_scatter | solution.py:392
  2916.0 364.9 %reduce-scatter.35.cloned.1.call-done = f32[128,1024]{1,0:T(8,128)} async-done(((f32[4096,1024]{1,0:T(8,128)}), f32[128,1024]{1,0:T(8,128)}) %reduce-scatter.35.cloned.1.call-update) | async-done | bytes 524304 | tf_op jit(solution)/shard_map/reduce_scatter | solution.py:394
  (339 shorter events, 261.2 us)
Async XLA Ops:
  7.2 271.9 %copy-start = (bf16[1024,1024]{1,0:T(8,128)(2,1)S(1)}, bf16[1024,1024]{1,0:T(8,128)(2,1)}, u32[]{:S(2)}) copy-start(bf16[1024,1024]{1,0:T(8,128)(2,1)} %param.26) | copy-start | bytes 6291460
  7.2 164.9 %all-gather.5.cloned.1.call-start = ((), (), s32[]{:S(2)}) async-start(), calls=%async_computation.18 | async-start | bytes 5242880 | tf_op jit(solution)/shard_map/all_gather | solution.py:174
  18.2 216.6 %all-gather.7.cloned.1.call-start = ((), (), s32[]{:S(2)}) async-start(), calls=%async_computation.19 | async-start | bytes 5242880 | tf_op jit(solution)/shard_map/all_gather | solution.py:285
  22.7 1332.1 %reduce-scatter.25.cloned.1.call-start = ((), (), s32[]{:S(2)}) async-start(), calls=%async_computation.12 | async-start | bytes 5242880 | tf_op jit(solution)/shard_map/reduce_scatter | solution.py:328
  28.8 9.4 copy-start.76
  28.8 10.0 copy-start.26
  172.1 155.7 %copy-start.2 = (pred[768,1024]{0,1:T(8,128)(4,1)}, pred[768,1024]{0,1:T(8,128)(4,1)S(1)}, u32[]{:S(2)}) copy-start(pred[768,1024]{0,1:T(8,128)(4,1)S(1)} %get-tuple-element.326) | copy-start | bytes 2359300
  214.8 19.9 copy-start.37
  277.4 72.6 %copy-start.60 = (f32[768]{0:T(1024)}, f32[768]{0:T(1024)S(1)}, u32[]{:S(2)}) copy-start(f32[768]{0:T(1024)S(1)} %broadcast_multiply_fusion.10) | copy-start | bytes 9220
  277.9 72.2 %copy-start.67 = (f32[768]{0:T(1024)}, f32[768]{0:T(1024)S(1)}, u32[]{:S(2)}) copy-start(f32[768]{0:T(1024)S(1)} %add_rsqrt_fusion.2) | copy-start | bytes 9220
  327.8 22.3 copy-start.15
  350.0 44.7 %slice-start = ((s8[8388608]{0:T(1024)(128)(4,1)}), s8[4194304]{0:T(1024)(128)(4,1)S(1)}, s32[]{:S(2)}) async-start(s8[8388608]{0:T(1024)(128)(4,1)} %bitcast.345), calls=%async_computation.26 | async-start | bytes 8388608
  354.7 40.0 %copy-start.6 = (f32[768,1024]{1,0:T(8,128)}, f32[768,1024]{1,0:T(8,128)S(1)}, u32[]{:S(2)}) copy-start(f32[768,1024]{1,0:T(8,128)S(1)} %get-tuple-element.335) | copy-start | bytes 9437188
  354.8 90.6 %copy-start.45 = (f32[768]{0:T(1024)}, f32[768]{0:T(1024)S(1)}, u32[]{:S(2)}) copy-start(f32[768]{0:T(1024)S(1)} %broadcast_multiply_fusion.9) | copy-start | bytes 9220
  355.2 90.2 %copy-start.53 = (f32[768]{0:T(1024)}, f32[768]{0:T(1024)S(1)}, u32[]{:S(2)}) copy-start(f32[768]{0:T(1024)S(1)} %add_rsqrt_fusion.1) | copy-start | bytes 9220
  355.5 39.2 %slice-start.1 = ((s8[8388608]{0:T(1024)(128)(4,1)}), s8[4194304]{0:T(1024)(128)(4,1)S(1)}, s32[]{:S(2)}) async-start(s8[8388608]{0:T(1024)(128)(4,1)} %bitcast.345), calls=%async_computation.27 | async-start | bytes 8388608
  355.5 39.2 %copy-start.86 = (f32[1024]{0:T(1024)S(1)}, f32[1024]{0:T(1024)}, u32[]{:S(2)}) copy-start(f32[1024]{0:T(1024)} %param.32) | copy-start | bytes 12292
  431.1 14.3 copy-start.7
  566.0 13.9 copy-start.41
  566.0 13.9 copy-start.61
  566.0 13.9 copy-start.68
  566.0 13.9 copy-start.71
  579.9 7.2 copy-start.16
  597.0 63.8 %copy-start.49 = (f32[768,16]{0,1:T(8,128)}, f32[768,16]{0,1:T(8,128)S(1)}, u32[]{:S(2)}) copy-start(f32[768,16]{0,1:T(8,128)S(1)} %multiply_reduce_fusion.2) | copy-start | bytes 147460
  649.3 11.5 copy-start.47
  654.1 772.3 %reduce-scatter.37.cloned.1.call-start = ((), (), s32[]{:S(2)}) async-start(), calls=%async_computation.20 | async-start | bytes 5242880
  661.0 42.2 %copy-start.4 = (bf16[768,16,64]{0,2,1:T(8,128)(2,1)S(1)}, bf16[768,16,64]{0,2,1:T(8,128)(2,1)}, u32[]{:S(2)}) copy-start(bf16[768,16,64]{0,2,1:T(8,128)(2,1)} %squeeze.88) | copy-start | bytes 4718596
  1266.1 33.1 %copy-start.66 = (f32[1024]{0:T(1024)S(1)}, f32[1024]{0:T(1024)}, u32[]{:S(2)}) copy-start(f32[1024]{0:T(1024)} %get-tuple-element.297) | copy-start | bytes 12292
  1266.1 33.1 %copy-start.78 = (f32[1024]{0:T(1024)S(1)}, f32[1024]{0:T(1024)}, u32[]{:S(2)}) copy-start(f32[1024]{0:T(1024)} %get-tuple-element.296) | copy-start | bytes 12292
  1266.1 33.0 %copy-start.80 = (f32[1024]{0:T(1024)S(1)}, f32[1024]{0:T(1024)}, u32[]{:S(2)}) copy-start(f32[1024]{0:T(1024)} %get-tuple-element.295) | copy-start | bytes 12292
  1266.1 486.6 %reduce-scatter.47.cloned.1.call-start = ((), (), s32[]{:S(2)}) async-start(), calls=%async_computation.25 | async-start | bytes 540672
  1326.2 427.9 %reduce-scatter.45.cloned.1.call-start = ((), (), s32[]{:S(2)}) async-start(), calls=%async_computation.24 | async-start | bytes 540672
  1329.1 441.1 %reduce-scatter.41.cloned.1.call-start = ((), (), s32[]{:S(2)}) async-start(), calls=%async_computation.22 | async-start | bytes 2162688
  1333.6 568.6 %reduce-scatter.31.cloned.1.call-start = ((), (), s32[]{:S(2)}) async-start(), calls=%async_computation.15 | async-start | bytes 4325376 | tf_op jit(solution)/shard_map/reduce_scatter | solution.py:391
  1339.9 711.9 %reduce-scatter.29.cloned.1.call-start = ((), (), s32[]{:S(2)}) async-start(), calls=%async_computation.14 | async-start | bytes 4325376 | tf_op jit(solution)/shard_map/reduce_scatter | solution.py:389
  1347.3 854.2 %reduce-scatter.27.cloned.1.call-start = ((), (), s32[]{:S(2)}) async-start(), calls=%async_computation.13 | async-start | bytes 4325376 | tf_op jit(solution)/shard_map/reduce_scatter | solution.py:388
  1354.4 1034.5 %reduce-scatter.43.cloned.1.call-start = ((), (), s32[]{:S(2)}) async-start(), calls=%async_computation.23 | async-start | bytes 8650752
  1370.3 1179.5 %reduce-scatter.39.cloned.1.call-start = ((), (), s32[]{:S(2)}) async-start(), calls=%async_computation.21 | async-start | bytes 12976128
  1384.2 10.5 copy-start.8
  1391.8 17.5 copy-start.17
  1639.1 8.3 copy-start.23
  1680.6 1235.4 %reduce-scatter.33.cloned.1.call-start = ((), (), s32[]{:S(2)}) async-start(), calls=%async_computation.16 | async-start | bytes 17301504 | tf_op jit(solution)/shard_map/reduce_scatter | solution.py:392
  1694.8 1586.2 %reduce-scatter.35.cloned.1.call-start = ((), (), s32[]{:S(2)}) async-start(), calls=%async_computation.17 | async-start | bytes 17301504 | tf_op jit(solution)/shard_map/reduce_scatter | solution.py:394
  1708.6 46.8 %copy-start.32 = (bf16[1,256,2048]{1,2,0:T(8,128)(2,1)S(1)}, bf16[1,256,2048]{1,2,0:T(8,128)(2,1)}, u32[]{:S(2)}) copy-start(bf16[1,256,2048]{1,2,0:T(8,128)(2,1)} %reduce-scatter.25.cloned.1.call-done) | copy-start | bytes 3145732
  1759.9 8.1 copy-start.19
  1759.9 8.1 copy-start.27
  1759.9 8.1 copy-start.29
  1759.9 1521.0 %copy-start.1 = (bf16[1024,1024]{1,0:T(8,128)(2,1)S(1)}, bf16[1024,1024]{1,0:T(8,128)(2,1)}, u32[]{:S(2)}) copy-start(bf16[1024,1024]{1,0:T(8,128)(2,1)} %param.26) | copy-start | bytes 6291460
  (59 other events, 182.0 us)
Sparse Core Ops, SparseCore 0:
  18.3 83.4 all-gather.4
  104.0 79.2 all-gather.6
  654.2 79.4 reduce-scatter.24
  1266.2 79.1 reduce-scatter.36
  1347.5 134.9 reduce-scatter.46
  1485.2 130.7 reduce-scatter.44
  1618.8 134.2 reduce-scatter.40
  1756.1 146.0 reduce-scatter.30
  1905.2 146.6 reduce-scatter.28
  2054.6 146.8 reduce-scatter.26
  2204.5 184.3 reduce-scatter.42
  2396.4 153.4 reduce-scatter.38
  2552.7 363.2 reduce-scatter.32
  2918.8 362.1 reduce-scatter.34
where the time goes:
time: 3320 us; the launch traced here: 3290 us
  waiting for transfers between devices  1510 us (45%)
  local copies, waits for them, and re-layouts  983 us (30%)
  matrix products  524 us (16%)
  other arithmetic  212 us (6%)
  blocking collectives  42.2 us (1%)
    unnamed x211, local copies, waits for them, and re-layouts  784 us
    reduce_scatter x1, waiting for transfers between devices, shards(): lax.psum_scatter(up_grad, ('dp', 'seq'), scatter_dimension=0, tiled=True)  366 us
    reduce_scatter x1, waiting for transfers between devices, shards(): lax.psum_scatter(down_grad, ('dp', 'seq'), scatter_dimension=0, tiled=True)  365 us
    unnamed x20, waiting for transfers between devices  349 us
    reduce_scatter x1, waiting for transfers between devices, shards(): lax.psum_scatter(self_out_grad, ('dp', 'seq'), scatter_dimension=0, tiled...  150 us
    reduce_scatter x1, waiting for transfers between devices, shards(): lax.psum_scatter(cross_query_grad, ('dp', 'seq'), scatter_dimension=0, ti...  150 us
    reduce_scatter x1, waiting for transfers between devices, shards(): lax.psum_scatter(cross_out_grad, ('dp', 'seq'), scatter_dimension=0, tile...  132 us
  transfers between devices with their start and end apart: 14, of which 7 were waited for; matrix products, arithmetic and copies ran while one was open for 39% of the time, Pallas kernels for 0%

commit v1 on v0

v1 whole, which is shorter than its diff:
```python
import functools
import math

import jax
import jax.numpy as jnp
from jax import lax
from jax.experimental import pallas as pl
from jax.experimental.pallas import tpu as pltpu
from jax.sharding import PartitionSpec as P

HEADS = 16
HEAD_DIM = 64
BUCKETS = 32
HALO = 512
TILE = 128
NEG = -1e30
SCALE = HEAD_DIM ** (-0.5)

bucket_edges = [
    int(math.ceil(16.0 * 8.0 ** (bucket_level / 16.0))) for bucket_level in range(1, 16)
]

def bucket_of(distance):
    forward_gap = jnp.maximum(distance, 0)
    far_bucket = jnp.full_like(forward_gap, 16)
    for bucket_edge in bucket_edges:
        far_bucket = far_bucket + (forward_gap >= bucket_edge).astype(jnp.int32)
    return jnp.where(forward_gap < 16, forward_gap, far_bucket)

def iota(shape, axis):
    return lax.broadcasted_iota(jnp.int32, shape, axis)

def dot(a, b, ca, cb):
    return lax.dot_general(a, b, (((ca,), (cb,)), ((), ())), preferred_element_type=jnp.float32)

def head_masks(dtype):
    lane = iota((TILE, TILE), 1)
    low = (lane < HEAD_DIM).astype(jnp.float32)
    return low.astype(dtype), (1.0 - low).astype(dtype)

def stacked(x, low, high):
    return jnp.concatenate([x * low, x * high], axis=0)

def near_bias(rel, near_ref, head):
    index = near_ref[...] + BUCKETS * head
    return jnp.concatenate(
        [jnp.take_along_axis(rel, index[:, :TILE], axis=1), jnp.take_along_axis(rel, index[:, TILE:], axis=1)],
        axis=1,
    )

def near_tables():
    row = iota((TILE, 2 * TILE), 0)
    col = iota((TILE, 2 * TILE), 1)
    near = bucket_of(row - col + TILE)
    gap = 2 * TILE - 1 - iota((2 * TILE, TILE), 0)
    lanes = iota((2 * TILE, TILE), 1)
    onehots = [(bucket_of(gap) + BUCKETS * h == lanes).astype(jnp.bfloat16) for h in range(4)]
    return near, jnp.concatenate(onehots, axis=0)

WINDOWS = ((-TILE, 2 * TILE), (-3 * TILE, 2 * TILE), (-4 * TILE, TILE))

def self_scores(w, qs, keys, rel, col31, start2, near_ref, heads, base):
    off, width = WINDOWS[w]
    s = dot(qs, keys, 1, 1)
    c = iota((2 * TILE, width), 1)
    if w == 0:
        bias = jnp.concatenate([near_bias(rel, near_ref, h) for h in heads], axis=0)
        r = iota((2 * TILE, width), 0) % TILE
        valid = (c >= start2 - (base + off)) & (c < r + TILE)
    else:
        bias = col31
        valid = c >= start2 - (base + off)
    return s + bias, valid

def self_fwd_kernel(nq, need_ref, q_ref, ko_ref, vo_ref, kh_ref, vh_ref, rel_ref, start_ref, near_ref,
                    mix_ref, lse_ref, kx, vx):
    local = nq * TILE
    kx[:HALO, :] = kh_ref[...]
    vx[:HALO, :] = vh_ref[...]
    kx[HALO:, :] = ko_ref[:local, :]
    vx[HALO:, :] = vo_ref[:local, :]
    low, high = head_masks(jnp.bfloat16)
    lane = iota((TILE, TILE), 1)

    def tile(t, _):
        i = lax.rem(t, nq)
        row0 = pl.multiple_of(t * TILE, TILE)
        base = pl.multiple_of(HALO + i * TILE, TILE)
        rows = pl.ds(row0, TILE)
        start = start_ref[pl.ds(pl.multiple_of(i * TILE, TILE), TILE), 0:1]
        start2 = jnp.concatenate([start, start], axis=0)
        rel = rel_ref[rows, :]

        def path(count):
            lses = []
            for p in range(2):
                lanes = slice(p * TILE, (p + 1) * TILE)
                heads = (2 * p, 2 * p + 1)
                q = q_ref[rows, lanes] * jnp.bfloat16(SCALE)
                qs = stacked(q, low, high)
                ko = ko_ref[rows, lanes]
                vo = vo_ref[rows, lanes]
                rel0 = jnp.concatenate([rel[:, BUCKETS * h : BUCKETS * h + 1] for h in heads], axis=0)
                col31 = jnp.concatenate([rel[:, BUCKETS * h + 31 : BUCKETS * h + 32] for h in heads], axis=0)
                own = jnp.sum(qs.astype(jnp.float32) * jnp.concatenate([ko, ko], axis=0).astype(jnp.float32), axis=1, keepdims=True) + rel0
                ss = []
                top = own
                for w in range(count):
                    off, width = WINDOWS[w]
                    keys = kx[pl.ds(pl.multiple_of(base + off, TILE), width), lanes]
                    s, valid = self_scores(w, qs, keys, rel, col31, start2, near_ref, heads, base)
                    s = jnp.where(valid, s, NEG)
                    ss.append(s)
                    top = jnp.maximum(top, jnp.max(s, axis=1, keepdims=True))
                pown = jnp.exp(own - top)
                total = pown
                acc = None
                for w in range(count):
                    off, width = WINDOWS[w]
                    pr = jnp.exp(ss[w] - top)
                    total = total + jnp.sum(pr, axis=1, keepdims=True)
                    vals = vx[pl.ds(pl.multiple_of(base + off, TILE), width), lanes]
                    o = dot(pr.astype(jnp.bfloat16), vals, 1, 0)
                    acc = o if acc is None else acc + o
                inv = 1.0 / total
                acc = acc * inv
                pown = (pown * inv)
                mixed = jnp.where(lane < HEAD_DIM, acc[:TILE], acc[TILE:])
                ow = jnp.where(lane < HEAD_DIM, pown[:TILE], pown[TILE:])
                mix_ref[rows, lanes] = (mixed + ow * vo.astype(jnp.float32)).astype(jnp.bfloat16)
                lse = top + jnp.log(total)
                lses += [lse[:TILE], lse[TILE:]]
            out = jnp.where(lane < 64, jnp.where(lane < 32, lses[0], lses[1]), jnp.where(lane < 96, lses[2], lses[3]))
            lse_ref[rows, :] = out

        for count in range(1, 4):
            @pl.when(need_ref[i] == count)
            def _():
                path(count)
        return 0

    lax.fori_loop(0, 3 * nq, tile, 0)

def self_forward(need, proj, halo_kv, rel, start, near):
    tokens = proj.shape[0]
    local = tokens // 3
    nq = local // TILE
    W = 256
    spec = lambda rows, base: pl.BlockSpec((rows, W), lambda g, *_: (0, base + g))
    return pl.pallas_call(
        functools.partial(self_fwd_kernel, nq),
        grid_spec=pltpu.PrefetchScalarGridSpec(
            num_scalar_prefetch=1, grid=(4,),
            in_specs=[spec(tokens, 0), spec(tokens, 4), spec(tokens, 8), spec(HALO, 0), spec(HALO, 4),
                      pl.BlockSpec((tokens, TILE), lambda g, *_: (0, g)),
                      pl.BlockSpec((local, TILE), lambda g, *_: (0, 0)),
                      pl.BlockSpec((TILE, 2 * TILE), lambda g, *_: (0, 0))],
            out_specs=[spec(tokens, 0), pl.BlockSpec((tokens, TILE), lambda g, *_: (0, g))],
            scratch_shapes=[pltpu.VMEM((HALO + local, W), jnp.bfloat16)] * 2),
        out_shape=[jax.ShapeDtypeStruct((tokens, 1024), jnp.bfloat16), jax.ShapeDtypeStruct((tokens, 512), jnp.float32)],
        compiler_params=pltpu.CompilerParams(vmem_limit_bytes=40 << 20),
        cost_estimate=pl.CostEstimate(flops=6_000_000_000, bytes_accessed=12_000_000, transcendentals=6_000_000),
        name="self_forward",
    )(need, proj, proj, proj, halo_kv, halo_kv, rel, start, near)

def self_bwd_kernel(nq, need_ref, q_ref, ko_ref, vo_ref, kh_ref, vh_ref, rel_ref, start_ref, near_ref, hot_ref,
                    mix_ref, lse_ref, up_ref, dproj_ref, dhalo_ref, drel_ref, kx, vx, dkt, dvt, dqa, dro):
    g = pl.program_id(0)
    local = nq * TILE
    kx[:HALO, :] = kh_ref[...]
    vx[:HALO, :] = vh_ref[...]
    kx[HALO:, :] = ko_ref[:local, :]
    vx[HALO:, :] = vo_ref[:local, :]
    dkt[...] = jnp.zeros_like(dkt)
    dvt[...] = jnp.zeros_like(dvt)
    low, high = head_masks(jnp.bfloat16)
    lane = iota((TILE, TILE), 1)
    gl = pl.multiple_of(g * 256, 256)
    flip = (iota((TILE, TILE), 0) + iota((TILE, TILE), 1) == TILE - 1).astype(jnp.float32).astype(jnp.bfloat16)

    def tile(t, _):
        i = lax.rem(t, nq)
        row0 = pl.multiple_of(t * TILE, TILE)
        base = pl.multiple_of(HALO + i * TILE, TILE)
        rows = pl.ds(row0, TILE)
        start = start_ref[pl.ds(pl.multiple_of(i * TILE, TILE), TILE), 0:1]
        start2 = jnp.concatenate([start, start], axis=0)
        rel = rel_ref[rows, :]
        need = need_ref[i]
        for p in range(2):
            lanes = slice(p * TILE, (p + 1) * TILE)
            heads = (2 * p, 2 * p + 1)
            q = q_ref[rows, lanes] * jnp.bfloat16(SCALE)
            qs = stacked(q, low, high)
            up = up_ref[rows, lanes]
            ups = stacked(up, low, high)
            ko = ko_ref[rows, lanes]
            vo = vo_ref[rows, lanes]
            rel0 = jnp.concatenate([rel[:, BUCKETS * h : BUCKETS * h + 1] for h in heads], axis=0)
            col31 = jnp.concatenate([rel[:, BUCKETS * h + 31 : BUCKETS * h + 32] for h in heads], axis=0)
            lse = jnp.concatenate([lse_ref[rows, BUCKETS * h : BUCKETS * h + 1] for h in heads], axis=0)
            qf = qs.astype(jnp.float32)
            upf = ups.astype(jnp.float32)
            own = jnp.sum(qf * jnp.concatenate([ko, ko], axis=0).astype(jnp.float32), axis=1, keepdims=True) + rel0
            mixf = mix_ref[rows, lanes].astype(jnp.float32)
            centre = jnp.sum(upf * jnp.concatenate([mixf, mixf], axis=0), axis=1, keepdims=True)
            pown = jnp.exp(own - lse)
            dpown = jnp.sum(upf * jnp.concatenate([vo, vo], axis=0).astype(jnp.float32), axis=1, keepdims=True)
            dsown = (pown * (dpown - centre)).astype(jnp.bfloat16).astype(jnp.float32)
            pown = pown.astype(jnp.bfloat16).astype(jnp.float32)

            def window(w):
                off, width = WINDOWS[w]
                at = pl.ds(pl.multiple_of(base + off, TILE), width)
                keys = kx[at, lanes]
                vals = vx[at, lanes]
                s, valid = self_scores(w, qs, keys, rel, col31, start2, near_ref, heads, base)
                pr = jnp.exp(jnp.where(valid, s - lse, NEG))
                dp = dot(ups, vals, 1, 1)
                ds = pr * (dp - centre)
                dsb = ds.astype(jnp.bfloat16)
                prb = pr.astype(jnp.bfloat16)
                dq = dot(dsb, keys, 1, 0)
                dkt[p, :, at] += dot(qs, dsb, 0, 0)
                dvt[p, :, at] += dot(ups, prb, 0, 0)
                return ds, dsb, dq

            ds, dsb, dq = window(0)
            dqa[...] = dq
            dr = jnp.zeros((TILE, TILE), jnp.float32)
            for j, h in enumerate(heads):
                turned = dot(flip, dsb[j * TILE : (j + 1) * TILE], 1, 0)
                u = pltpu.roll(turned, 0, 1, stride=1, stride_axis=0)
                dr = dr + dot(u.astype(jnp.bfloat16), hot_ref[h * 2 * TILE : (h + 1) * 2 * TILE, :], 1, 0)
            dr = dot(flip, dr.astype(jnp.bfloat16), 1, 0)
            for j, h in enumerate(heads):
                dr = dr + jnp.where(lane == BUCKETS * h, dsown[j * TILE : (j + 1) * TILE], 0.0)
            dro[...] = dr

            for w in (1, 2):
                @pl.when(need > w)
                def _():
                    ds, dsb, dq = window(w)
                    dqa[...] += dq
                    far = jnp.sum(dsb.astype(jnp.float32), axis=1, keepdims=True)
                    dro[...] += jnp.where(lane == BUCKETS * heads[0] + 31, far[:TILE], 0.0) + jnp.where(lane == BUCKETS * heads[1] + 31, far[TILE:], 0.0)

            dq = dqa[...]
            head0 = lane < HEAD_DIM
            dq = jnp.where(head0, dq[:TILE], dq[TILE:])
            dso = jnp.where(head0, dsown[:TILE], dsown[TILE:])
            pro = jnp.where(head0, pown[:TILE], pown[TILE:])
            col = pl.multiple_of(gl + p * TILE, TILE)
            dproj_ref[rows, pl.ds(col, TILE)] = (SCALE * (dq + dso * ko.astype(jnp.float32))).astype(jnp.bfloat16)
            dproj_ref[rows, pl.ds(col + 1024, TILE)] = (dso * q.astype(jnp.float32)).astype(jnp.bfloat16)
            dproj_ref[rows, pl.ds(col + 2048, TILE)] = (pro * up.astype(jnp.float32)).astype(jnp.bfloat16)
            if p == 0:
                drel_ref[rows, :] = dro[...].astype(jnp.bfloat16)
            else:
                drel_ref[rows, :] = (drel_ref[rows, :].astype(jnp.float32) + dro[...]).astype(jnp.bfloat16)
        return 0

    lax.fori_loop(0, 3 * nq, tile, 0)
    for p in range(2):
        for j, acc in enumerate((dkt, dvt)):
            col = pl.multiple_of(gl + p * TILE + 1024 * j, TILE)
            full = acc[p, :, :].T
            dhalo_ref[:, pl.ds(col, TILE)] = full[:HALO].astype(jnp.bfloat16)
            colp = pl.multiple_of(col + 1024, TILE)
            dproj_ref[:local, pl.ds(colp, TILE)] = (full[HALO:] + dproj_ref[:local, pl.ds(colp, TILE)].astype(jnp.float32)).astype(jnp.bfloat16)

def self_backward(need, proj, halo_kv, rel, start, near, hot, mix, lse, up):
    tokens = proj.shape[0]
    local = tokens // 3
    nq = local // TILE
    W = 256
    spec = lambda rows, base: pl.BlockSpec((rows, W), lambda g, *_: (0, base + g))
    whole = lambda rows, cols: pl.BlockSpec((rows, cols), lambda g, *_: (0, 0))
    return pl.pallas_call(
        functools.partial(self_bwd_kernel, nq),
        grid_spec=pltpu.PrefetchScalarGridSpec(
            num_scalar_prefetch=1, grid=(4,),
            in_specs=[spec(tokens, 0), spec(tokens, 4), spec(tokens, 8), spec(HALO, 0), spec(HALO, 4),
                      pl.BlockSpec((tokens, TILE), lambda g, *_: (0, g)),
                      whole(local, TILE), whole(TILE, 2 * TILE), whole(8 * TILE, TILE),
                      spec(tokens, 0), pl.BlockSpec((tokens, TILE), lambda g, *_: (0, g)), spec(tokens, 0)],
            out_specs=[whole(tokens, 3072), whole(HALO, 2048), pl.BlockSpec((tokens, TILE), lambda g, *_: (0, g))],
            scratch_shapes=[pltpu.VMEM((HALO + local, W), jnp.bfloat16)] * 2
            + [pltpu.VMEM((2, TILE, HALO + local), jnp.float32)] * 2
            + [pltpu.VMEM((2 * TILE, TILE), jnp.float32), pltpu.VMEM((TILE, TILE), jnp.float32)]),
        out_shape=[jax.ShapeDtypeStruct((tokens, 3072), jnp.bfloat16), jax.ShapeDtypeStruct((HALO, 2048), jnp.bfloat16),
                   jax.ShapeDtypeStruct((tokens, 512), jnp.bfloat16)],
        compiler_params=pltpu.CompilerParams(vmem_limit_bytes=48 << 20),
        cost_estimate=pl.CostEstimate(flops=20_000_000_000, bytes_accessed=24_000_000, transcendentals=6_000_000),
        name="self_backward",
    )(need, proj, proj, proj, halo_kv, halo_kv, rel, start, near, hot, mix, lse, up)

def load_shards(z_ref, shards, local, kv_ref, kx):
    for k in range(shards):
        at = lax.rem(z_ref[0] - k + shards, shards) * local
        kx[pl.ds(pl.multiple_of(at, TILE), local), :] = kv_ref[k * local : (k + 1) * local, :]
    kx[shards * local :, :] = jnp.zeros((TILE, kx.shape[1]), kx.dtype)

def cross_fwd_kernel(nq, shards, z_ref, lo_ref, count_ref, q_ref, k_ref, v_ref, from_ref, to_ref, mix_ref, lse_ref, kx, vx):
    local = nq * TILE
    load_shards(z_ref, shards, local, k_ref, kx)
    load_shards(z_ref, shards, local, v_ref, vx)
    low, high = head_masks(jnp.bfloat16)
    lane = iota((TILE, TILE), 1)
    W = 2 * TILE

    def tile(t, _):
        i = lax.rem(t, nq)
        row0 = pl.multiple_of(t * TILE, TILE)
        here = pl.ds(pl.multiple_of(i * TILE, TILE), TILE)
        rows = pl.ds(row0, TILE)
        lo = lo_ref[i]
        first = from_ref[here, 0:1]
        last = to_ref[here, 0:1]
        first = jnp.concatenate([first, first], axis=0)
        last = jnp.concatenate([last, last], axis=0)
        lses = []
        for p in range(2):
            lanes = slice(p * TILE, (p + 1) * TILE)
            qs = stacked(q_ref[rows, lanes] * jnp.bfloat16(SCALE), low, high)

            def step(w, carry):
                top, total, acc = carry
                at = pl.multiple_of(lo + w * W, TILE)
                s = dot(qs, kx[pl.ds(at, W), lanes], 1, 1)
                c = iota((W, W), 1)
                valid = (c >= first - at) & (c < last - at)
                s = jnp.where(valid, s, NEG)
                new = jnp.maximum(top, jnp.max(s, axis=1, keepdims=True))
                fade = jnp.exp(top - new)
                pr = jnp.where(valid, jnp.exp(s - new), 0.0)
                total = total * fade + jnp.sum(pr, axis=1, keepdims=True)
                acc = acc * fade + dot(pr.astype(jnp.bfloat16), vx[pl.ds(at, W), lanes], 1, 0)
                return new, total, acc

            carry = (jnp.full((W, 1), NEG, jnp.float32), jnp.zeros((W, 1), jnp.float32), jnp.zeros((W, TILE), jnp.float32))
            top, total, acc = lax.fori_loop(0, count_ref[i], step, carry)
            acc = acc * (1.0 / total)
            mix_ref[rows, lanes] = jnp.where(lane < HEAD_DIM, acc[:TILE], acc[TILE:]).astype(jnp.bfloat16)
            lse = top + jnp.log(total)
            lses += [lse[:TILE], lse[TILE:]]
        lse_ref[rows, :] = jnp.where(lane < 64, jnp.where(lane < 32, lses[0], lses[1]), jnp.where(lane < 96, lses[2], lses[3]))
        return 0

    lax.fori_loop(0, 3 * nq, tile, 0)

def cross_forward(z, lo, count, q, kv, first, last):
    tokens = q.shape[0]
    local = tokens // 3
    nq = local // TILE
    full = kv.shape[0]
    W = 256
    spec = lambda rows, base: pl.BlockSpec((rows, W), lambda g, *_: (0, base + g))
    whole = lambda rows, cols: pl.BlockSpec((rows, cols), lambda g, *_: (0, 0))
    return pl.pallas_call(
        functools.partial(cross_fwd_kernel, nq, full // local),
        grid_spec=pltpu.PrefetchScalarGridSpec(
            num_scalar_prefetch=3, grid=(4,),
            in_specs=[spec(tokens, 0), spec(full, 0), spec(full, 4), whole(local, TILE), whole(local, TILE)],
            out_specs=[spec(tokens, 0), pl.BlockSpec((tokens, TILE), lambda g, *_: (0, g))],
            scratch_shapes=[pltpu.VMEM((full + TILE, W), jnp.bfloat16)] * 2),
        out_shape=[jax.ShapeDtypeStruct((tokens, 1024), jnp.bfloat16), jax.ShapeDtypeStruct((tokens, 512), jnp.float32)],
        compiler_params=pltpu.CompilerParams(vmem_limit_bytes=40 << 20),
        cost_estimate=pl.CostEstimate(flops=6_000_000_000, bytes_accessed=12_000_000, transcendentals=6_000_000),
        name="cross_forward",
    )(z, lo, count, q, kv, kv, first, last)

def cross_bwd_kernel(nq, shards, z_ref, lo_ref, count_ref, q_ref, k_ref, v_ref, from_ref, to_ref, mix_ref, lse_ref, up_ref,
                     dq_ref, dkv_ref, kx, vx, dkt, dvt, dqa):
    g = pl.program_id(0)
    local = nq * TILE
    load_shards(z_ref, shards, local, k_ref, kx)
    load_shards(z_ref, shards, local, v_ref, vx)
    dkt[...] = jnp.zeros_like(dkt)
    dvt[...] = jnp.zeros_like(dvt)
    low, high = head_masks(jnp.bfloat16)
    lane = iota((TILE, TILE), 1)
    W = 2 * TILE

    def tile(t, _):
        i = lax.rem(t, nq)
        row0 = pl.multiple_of(t * TILE, TILE)
        here = pl.ds(pl.multiple_of(i * TILE, TILE), TILE)
        rows = pl.ds(row0, TILE)
        lo = lo_ref[i]
        first = from_ref[here, 0:1]
        last = to_ref[here, 0:1]
        first = jnp.concatenate([first, first], axis=0)
        last = jnp.concatenate([last, last], axis=0)
        for p in range(2):
            lanes = slice(p * TILE, (p + 1) * TILE)
            heads = (2 * p, 2 * p + 1)
            qs = stacked(q_ref[rows, lanes] * jnp.bfloat16(SCALE), low, high)
            ups = stacked(up_ref[rows, lanes], low, high)
            lse = jnp.concatenate([lse_ref[rows, BUCKETS * h : BUCKETS * h + 1] for h in heads], axis=0)
            mixf = mix_ref[rows, lanes].astype(jnp.float32)
            centre = jnp.sum(ups.astype(jnp.float32) * jnp.concatenate([mixf, mixf], axis=0), axis=1, keepdims=True)
            dqa[...] = jnp.zeros_like(dqa)

            def step(w, _):
                at = pl.multiple_of(lo + w * W, TILE)
                keys = kx[pl.ds(at, W), lanes]
                s = dot(qs, keys, 1, 1)
                c = iota((W, W), 1)
                valid = (c >= first - at) & (c < last - at)
                pr = jnp.exp(jnp.where(valid, s - lse, NEG))
                dp = dot(ups, vx[pl.ds(at, W), lanes], 1, 1)
                dsb = (pr * (dp - centre)).astype(jnp.bfloat16)
                dqa[...] += dot(dsb, keys, 1, 0)
                dkt[p, :, pl.ds(at, W)] += dot(qs, dsb, 0, 0)
                dvt[p, :, pl.ds(at, W)] += dot(ups, pr.astype(jnp.bfloat16), 0, 0)
                return 0

            lax.fori_loop(0, count_ref[i], step, 0)
            dq = dqa[...]
            dq_ref[rows, lanes] = (SCALE * jnp.where(lane < HEAD_DIM, dq[:TILE], dq[TILE:])).astype(jnp.bfloat16)
        return 0

    lax.fori_loop(0, 3 * nq, tile, 0)
    for p in range(2):
        for j, acc in enumerate((dkt, dvt)):
            col = pl.multiple_of(g * 256 + p * TILE + 1024 * j, TILE)
            for k in range(shards):
                at = lax.rem(z_ref[0] - k + shards, shards) * local
                part = acc[p, :, pl.ds(pl.multiple_of(at, TILE), local)].T
                dkv_ref[k * local : (k + 1) * local, pl.ds(col, TILE)] = part.astype(jnp.bfloat16)

def cross_backward(z, lo, count, q, kv, first, last, mix, lse, up):
    tokens = q.shape[0]
    local = tokens // 3
    nq = local // TILE
    full = kv.shape[0]
    W = 256
    spec = lambda rows, base: pl.BlockSpec((rows, W), lambda g, *_: (0, base + g))
    whole = lambda rows, cols: pl.BlockSpec((rows, cols), lambda g, *_: (0, 0))
    return pl.pallas_call(
        functools.partial(cross_bwd_kernel, nq, full // local),
        grid_spec=pltpu.PrefetchScalarGridSpec(
            num_scalar_prefetch=3, grid=(4,),
            in_specs=[spec(tokens, 0), spec(full, 0), spec(full, 4), whole(local, TILE), whole(local, TILE),
                      spec(tokens, 0), pl.BlockSpec((tokens, TILE), lambda g, *_: (0, g)), spec(tokens, 0)],
            out_specs=[spec(tokens, 0), whole(full, 2048)],
            scratch_shapes=[pltpu.VMEM((full + TILE, W), jnp.bfloat16)] * 2
            + [pltpu.VMEM((2, TILE, full + TILE), jnp.float32)] * 2
            + [pltpu.VMEM((W, TILE), jnp.float32)]),
        out_shape=[jax.ShapeDtypeStruct((tokens, 1024), jnp.bfloat16), jax.ShapeDtypeStruct((full, 2048), jnp.bfloat16)],
        compiler_params=pltpu.CompilerParams(vmem_limit_bytes=48 << 20),
        cost_estimate=pl.CostEstimate(flops=20_000_000_000, bytes_accessed=24_000_000, transcendentals=6_000_000),
        name="cross_backward",
    )(z, lo, count, q, kv, kv, first, last, mix, lse, up)

def gelu_parts(x):
    u = jnp.abs(x) * (0.5**0.5)
    t = 1.0 / (1.0 + 0.5 * u)
    poly = jnp.float32(0.17087277)
    for coef in (-0.82215223, 1.48851587, -1.13520398, 0.27886807, -0.18628806, 0.09678418, 0.37409196, 1.00002368, -1.26551223):
        poly = poly * t + coef
    square = u * u
    half = 0.5 * t * jnp.exp(poly - square)
    below = jnp.where(x >= 0, 1.0 - half, half)
    dense = jnp.exp(-square) * (1.0 / math.sqrt(2.0 * math.pi))
    return x * below, below + x * dense


def up_kernel(x_ref, w_ref, b_ref, act_ref, slope_ref):
    rows = x_ref.shape[0]
    step = 256 if rows % 256 == 0 else TILE
    for r in range(0, rows, step):
        pre = dot(x_ref[r : r + step, :], w_ref[...], 1, 0) + b_ref[...]
        value, slope = gelu_parts(pre)
        act_ref[r : r + step, :] = value.astype(jnp.bfloat16)
        slope_ref[r : r + step, :] = slope.astype(jnp.bfloat16)


def up_gelu(x, w, b):
    tokens, width = x.shape
    hidden = w.shape[1]
    block = 512
    out = pl.BlockSpec((tokens, block), lambda j: (0, j))
    return pl.pallas_call(
        up_kernel,
        grid=(hidden // block,),
        in_specs=[
            pl.BlockSpec((tokens, width), lambda j: (0, 0)),
            pl.BlockSpec((width, block), lambda j: (0, j)),
            pl.BlockSpec((1, block), lambda j: (0, j)),
        ],
        out_specs=[out, out],
        out_shape=[jax.ShapeDtypeStruct((tokens, hidden), jnp.bfloat16)] * 2,
        compiler_params=pltpu.CompilerParams(vmem_limit_bytes=40 << 20),
        cost_estimate=pl.CostEstimate(
            flops=2 * tokens * width * hidden * 3, bytes_accessed=22_000_000, transcendentals=6_000_000
        ),
        name="up_gelu",
    )(x, w, b.reshape(1, hidden))


def normalize(hidden, gain, shift):
    centre = hidden - jnp.mean(hidden, axis=-1, keepdims=True)
    scale_inv = lax.rsqrt(jnp.mean(centre * centre, axis=-1, keepdims=True) + 1e-05)
    unit = centre * scale_inv
    return (unit * gain + shift, unit, scale_inv)


def normalize_back(upstream, unit, scale_inv, gain):
    along = upstream * gain
    inner = (
        along
        - jnp.mean(along, axis=-1, keepdims=True)
        - unit * jnp.mean(along * unit, axis=-1, keepdims=True)
    )
    return (scale_inv * inner, jnp.sum(upstream * unit, axis=0), jnp.sum(upstream, axis=0))


def flip_pairs(size, bit):
    return [(i, i ^ (1 << bit)) for i in range(size)]


class Mesh:
    def __init__(self):
        self.dp = lax.axis_size("dp")
        self.seq = lax.axis_size("seq")
        dp_bits = self.dp.bit_length() - 1
        seq_bits = self.seq.bit_length() - 1
        d, z = lax.axis_index("dp"), lax.axis_index("seq")
        self.bits = [("dp", self.dp, k, (d >> k) & 1) for k in reversed(range(dp_bits))]
        self.bits += [("seq", self.seq, k, (z >> k) & 1) for k in reversed(range(seq_bits))]
        core = dp_bits - 1
        rest = list(reversed(range(dp_bits - 1)))
        tail = [dp_bits + k for k in reversed(range(seq_bits))]
        self.orders = ([core] + rest + tail, [core] + rest[::-1] + tail)

    def swap(self, x, bit):
        axis, size, k, _ = self.bits[bit]
        return lax.ppermute(x, axis, flip_pairs(size, k))


def pick(x, axes, bit, index):
    at = axes.index(bit)
    return lax.dynamic_index_in_dim(x, index, at, keepdims=False), axes[:at] + axes[at + 1 :]


def pick_columns(x, mesh, fixed):
    total = len(mesh.bits)
    tokens, width = x.shape
    x = x.reshape((tokens,) + (2,) * total + (width >> total,))
    axes = list(range(total))
    for bit, index in fixed:
        at = axes.index(bit)
        x = lax.dynamic_index_in_dim(x, index, at + 1, keepdims=False)
        axes.pop(at)
    return x.reshape(tokens, -1)


def scatter_sum(mesh, order, terms):
    total = len(mesh.bits)
    width = terms[0][0].shape[1]
    deep = width >> total
    me = [bit[3] for bit in mesh.bits]
    b0, b1 = order[0], order[1]

    def product(fixed):
        out = None
        for left, right in terms:
            part = lax.dot_general(
                pick_columns(left, mesh, fixed), right, (((0,), (0,)), ((), ())), preferred_element_type=jnp.float32
            )
            out = part if out is None else out + part
        return out

    columns = terms[0][1].shape[1]
    axes0 = [b for b in range(total) if b != b0]
    axes1 = [b for b in axes0 if b != b1]
    first = mesh.swap(product([(b0, 1 - me[b0])]).astype(jnp.bfloat16), b0)
    first = first.reshape((2,) * len(axes0) + (deep, columns))
    theirs, _ = pick(first, axes0, b1, 1 - me[b1])
    mine, _ = pick(first, axes0, b1, me[b1])
    rows = deep << len(axes1)
    send = product([(b0, me[b0]), (b1, 1 - me[b1])]) + theirs.reshape(rows, columns).astype(jnp.float32)
    second = mesh.swap(send.astype(jnp.bfloat16), b1)
    keep = product([(b0, me[b0]), (b1, me[b1])]) + mine.reshape(rows, columns).astype(jnp.float32)
    keep = keep + second.astype(jnp.float32)
    return halve(mesh, keep.astype(jnp.bfloat16).reshape((2,) * len(axes1) + (deep, columns)), axes1, order[2:])


def halve(mesh, value, axes, order):
    kind = value.dtype
    last = len(order) - 1
    for n, bit in enumerate(order):
        index = mesh.bits[bit][3]
        theirs, _ = pick(value, axes, bit, 1 - index)
        mine, axes = pick(value, axes, bit, index)
        value = mine.astype(jnp.float32) + mesh.swap(theirs, bit).astype(jnp.float32)
        if n < last:
            value = value.astype(kind)
    return value


def shards(
    inputs,
    encoded,
    target_lengths,
    source_lengths,
    query_key_value,
    bucket_weight,
    self_output,
    cross_query,
    cross_key_value,
    cross_output,
    up_weight,
    up_bias,
    down_weight,
    down_bias,
    norm_gain,
    norm_shift,
    cotangent,
):
    row_count, streams, local, width = inputs.shape
    mesh = Mesh()
    size = mesh.seq
    full = local * size
    z = lax.axis_index("seq")
    begin = z * local
    bf16, f32 = jnp.bfloat16, jnp.float32
    tokens = streams * local
    up_chain = [(i, i + 1) for i in range(size - 1)]
    down_chain = [(i + 1, i) for i in range(size - 1)]

    def mm(left, right):
        return jnp.dot(left, right, preferred_element_type=f32)

    def mm_t(left, right):
        return lax.dot_general(left, right, (((1,), (1,)), ((), ())), preferred_element_type=f32)

    flat = inputs.reshape(tokens, width)
    main = flat[:local]
    hops = HALO // local
    passing, pieces = main, []
    for _ in range(hops):
        passing = lax.ppermute(passing, "seq", up_chain)
        pieces.insert(0, passing)
    halo = jnp.concatenate(pieces, axis=0)
    own_source = encoded.reshape(local, width)
    waiting, halo = lax.optimization_barrier((own_source, halo))
    sources = [own_source] + [
        lax.ppermute(waiting, "seq", [(i, (i + k) % size) for i in range(size)]) for k in range(1, size)
    ]
    source = jnp.concatenate(sources, axis=0)

    here = begin + jnp.arange(local, dtype=jnp.int32)
    ends = jnp.cumsum(target_lengths[0])
    source_ends = jnp.cumsum(source_lengths[0])
    passed = here[:, None] >= ends[None, :]
    number = jnp.sum(passed.astype(jnp.int32), axis=1)
    start = jnp.max(jnp.where(passed, ends[None, :], 0), axis=1) - begin + HALO
    is_doc = number[:, None] == jnp.arange(ends.shape[0] + 1, dtype=jnp.int32)[None, :]
    zero = jnp.zeros((1,), jnp.int32)
    first = jnp.sum(jnp.where(is_doc, jnp.concatenate([zero, source_ends])[None, :], 0), axis=1)
    last = jnp.sum(jnp.where(is_doc, jnp.concatenate([source_ends, zero + full])[None, :], 0), axis=1)
    edge = start[::TILE]
    at = HALO + TILE * jnp.arange(local // TILE, dtype=jnp.int32)
    need = 1 + (edge < at - TILE).astype(jnp.int32) + (edge < at - 3 * TILE).astype(jnp.int32)
    low_key = first[::TILE] // TILE * TILE
    count = (last[TILE - 1 :: TILE] - low_key + 2 * TILE - 1) // (2 * TILE)

    def wide(column):
        return jnp.broadcast_to(column[:, None], (local, TILE))

    start, first, last = wide(start), wide(first), wide(last)
    near, hot = near_tables()
    z_one = z.reshape(1).astype(jnp.int32)

    proj = mm(flat, query_key_value).astype(bf16)
    relative = mm(flat, bucket_weight)
    halo_kv = mm(halo, query_key_value[:, width:]).astype(bf16)
    self_mix, self_log = self_forward(need, proj, halo_kv, relative, start, near)
    hidden_one, unit_one, inv_one = normalize(flat.astype(f32) + mm(self_mix, self_output), norm_gain[0], norm_shift[0])
    low_one = hidden_one.astype(bf16)
    cross_q = mm(low_one, cross_query).astype(bf16)
    source_kv = mm(source, cross_key_value).astype(bf16)
    cross_mix, cross_log = cross_forward(z_one, low_key, count, cross_q, source_kv, first, last)
    hidden_two, unit_two, inv_two = normalize(hidden_one + mm(cross_mix, cross_output), norm_gain[1], norm_shift[1])
    low_two = hidden_two.astype(bf16)
    activated, slope = up_gelu(low_two, up_weight, up_bias)
    branch_three = mm(activated, down_weight) + down_bias
    result, unit_three, inv_three = normalize(hidden_two + branch_three, norm_gain[2], norm_shift[2])

    three_grad, gain_three, shift_three = normalize_back(
        cotangent.reshape(tokens, width).astype(f32), unit_three, inv_three, norm_gain[2]
    )
    three_low = three_grad.astype(bf16)
    down_bias_grad = jnp.sum(three_grad, axis=0)
    down_grad = scatter_sum(mesh, mesh.orders[1], [(activated, three_low)])
    pre_grad = mm_t(three_low, down_weight).astype(bf16).astype(f32) * slope.astype(f32)
    up_bias_grad = jnp.sum(pre_grad, axis=0)
    pre_low = pre_grad.astype(bf16)
    up_grad = scatter_sum(mesh, mesh.orders[0], [(low_two, pre_low)])
    hidden_two_grad = three_grad + mm_t(pre_low, up_weight).astype(bf16).astype(f32)
    two_grad, gain_two, shift_two = normalize_back(hidden_two_grad, unit_two, inv_two, norm_gain[1])
    two_low = two_grad.astype(bf16)
    cross_out_grad = scatter_sum(mesh, mesh.orders[1], [(cross_mix, two_low)])
    cross_up = mm_t(two_low, cross_output).astype(bf16)
    query_low, source_low = cross_backward(
        z_one, low_key, count, cross_q, source_kv, first, last, cross_mix, cross_log, cross_up
    )
    cross_kv_grad = scatter_sum(mesh, mesh.orders[0], [(source, source_low)])
    cross_query_grad = scatter_sum(mesh, mesh.orders[1], [(low_one, query_low)])
    source_back = mm_t(source_low, cross_key_value)
    encoded_grad = source_back[:local]
    back_low = source_back[local:].astype(bf16)
    for k in range(1, size):
        part = back_low[(k - 1) * local : k * local]
        encoded_grad = encoded_grad + lax.ppermute(
            part, "seq", [(i, (i - k) % size) for i in range(size)]
        ).astype(f32)
    hidden_one_grad = two_grad + mm_t(query_low, cross_query).astype(bf16).astype(f32)
    one_grad, gain_one, shift_one = normalize_back(hidden_one_grad, unit_one, inv_one, norm_gain[0])
    one_low = one_grad.astype(bf16)
    self_out_grad = scatter_sum(mesh, mesh.orders[1], [(self_mix, one_low)])
    self_up = mm_t(one_low, self_output).astype(bf16)
    proj_low, halo_low, table_low = self_backward(
        need, proj, halo_kv, relative, start, near, hot, self_mix, self_log, self_up
    )
    halo_back = mm_t(halo_low, query_key_value[:, width:]).astype(bf16)
    passing = halo_back[:local]
    for k in range(hops):
        passing = lax.ppermute(passing, "seq", down_chain)
        if k + 1 < hops:
            passing = (passing.astype(f32) + halo_back[(k + 1) * local : (k + 2) * local].astype(f32)).astype(bf16)
    q_grad = scatter_sum(mesh, mesh.orders[0], [(flat, proj_low[:, :width])])
    k_grad = scatter_sum(
        mesh, mesh.orders[0], [(flat, proj_low[:, width : 2 * width]), (halo, halo_low[:, :width])]
    )
    v_grad = scatter_sum(mesh, mesh.orders[1], [(flat, proj_low[:, 2 * width :]), (halo, halo_low[:, width:])])
    bucket_grad = scatter_sum(mesh, mesh.orders[1], [(flat, table_low)])
    back = mm_t(proj_low, query_key_value) + mm_t(table_low, bucket_weight)
    back = back.reshape(streams, local, width)
    back = jnp.concatenate([back[:1] + passing[None].astype(f32), back[1:]], axis=0).reshape(tokens, width)
    inputs_grad = one_grad + back.astype(bf16).astype(f32)

    devices = mesh.dp * mesh.seq
    gains = jnp.stack([gain_one, gain_two, gain_three]).reshape(3, devices, -1).transpose(1, 0, 2)
    shifts = jnp.stack([shift_one, shift_two, shift_three]).reshape(3, devices, -1).transpose(1, 0, 2)
    each = width // devices
    small = jnp.concatenate(
        [
            up_bias_grad.reshape(devices, -1),
            down_bias_grad.reshape(devices, -1),
            gains.reshape(devices, -1),
            shifts.reshape(devices, -1),
        ],
        axis=1,
    )
    bits = len(mesh.bits)
    small = halve(mesh, small.reshape((2,) * bits + (1, -1)), list(range(bits)), mesh.orders[0])[0]
    wide_each = up_bias_grad.shape[0] // devices
    cuts = [wide_each, wide_each + each, wide_each + 4 * each]
    up_bias_grad, down_bias_grad, gains, shifts = jnp.split(small, cuts)
    return (
        result.astype(bf16).reshape(inputs.shape),
        inputs_grad.astype(bf16).reshape(inputs.shape),
        encoded_grad.astype(bf16).reshape(encoded.shape),
        jnp.concatenate([q_grad, k_grad, v_grad], axis=1),
        bucket_grad,
        self_out_grad,
        cross_query_grad,
        cross_kv_grad,
        cross_out_grad,
        up_grad,
        up_bias_grad,
        down_grad,
        down_bias_grad,
        gains.reshape(3, each),
        shifts.reshape(3, each),
    )


def solution(mesh):
    placed = (
        P("dp", None, "seq", None),
        P("dp", "seq", None),
        P("dp", None),
        P("dp", None),
        P(),
        P(),
        P(),
        P(),
        P(),
        P(),
        P(),
        P(),
        P(),
        P(),
        P(),
        P(),
        P("dp", None, "seq", None),
    )
    return jax.shard_map(
        shards,
        mesh=mesh,
        in_specs=placed,
        out_specs=(
            P("dp", None, "seq", None),
            P("dp", None, "seq", None),
            P("dp", "seq", None),
            P(("dp", "seq"), None),
            P(("dp", "seq"), None),
            P(("dp", "seq"), None),
            P(("dp", "seq"), None),
            P(("dp", "seq"), None),
            P(("dp", "seq"), None),
            P(("dp", "seq"), None),
            P(("dp", "seq")),
            P(("dp", "seq"), None),
            P(("dp", "seq")),
            P(None, ("dp", "seq")),
            P(None, ("dp", "seq")),
        ),
        check_vma=False,
    )
```

time: 3320 us -> 926 us (0.28)
  waiting for transfers between devices: 1510 us -> 209 us
  local copies, waits for them, and re-layouts: 983 us -> 102 us
  matrix products: 524 us -> 168 us
  Pallas kernels: 0 us -> 224 us
  other arithmetic: 212 us -> 40.8 us
  starting transfers between devices: 0.99 us -> 169 us
  blocking collectives: 42.2 us -> 0 us
    reduce_scatter x6 -> x0, waiting for transfers between devices: 1160 us -> none  [the longest x1 366 us: shards(): lax.psum_scatter(up_grad, ('dp', 'seq'), scatter_dimension=0, tiled=True)]
    unnamed x211 -> x257, local copies, waits for them, and re-layouts: 784 us -> 17.9 us
    dot_general x38 -> x53, matrix products: 524 us -> 168 us  [the longest x36 70.3 us: product(): lax.dot_general(pick_columns(left, mesh, fixed), right, (((0,), (0,)), ((...]
    unnamed x20 -> x0, waiting for transfers between devices: 349 us -> none
    pallas_call x0 -> x5, Pallas kernels: none -> 224 us  [the longest x1 74.9 us: self_backward(): pl.pallas_call(functools.partial(self_bwd_kernel, nq), grid_spec=pltpu.Pr...]
    ppermute x0 -> x65, waiting for transfers between devices: none -> 209 us  [the longest x55 188 us: swap(): return lax.ppermute(x, axis, flip_pairs(size, k))]
    ppermute x0 -> x65, starting transfers between devices: none -> 169 us  [the longest x3 86.3 us: shards(): lax.ppermute(part, 'seq', [(i, (i - k) % size) for i in range(size)])]
    convert_element_type x5 -> x37, other arithmetic: 91.6 us -> 17.9 us  [the longest x10 5.92 us: scatter_sum(): keep.astype(jnp.bfloat16).reshape((2,) * len(axes1) + (deep, columns))]
  transfers between devices with their start and end apart: 14 -> 65, of which waited for: 7 -> 38; matrix products, arithmetic and copies ran while one was open for 39% -> 19% of each run, Pallas kernels for 0% -> 4%
where the time goes in v1:
time: 926 us; the launch traced here: 916 us
  Pallas kernels  224 us (24%)
  waiting for transfers between devices  209 us (23%)
  starting transfers between devices  169 us (18%)
  matrix products  168 us (18%)
  local copies, waits for them, and re-layouts  102 us (11%)
  other arithmetic  40.8 us (4%)
    ppermute x55, waiting for transfers between devices, swap(): return lax.ppermute(x, axis, flip_pairs(size, k))  188 us
    ppermute x3, starting transfers between devices, shards(): lax.ppermute(part, 'seq', [(i, (i - k) % size) for i in range(size)])  86.3 us
    pallas_call x1, Pallas kernels, self_backward(): pl.pallas_call(functools.partial(self_bwd_kernel, nq), grid_spec=pltpu.Pr...  74.9 us
    dot_general x36, matrix products, product(): lax.dot_general(pick_columns(left, mesh, fixed), right, (((0,), (0,)), ((...  70.3 us
    ppermute x55, starting transfers between devices, swap(): return lax.ppermute(x, axis, flip_pairs(size, k))  65.4 us
    dot_general x9, matrix products, mm_t(): lax.dot_general(left, right, (((1,), (1,)), ((), ())), preferred_element_...  59 us
    pallas_call x1, Pallas kernels, cross_backward(): pl.pallas_call(functools.partial(cross_bwd_kernel, nq, full // local), gr...  46.3 us
    pallas_call x1, Pallas kernels, cross_forward(): pl.pallas_call(functools.partial(cross_fwd_kernel, nq, full // local), gr...  39.9 us
  transfers between devices with their start and end apart: 65, of which 38 were waited for; matrix products, arithmetic and copies ran while one was open for 19% of the time, Pallas kernels for 4%

profile of v1, /device:TPU:0, one launch (start us, length us, event | category | flops | bytes accessed | tf_op | source)
XLA Modules:
  0.0 915.7 jit_solution(8232869579537991041)
XLA Ops:
  2.9 5.8 collective-permute-start
  8.8 4.2 copy.100
  16.5 5.3 reshape_reshape.2
  22.5 9.0 convolution_convert_fusion.2.q_ref.ko_ref.vo_ref
  40.4 10.1 %collective-permute-done.1 = bf16[256,1024]{0,1:T(8,128)(2,1)S(1)} collective-permute-done((bf16[256,1024]{0,1:T(8,128)(2,1)}, bf16[256,1024]{0,1:T(8,128)(2,1)S(1)}, u32[]{:S(2)}, u32[]{:S(2)}) %collective-permute-start.1) | collective-permute-done | bytes 524320 | tf_op jit(solution)/shard_map/ppermute | solution.py:645
  60.7 36.7 %self_forward.1 = (bf16[768,1024]{1,0:T(8,128)(2,1)S(1)}, f32[768,512]{1,0:T(8,128)S(1)}) custom-call(s32[2]{0:T(128)S(1)} %fusion.160.need_ref, bf16[768,3072]{1,0:T(8,128)(2,1)S(1)} %bitcast.484, bf16[768,3072]{1,0:T(8,128)(2,1)S(1)} %bitcast.484, bf16[768,3072]{1,0:T(8,128)(2,1)S(1)} %bitcast.484, bf16[512,2048]{1,0:T(8,128)(2,1)S(1)} %fusion.20.kh_ref.vh_ref, ...), custom_call_target="tpu_custom_call" | custom-call | flops 6000000000 | bytes 12000000 | tf_op jit(solution)/shard_map/self_forward/pallas_call | solution.py:150
  124.8 6.3 convolution_convert_fusion.4.k_ref.v_ref
  131.4 39.9 %cross_forward.1 = (bf16[768,1024]{1,0:T(8,128)(2,1)S(1)}, f32[768,512]{1,0:T(8,128)S(1)}) custom-call(s32[1]{0:T(128)} %bitcast.7.z_ref, s32[2]{0:T(128)S(1)} %get-tuple-element.66.lo_ref, s32[2]{0:T(128)S(1)} %get-tuple-element.65.count_ref, bf16[768,1024]{1,0:T(8,128)(2,1)S(1)} %convolution_convert_fusion.10.q_ref, ...), custom_call_target="tpu_custom_call" | custom-call | flops 6000000000 | bytes 12000000 | tf_op jit(solution)/shard_map/cross_forward/pallas_call | solution.py:360
  175.2 26.0 %up_gelu.1 = (bf16[768,4096]{1,0:T(8,128)(2,1)S(1)}, bf16[768,4096]{1,0:T(8,128)(2,1)S(1)}) custom-call(bf16[768,1024]{1,0:T(8,128)(2,1)S(1)} %fusion.25.x_ref, bf16[1024,4096]{1,0:T(8,128)(2,1)} %w_ref.1, f32[1,4096]{1,0:T(1,128)S(1)} %bitcast.482), custom_call_target="tpu_custom_call" | custom-call | flops 19327352832 | bytes 22000000 | tf_op jit(solution)/shard_map/up_gelu/pallas_call | solution.py:485
  201.2 12.5 %fusion.173 = (f32[768]{0:T(1024)S(1)}, f32[768,1024]{1,0:T(8,128)S(1)}) fusion(f32[1024]{0:T(1024)S(1)} %copy-done.108, bf16[768,4096]{1,0:T(8,128)(2,1)S(1)} %get-tuple-element.32, bf16[4096,1024]{1,0:T(8,128)(2,1)} %param.29, f32[1024]{0:T(1024)S(1)} %bitcast.592, f32[1024]{0:T(1024)S(1)} %bitcast.587, f32[768]{0:T(1024)S(1)} %add_rsqrt_fusion.1, ...), kind=kOutput, calls=%fused_computation.455 | convolution fusion | flops 6447954944 | bytes 20993024 | tf_op jit(solution)/shard_map/dot_general | solution.py:635
  221.5 13.2 %fusion = (f32[4096]{0:T(1024)}, bf16[768,4096]{1,0:T(8,128)(2,1)}) fusion(bf16[768,4096]{1,0:T(8,128)(2,1)S(1)} %get-tuple-element.33, bf16[768,1024]{1,0:T(8,128)(2,1)S(1)} %convert_element_type.995, bf16[4096,1024]{1,0:T(8,128)(2,1)} %param.29), kind=kOutput, calls=%fused_computation.1 | convolution fusion | flops 6461321216 | bytes 22560768 | tf_op jit(solution)/shard_map/dot_general | solution.py:638
  234.7 12.4 %multiply_reduce_fusion = (f32[1024]{0:T(1024)S(1)}, f32[768]{0:T(1024)S(1)}, f32[768]{0:T(1024)S(1)}, f32[1024]{0:T(1024)S(1)}, f32[768,1024]{1,0:T(8,128)S(1)}) fusion(f32[768,1024]{1,0:T(8,128)S(1)} %copy-done.26, f32[768]{0:T(1024)S(1)} %add_rsqrt_fusion.1, f32[768]{0:T(1024)S(1)} %broadcast_multiply_fusion.7, f32[1024]{0:T(1024)S(1)} %bitcast.588, ...), kind=kOutput, calls=%fused_computation.35 | convolution fusion | flops 6451884032 | bytes 24141824 | tf_op jit(solution)/shard_map/dot_general | solution.py:638
  252.4 46.3 %cross_backward.1 = (bf16[768,1024]{1,0:T(8,128)(2,1)S(1)}, bf16[1024,2048]{1,0:T(8,128)(2,1)}) custom-call(s32[1]{0:T(128)} %bitcast.7.z_ref, s32[2]{0:T(128)S(1)} %get-tuple-element.66.lo_ref, s32[2]{0:T(128)S(1)} %get-tuple-element.65.count_ref, bf16[768,1024]{1,0:T(8,128)(2,1)S(1)} %copy-done.20, bf16[1024,2048]{1,0:T(8,128)(2,1)} %copy-done.18, ...), custom_call_target="tpu_custom_call" | custom-call | flops 20000000000 | bytes 24000000 | tf_op jit(solution)/shard_map/cross_backward/pallas_call | solution.py:441
  298.7 5.0 multiply_reduce_fusion.1
  309.3 74.9 %self_backward.1 = (bf16[768,3072]{1,0:T(8,128)(2,1)}, bf16[512,2048]{1,0:T(8,128)(2,1)}, bf16[768,512]{1,0:T(8,128)(2,1)S(1)}) custom-call(s32[2]{0:T(128)S(1)} %fusion.160.need_ref, bf16[768,3072]{1,0:T(8,128)(2,1)} %convolution_convert_fusion.2.q_ref.ko_ref.vo_ref, bf16[768,3072]{1,0:T(8,128)(2,1)} %convolution_convert_fusion.2.q_ref.ko_ref.vo_ref, ...), custom_call_target="tpu_custom_call" | custom-call | flops 20000000000 | bytes 24000000 | tf_op jit(solution)/shard_map/self_backward/pallas_call | solution.py:279
  384.2 8.8 fusion.176
  408.6 11.0 %reshape.701 = bf16[768,2,2,2,2,2,128]{6,5,4,3,2,1,0:T(2,128)(2,1)} reshape(bf16[768,4096]{1,0:T(8,128)(2,1)} %copy-done.2) | data formatting | bytes 12582912 | tf_op jit(solution)/shard_map/reshape | solution.py:551
  419.6 5.8 constant_dynamic-slice_fusion.3
  425.5 3.9 constant_dynamic-slice_fusion.5
  433.5 4.7 fusion.38
  440.4 6.3 fusion.174
  447.9 82.5 %collective-permute-start.9 = (bf16[256,1024]{1,0:T(8,128)(2,1)}, bf16[256,1024]{1,0:T(8,128)(2,1)}, u32[]{:S(2)}, u32[]{:S(2)}) collective-permute-start(bf16[256,1024]{1,0:T(8,128)(2,1)} %get-tuple-element.85), channel_id=1, source_target_pairs={{0,1},{1,2},{2,3},{3,0},{4,5},{5,6},{6,7},{7,4},{8,9},{9,10},{10,1... | collective-permute-start | bytes 1572872 | tf_op jit(solution)/shard_map/ppermute | solution.py:718
  549.5 3.8 convolution_convert_fusion.5
  556.7 3.9 fusion.182
  560.7 5.5 convolution_convert_fusion.1
  567.8 3.8 reshape.702
  571.6 5.7 fusion.183
  577.2 6.2 reshape.703
  583.4 8.0 convolution_convert_fusion.3
  596.9 27.0 %collective-permute-start.57 = (f32[2,2,1,352]{3,2,1,0:T(1,128)S(1)}, f32[2,2,1,352]{3,2,1,0:T(1,128)S(1)}, u32[]{:S(2)}, u32[]{:S(2)}) collective-permute-start(f32[2,2,1,352]{3,2,1,0:T(1,128)S(1)} %fusion.135), channel_id=1, source_target_pairs={{0,16},{4,20},{8,24},{12,28},{16,0},{20,4},{24,8},{28,12},{1,17},{... | collective-permute-start | bytes 16904 | tf_op jit(solution)/shard_map/ppermute | solution.py:540
  632.7 3.8 reshape.705
  649.4 4.4 collective-permute-done.27
  674.0 11.6 %collective-permute-done.6 = bf16[256,1024]{1,0:T(8,128)(2,1)S(1)} collective-permute-done((bf16[256,1024]{1,0:T(8,128)(2,1)S(1)}, bf16[256,1024]{1,0:T(8,128)(2,1)S(1)}, u32[]{:S(2)}, u32[]{:S(2)}) %collective-permute-start.6) | collective-permute-done | bytes 524320 | tf_op jit(solution)/shard_map/ppermute | solution.py:732
  693.8 6.7 collective-permute-done.16
  702.8 7.5 collective-permute-done.11
  713.8 11.3 %collective-permute-done.36 = bf16[256,1024]{1,0:T(8,128)(2,1)S(1)} collective-permute-done((bf16[256,1024]{1,0:T(8,128)(2,1)S(1)}, bf16[256,1024]{1,0:T(8,128)(2,1)S(1)}, u32[]{:S(2)}, u32[]{:S(2)}) %collective-permute-start.36) | collective-permute-done | bytes 524320 | tf_op jit(solution)/shard_map/ppermute | solution.py:540
  725.7 8.6 collective-permute-done.46
  737.0 6.3 collective-permute-done.17
  747.1 5.4 collective-permute-done.32
  792.3 9.1 collective-permute-done.41
  811.8 10.9 %collective-permute-done.42 = bf16[2,2,32,2048]{3,2,0,1:T(8,128)(2,1)S(1)} collective-permute-done((bf16[2,2,32,2048]{3,2,0,1:T(8,128)(2,1)S(1)}, bf16[2,2,32,2048]{3,2,0,1:T(8,128)(2,1)S(1)}, u32[]{:S(2)}, u32[]{:S(2)}) %collective-permute-start.42) | collective-permute-done | bytes 524320 | tf_op jit(solution)/shard_map/ppermute | solution.py:540
  829.3 15.4 %collective-permute-done.51 = bf16[256,4096]{1,0:T(8,128)(2,1)S(1)} collective-permute-done((bf16[256,4096]{1,0:T(8,128)(2,1)S(1)}, bf16[256,4096]{1,0:T(8,128)(2,1)S(1)}, u32[]{:S(2)}, u32[]{:S(2)}) %collective-permute-start.51) | collective-permute-done | bytes 2097184 | tf_op jit(solution)/shard_map/ppermute | solution.py:540
  847.3 26.4 %collective-permute-done.61 = bf16[1024,1024]{1,0:T(8,128)(2,1)S(1)} collective-permute-done((bf16[1024,1024]{1,0:T(8,128)(2,1)S(1)}, bf16[1024,1024]{1,0:T(8,128)(2,1)S(1)}, u32[]{:S(2)}, u32[]{:S(2)}) %collective-permute-start.61) | collective-permute-done | bytes 2097184 | tf_op jit(solution)/shard_map/ppermute | solution.py:540
  876.4 8.5 collective-permute-done.52
  886.1 4.1 collective-permute-done.62
  890.8 6.3 collective-permute-done.53
  898.7 6.5 collective-permute-done.63
  908.2 6.4 collective-permute-done.64
  (603 shorter events, 259.0 us)
Async XLA Ops:
  2.9 33.4 %collective-permute-start = (bf16[256,1024]{0,1:T(8,128)(2,1)}, bf16[256,1024]{0,1:T(8,128)(2,1)}, u32[]{:S(2)}, u32[]{:S(2)}) collective-permute-start(bf16[256,1024]{0,1:T(8,128)(2,1)} %bitcast.4), channel_id=1, source_target_pairs={{0,1},{1,2},{2,3},{4,5},{5,6},{6,7},{8,9},{9,10},{10,11},{12,13},{... | collective-permute-start | bytes 1572872 | tf_op jit(solution)/shard_map/ppermute | solution.py:645
  36.4 14.2 %collective-permute-start.1 = (bf16[256,1024]{0,1:T(8,128)(2,1)}, bf16[256,1024]{0,1:T(8,128)(2,1)S(1)}, u32[]{:S(2)}, u32[]{:S(2)}) collective-permute-start(bf16[256,1024]{0,1:T(8,128)(2,1)} %collective-permute-done), channel_id=1, source_target_pairs={{0,1},{1,2},{2,3},{4,5},{5,6},{6,7},{8,9},{9,10},{10,11},{12,13},{... | collective-permute-start | bytes 1572872 | tf_op jit(solution)/shard_map/ppermute | solution.py:645
  51.7 72.7 %collective-permute-start.4 = (bf16[256,1024]{0,1:T(8,128)(2,1)S(1)}, bf16[256,1024]{0,1:T(8,128)(2,1)}, u32[]{:S(2)}, u32[]{:S(2)}) collective-permute-start(bf16[256,1024]{0,1:T(8,128)(2,1)S(1)} %bitcast.528), channel_id=1, source_target_pairs={{0,3},{1,0},{2,1},{3,2},{4,7},{5,4},{6,5},{7,6},{8,11},{9,8},{10,9... | collective-permute-start | bytes 1572872 | tf_op jit(solution)/shard_map/ppermute | solution.py:651
  54.9 69.6 %collective-permute-start.3 = (bf16[256,1024]{0,1:T(8,128)(2,1)S(1)}, bf16[256,1024]{0,1:T(8,128)(2,1)}, u32[]{:S(2)}, u32[]{:S(2)}) collective-permute-start(bf16[256,1024]{0,1:T(8,128)(2,1)S(1)} %bitcast.529), channel_id=1, source_target_pairs={{0,2},{1,3},{2,0},{3,1},{4,6},{5,7},{6,4},{7,5},{8,10},{9,11},{10,... | collective-permute-start | bytes 1572872 | tf_op jit(solution)/shard_map/ppermute | solution.py:651
  55.6 68.9 %collective-permute-start.2 = (bf16[256,1024]{0,1:T(8,128)(2,1)S(1)}, bf16[256,1024]{0,1:T(8,128)(2,1)}, u32[]{:S(2)}, u32[]{:S(2)}) collective-permute-start(bf16[256,1024]{0,1:T(8,128)(2,1)S(1)} %bitcast.530), channel_id=1, source_target_pairs={{0,1},{1,2},{2,3},{3,0},{4,5},{5,6},{6,7},{7,4},{8,9},{9,10},{10,1... | collective-permute-start | bytes 1572872 | tf_op jit(solution)/shard_map/ppermute | solution.py:651
  439.1 220.0 %collective-permute-start.5 = (bf16[256,1024]{1,0:T(8,128)(2,1)}, bf16[256,1024]{1,0:T(8,128)(2,1)}, u32[]{:S(2)}, u32[]{:S(2)}) collective-permute-start(bf16[256,1024]{1,0:T(8,128)(2,1)} %slice.120), channel_id=1, source_target_pairs={{1,0},{2,1},{3,2},{5,4},{6,5},{7,6},{9,8},{10,9},{11,10},{13,12},{... | collective-permute-start | bytes 1572872 | tf_op jit(solution)/shard_map/ppermute | solution.py:732
  447.9 206.0 %collective-permute-start.9 = (bf16[256,1024]{1,0:T(8,128)(2,1)}, bf16[256,1024]{1,0:T(8,128)(2,1)}, u32[]{:S(2)}, u32[]{:S(2)}) collective-permute-start(bf16[256,1024]{1,0:T(8,128)(2,1)} %get-tuple-element.85), channel_id=1, source_target_pairs={{0,1},{1,2},{2,3},{3,0},{4,5},{5,6},{6,7},{7,4},{8,9},{9,10},{10,1... | collective-permute-start | bytes 1572872 | tf_op jit(solution)/shard_map/ppermute | solution.py:718
  530.5 124.1 %collective-permute-start.8 = (bf16[256,1024]{1,0:T(8,128)(2,1)}, bf16[256,1024]{1,0:T(8,128)(2,1)}, u32[]{:S(2)}, u32[]{:S(2)}) collective-permute-start(bf16[256,1024]{1,0:T(8,128)(2,1)} %get-tuple-element.86), channel_id=1, source_target_pairs={{0,2},{1,3},{2,0},{3,1},{4,6},{5,7},{6,4},{7,5},{8,10},{9,11},{10,... | collective-permute-start | bytes 1572872 | tf_op jit(solution)/shard_map/ppermute | solution.py:718
  542.3 96.6 %collective-permute-start.25 = (bf16[512,512]{1,0:T(8,128)(2,1)}, bf16[512,512]{1,0:T(8,128)(2,1)}, u32[]{:S(2)}, u32[]{:S(2)}) collective-permute-start(bf16[512,512]{1,0:T(8,128)(2,1)} %convolution_convert_fusion.15), channel_id=1, source_target_pairs={{0,4},{4,0},{8,12},{12,8},{16,20},{20,16},{24,28},{28,24},{1,5},{5... | collective-permute-start | bytes 1572872 | tf_op jit(solution)/shard_map/ppermute | solution.py:540
  567.2 25.8 %collective-permute-start.55 = (f32[2,2,2,2,1,352]{5,4,3,2,1,0:T(1,128)S(1)}, f32[2,2,2,2,1,352]{5,4,3,2,1,0:T(1,128)S(1)}, u32[]{:S(2)}, u32[]{:S(2)}) collective-permute-start(f32[2,2,2,2,1,352]{5,4,3,2,1,0:T(1,128)S(1)} %fusion.129), channel_id=1, source_target_pairs={{0,4},{4,0},{8,12},{12,8},{16,20},{20,16},{24,28},{28,24},{1,5},{5... | collective-permute-start | bytes 67592 | tf_op jit(solution)/shard_map/ppermute | solution.py:540
  596.9 28.6 %collective-permute-start.57 = (f32[2,2,1,352]{3,2,1,0:T(1,128)S(1)}, f32[2,2,1,352]{3,2,1,0:T(1,128)S(1)}, u32[]{:S(2)}, u32[]{:S(2)}) collective-permute-start(f32[2,2,1,352]{3,2,1,0:T(1,128)S(1)} %fusion.135), channel_id=1, source_target_pairs={{0,16},{4,20},{8,24},{12,28},{16,0},{20,4},{24,8},{28,12},{1,17},{... | collective-permute-start | bytes 16904 | tf_op jit(solution)/shard_map/ppermute | solution.py:540
  629.2 7.4 collective-permute-start.59
  636.5 18.1 %collective-permute-start.7 = (bf16[256,1024]{1,0:T(8,128)(2,1)}, bf16[256,1024]{1,0:T(8,128)(2,1)}, u32[]{:S(2)}, u32[]{:S(2)}) collective-permute-start(bf16[256,1024]{1,0:T(8,128)(2,1)} %get-tuple-element.84), channel_id=1, source_target_pairs={{0,3},{1,0},{2,1},{3,2},{4,7},{5,4},{6,5},{7,6},{8,11},{9,8},{10,9... | collective-permute-start | bytes 1572872 | tf_op jit(solution)/shard_map/ppermute | solution.py:718
  653.9 11.3 %collective-permute-start.20 = (bf16[512,1024]{1,0:T(8,128)(2,1)}, bf16[512,1024]{1,0:T(8,128)(2,1)S(1)}, u32[]{:S(2)}, u32[]{:S(2)}) collective-permute-start(bf16[512,1024]{1,0:T(8,128)(2,1)} %add_convert_fusion.1), channel_id=1, source_target_pairs={{0,4},{4,0},{8,12},{12,8},{16,20},{20,16},{24,28},{28,24},{1,5},{5... | collective-permute-start | bytes 3145736 | tf_op jit(solution)/shard_map/ppermute | solution.py:540
  654.0 11.9 %collective-permute-start.15 = (bf16[512,1024]{1,0:T(8,128)(2,1)}, bf16[512,1024]{1,0:T(8,128)(2,1)S(1)}, u32[]{:S(2)}, u32[]{:S(2)}) collective-permute-start(bf16[512,1024]{1,0:T(8,128)(2,1)} %add_convert_fusion.2), channel_id=1, source_target_pairs={{0,4},{4,0},{8,12},{12,8},{16,20},{20,16},{24,28},{28,24},{1,5},{5... | collective-permute-start | bytes 3145736 | tf_op jit(solution)/shard_map/ppermute | solution.py:540
  654.5 11.5 %collective-permute-start.10 = (bf16[512,1024]{1,0:T(8,128)(2,1)}, bf16[512,1024]{1,0:T(8,128)(2,1)S(1)}, u32[]{:S(2)}, u32[]{:S(2)}) collective-permute-start(bf16[512,1024]{1,0:T(8,128)(2,1)} %convolution_convert_fusion.14), channel_id=1, source_target_pairs={{0,4},{4,0},{8,12},{12,8},{16,20},{20,16},{24,28},{28,24},{1,5},{5... | collective-permute-start | bytes 3145736 | tf_op jit(solution)/shard_map/ppermute | solution.py:540
  659.1 7.6 collective-permute-start.30
  665.2 112.5 %collective-permute-start.40 = (bf16[512,2048]{1,0:T(8,128)(2,1)S(1)}, bf16[512,2048]{1,0:T(8,128)(2,1)S(1)}, u32[]{:S(2)}, u32[]{:S(2)}) collective-permute-start(bf16[512,2048]{1,0:T(8,128)(2,1)S(1)} %copy-done.106), channel_id=1, source_target_pairs={{0,4},{4,0},{8,12},{12,8},{16,20},{20,16},{24,28},{28,24},{1,5},{5... | collective-permute-start | bytes 6291464 | tf_op jit(solution)/shard_map/ppermute | solution.py:540
  666.0 135.9 %collective-permute-start.50 = (bf16[512,4096]{1,0:T(8,128)(2,1)}, bf16[512,4096]{1,0:T(8,128)(2,1)S(1)}, u32[]{:S(2)}, u32[]{:S(2)}) collective-permute-start(bf16[512,4096]{1,0:T(8,128)(2,1)} %convolution_convert_fusion.1), channel_id=1, source_target_pairs={{0,4},{4,0},{8,12},{12,8},{16,20},{20,16},{24,28},{28,24},{1,5},{5... | collective-permute-start | bytes 12582920 | tf_op jit(solution)/shard_map/ppermute | solution.py:540
  667.9 155.0 %collective-permute-start.60 = (bf16[2048,1024]{1,0:T(8,128)(2,1)S(1)}, bf16[2048,1024]{1,0:T(8,128)(2,1)S(1)}, u32[]{:S(2)}, u32[]{:S(2)}) collective-permute-start(bf16[2048,1024]{1,0:T(8,128)(2,1)S(1)} %copy-done.102), channel_id=1, source_target_pairs={{0,4},{4,0},{8,12},{12,8},{16,20},{20,16},{24,28},{28,24},{1,5},{5... | collective-permute-start | bytes 12582920 | tf_op jit(solution)/shard_map/ppermute | solution.py:540
  669.5 16.1 %collective-permute-start.6 = (bf16[256,1024]{1,0:T(8,128)(2,1)S(1)}, bf16[256,1024]{1,0:T(8,128)(2,1)S(1)}, u32[]{:S(2)}, u32[]{:S(2)}) collective-permute-start(bf16[256,1024]{1,0:T(8,128)(2,1)S(1)} %add_convert_fusion.3), channel_id=1, source_target_pairs={{1,0},{2,1},{3,2},{5,4},{6,5},{7,6},{9,8},{10,9},{11,10},{13,12},{... | collective-permute-start | bytes 1572872 | tf_op jit(solution)/shard_map/ppermute | solution.py:732
  671.1 20.2 %collective-permute-start.21 = (bf16[256,1024]{1,0:T(8,128)(2,1)S(1)}, bf16[256,1024]{1,0:T(8,128)(2,1)S(1)}, u32[]{:S(2)}, u32[]{:S(2)}) collective-permute-start(bf16[256,1024]{1,0:T(8,128)(2,1)S(1)} %fusion.70), channel_id=1, source_target_pairs={{0,16},{4,20},{8,24},{12,28},{16,0},{20,4},{24,8},{28,12},{1,17},{... | collective-permute-start | bytes 1572872 | tf_op jit(solution)/shard_map/ppermute | solution.py:540
  685.6 14.8 %collective-permute-start.16 = (bf16[256,1024]{1,0:T(8,128)(2,1)S(1)}, bf16[256,1024]{1,0:T(8,128)(2,1)S(1)}, u32[]{:S(2)}, u32[]{:S(2)}) collective-permute-start(bf16[256,1024]{1,0:T(8,128)(2,1)S(1)} %fusion.73), channel_id=1, source_target_pairs={{0,8},{4,12},{8,0},{12,4},{16,24},{20,28},{24,16},{28,20},{1,9},{5... | collective-permute-start | bytes 1572872 | tf_op jit(solution)/shard_map/ppermute | solution.py:540
  691.4 18.9 %collective-permute-start.11 = (bf16[256,1024]{1,0:T(8,128)(2,1)S(1)}, bf16[256,1024]{1,0:T(8,128)(2,1)S(1)}, u32[]{:S(2)}, u32[]{:S(2)}) collective-permute-start(bf16[256,1024]{1,0:T(8,128)(2,1)S(1)} %fusion.76), channel_id=1, source_target_pairs={{0,8},{4,12},{8,0},{12,4},{16,24},{20,28},{24,16},{28,20},{1,9},{5... | collective-permute-start | bytes 1572872 | tf_op jit(solution)/shard_map/ppermute | solution.py:540
  700.5 12.3 %collective-permute-start.31 = (bf16[256,1024]{1,0:T(8,128)(2,1)S(1)}, bf16[256,1024]{1,0:T(8,128)(2,1)S(1)}, u32[]{:S(2)}, u32[]{:S(2)}) collective-permute-start(bf16[256,1024]{1,0:T(8,128)(2,1)S(1)} %fusion.67), channel_id=1, source_target_pairs={{0,16},{4,20},{8,24},{12,28},{16,0},{20,4},{24,8},{28,12},{1,17},{... | collective-permute-start | bytes 1572872 | tf_op jit(solution)/shard_map/ppermute | solution.py:540
  710.3 14.9 %collective-permute-start.36 = (bf16[256,1024]{1,0:T(8,128)(2,1)S(1)}, bf16[256,1024]{1,0:T(8,128)(2,1)S(1)}, u32[]{:S(2)}, u32[]{:S(2)}) collective-permute-start(bf16[256,1024]{1,0:T(8,128)(2,1)S(1)} %fusion.64), channel_id=1, source_target_pairs={{0,16},{4,20},{8,24},{12,28},{16,0},{20,4},{24,8},{28,12},{1,17},{... | collective-permute-start | bytes 1572872 | tf_op jit(solution)/shard_map/ppermute | solution.py:540
  712.8 21.5 %collective-permute-start.46 = (bf16[256,1024]{1,0:T(8,128)(2,1)S(1)}, bf16[256,1024]{1,0:T(8,128)(2,1)S(1)}, u32[]{:S(2)}, u32[]{:S(2)}) collective-permute-start(bf16[256,1024]{1,0:T(8,128)(2,1)S(1)} %fusion.60), channel_id=1, source_target_pairs={{0,16},{4,20},{8,24},{12,28},{16,0},{20,4},{24,8},{28,12},{1,17},{... | collective-permute-start | bytes 1572872 | tf_op jit(solution)/shard_map/ppermute | solution.py:540
  725.1 11.4 %collective-permute-start.22 = (bf16[2,2,32,1024]{3,2,0,1:T(8,128)(2,1)S(1)}, bf16[2,2,32,1024]{3,2,0,1:T(8,128)(2,1)S(1)}, u32[]{:S(2)}, u32[]{:S(2)}) collective-permute-start(bf16[2,2,32,1024]{3,2,0,1:T(8,128)(2,1)S(1)} %bitcast.570), channel_id=1, source_target_pairs={{0,8},{4,12},{8,0},{12,4},{16,24},{20,28},{24,16},{28,20},{1,9},{5... | collective-permute-start | bytes 786440 | tf_op jit(solution)/shard_map/ppermute | solution.py:540
  734.3 9.0 collective-permute-start.17
  736.6 9.5 %collective-permute-start.12 = (bf16[2,2,32,1024]{3,2,0,1:T(8,128)(2,1)S(1)}, bf16[2,2,32,1024]{3,2,0,1:T(8,128)(2,1)S(1)}, u32[]{:S(2)}, u32[]{:S(2)}) collective-permute-start(bf16[2,2,32,1024]{3,2,0,1:T(8,128)(2,1)S(1)} %bitcast.575), channel_id=1, source_target_pairs={{0,16},{4,20},{8,24},{12,28},{16,0},{20,4},{24,8},{28,12},{1,17},{... | collective-permute-start | bytes 786440 | tf_op jit(solution)/shard_map/ppermute | solution.py:540
  743.3 9.2 %collective-permute-start.32 = (bf16[2,2,32,1024]{3,2,0,1:T(8,128)(2,1)S(1)}, bf16[2,2,32,1024]{3,2,0,1:T(8,128)(2,1)S(1)}, u32[]{:S(2)}, u32[]{:S(2)}) collective-permute-start(bf16[2,2,32,1024]{3,2,0,1:T(8,128)(2,1)S(1)} %bitcast.574), channel_id=1, source_target_pairs={{0,8},{4,12},{8,0},{12,4},{16,24},{20,28},{24,16},{28,20},{1,9},{5... | collective-permute-start | bytes 786440 | tf_op jit(solution)/shard_map/ppermute | solution.py:540
  746.1 10.9 %collective-permute-start.37 = (bf16[2,2,32,1024]{3,2,0,1:T(8,128)(2,1)S(1)}, bf16[2,2,32,1024]{3,2,0,1:T(8,128)(2,1)S(1)}, u32[]{:S(2)}, u32[]{:S(2)}) collective-permute-start(bf16[2,2,32,1024]{3,2,0,1:T(8,128)(2,1)S(1)} %bitcast.573), channel_id=1, source_target_pairs={{0,8},{4,12},{8,0},{12,4},{16,24},{20,28},{24,16},{28,20},{1,9},{5... | collective-permute-start | bytes 786440 | tf_op jit(solution)/shard_map/ppermute | solution.py:540
  774.6 8.7 collective-permute-start.24
  777.2 8.2 collective-permute-start.19
  777.8 8.7 collective-permute-start.14
  783.3 18.1 %collective-permute-start.41 = (bf16[256,2048]{1,0:T(8,128)(2,1)S(1)}, bf16[256,2048]{1,0:T(8,128)(2,1)S(1)}, u32[]{:S(2)}, u32[]{:S(2)}) collective-permute-start(bf16[256,2048]{1,0:T(8,128)(2,1)S(1)} %fusion.35), channel_id=1, source_target_pairs={{0,8},{4,12},{8,0},{12,4},{16,24},{20,28},{24,16},{28,20},{1,9},{5... | collective-permute-start | bytes 3145736 | tf_op jit(solution)/shard_map/ppermute | solution.py:540
  790.5 19.8 %collective-permute-start.49 = (bf16[32,1024]{1,0:T(8,128)(2,1)S(1)}, bf16[32,1024]{1,0:T(8,128)(2,1)S(1)}, u32[]{:S(2)}, u32[]{:S(2)}) collective-permute-start(bf16[32,1024]{1,0:T(8,128)(2,1)S(1)} %dynamic-slice_bitcast_fusion.12), channel_id=1, source_target_pairs={{0,2},{1,3},{2,0},{3,1},{4,6},{5,7},{6,4},{7,5},{8,10},{9,11},{10,... | collective-permute-start | bytes 196616 | tf_op jit(solution)/shard_map/ppermute | solution.py:540
  805.5 39.2 %collective-permute-start.51 = (bf16[256,4096]{1,0:T(8,128)(2,1)S(1)}, bf16[256,4096]{1,0:T(8,128)(2,1)S(1)}, u32[]{:S(2)}, u32[]{:S(2)}) collective-permute-start(bf16[256,4096]{1,0:T(8,128)(2,1)S(1)} %fusion.5), channel_id=1, source_target_pairs={{0,8},{4,12},{8,0},{12,4},{16,24},{20,28},{24,16},{28,20},{1,9},{5... | collective-permute-start | bytes 6291464 | tf_op jit(solution)/shard_map/ppermute | solution.py:540
  807.5 15.2 %collective-permute-start.42 = (bf16[2,2,32,2048]{3,2,0,1:T(8,128)(2,1)S(1)}, bf16[2,2,32,2048]{3,2,0,1:T(8,128)(2,1)S(1)}, u32[]{:S(2)}, u32[]{:S(2)}) collective-permute-start(bf16[2,2,32,2048]{3,2,0,1:T(8,128)(2,1)S(1)} %bitcast.566), channel_id=1, source_target_pairs={{0,16},{4,20},{8,24},{12,28},{16,0},{20,4},{24,8},{28,12},{1,17},{... | collective-permute-start | bytes 1572872 | tf_op jit(solution)/shard_map/ppermute | solution.py:540
  822.8 24.1 %collective-permute-start.43 = (bf16[2,32,2048]{2,1,0:T(8,128)(2,1)S(1)}, bf16[2,32,2048]{2,1,0:T(8,128)(2,1)S(1)}, u32[]{:S(2)}, u32[]{:S(2)}) collective-permute-start(bf16[2,32,2048]{2,1,0:T(8,128)(2,1)S(1)} %dynamic-slice_bitcast_fusion.4), channel_id=1, source_target_pairs={{0,1},{1,0},{2,3},{3,2},{4,5},{5,4},{6,7},{7,6},{8,9},{9,8},{10,11... | collective-permute-start | bytes 786440 | tf_op jit(solution)/shard_map/ppermute | solution.py:540
  826.8 46.9 %collective-permute-start.61 = (bf16[1024,1024]{1,0:T(8,128)(2,1)S(1)}, bf16[1024,1024]{1,0:T(8,128)(2,1)S(1)}, u32[]{:S(2)}, u32[]{:S(2)}) collective-permute-start(bf16[1024,1024]{1,0:T(8,128)(2,1)S(1)} %fusion.2), channel_id=1, source_target_pairs={{0,16},{4,20},{8,24},{12,28},{16,0},{20,4},{24,8},{28,12},{1,17},{... | collective-permute-start | bytes 6291464 | tf_op jit(solution)/shard_map/ppermute | solution.py:540
  846.1 38.8 %collective-permute-start.52 = (bf16[2,2,32,4096]{3,2,0,1:T(8,128)(2,1)S(1)}, bf16[2,2,32,4096]{3,2,0,1:T(8,128)(2,1)S(1)}, u32[]{:S(2)}, u32[]{:S(2)}) collective-permute-start(bf16[2,2,32,4096]{3,2,0,1:T(8,128)(2,1)S(1)} %bitcast.550), channel_id=1, source_target_pairs={{0,16},{4,20},{8,24},{12,28},{16,0},{20,4},{24,8},{28,12},{1,17},{... | collective-permute-start | bytes 3145736 | tf_op jit(solution)/shard_map/ppermute | solution.py:540
  847.0 38.3 %collective-permute-start.44 = (bf16[32,2048]{1,0:T(8,128)(2,1)S(1)}, bf16[32,2048]{1,0:T(8,128)(2,1)S(1)}, u32[]{:S(2)}, u32[]{:S(2)}) collective-permute-start(bf16[32,2048]{1,0:T(8,128)(2,1)S(1)} %dynamic-slice_bitcast_fusion.6), channel_id=1, source_target_pairs={{0,2},{1,3},{2,0},{3,1},{4,6},{5,7},{6,4},{7,5},{8,10},{9,11},{10,... | collective-permute-start | bytes 393224 | tf_op jit(solution)/shard_map/ppermute | solution.py:540
  875.3 14.9 %collective-permute-start.62 = (bf16[2,2,128,1024]{3,2,0,1:T(8,128)(2,1)S(1)}, bf16[2,2,128,1024]{3,2,0,1:T(8,128)(2,1)S(1)}, u32[]{:S(2)}, u32[]{:S(2)}) collective-permute-start(bf16[2,2,128,1024]{3,2,0,1:T(8,128)(2,1)S(1)} %bitcast.551), channel_id=1, source_target_pairs={{0,8},{4,12},{8,0},{12,4},{16,24},{20,28},{24,16},{28,20},{1,9},{5... | collective-permute-start | bytes 3145736 | tf_op jit(solution)/shard_map/ppermute | solution.py:540
  885.2 11.8 %collective-permute-start.53 = (bf16[2,32,4096]{2,1,0:T(8,128)(2,1)S(1)}, bf16[2,32,4096]{2,1,0:T(8,128)(2,1)S(1)}, u32[]{:S(2)}, u32[]{:S(2)}) collective-permute-start(bf16[2,32,4096]{2,1,0:T(8,128)(2,1)S(1)} %dynamic-slice_bitcast_fusion.1), channel_id=1, source_target_pairs={{0,1},{1,0},{2,3},{3,2},{4,5},{5,4},{6,7},{7,6},{8,9},{9,8},{10,11... | collective-permute-start | bytes 1572872 | tf_op jit(solution)/shard_map/ppermute | solution.py:540
  890.7 14.5 %collective-permute-start.63 = (bf16[2,128,1024]{2,1,0:T(8,128)(2,1)S(1)}, bf16[2,128,1024]{2,1,0:T(8,128)(2,1)S(1)}, u32[]{:S(2)}, u32[]{:S(2)}) collective-permute-start(bf16[2,128,1024]{2,1,0:T(8,128)(2,1)S(1)} %dynamic-slice_bitcast_fusion), channel_id=1, source_target_pairs={{0,1},{1,0},{2,3},{3,2},{4,5},{5,4},{6,7},{7,6},{8,9},{9,8},{10,11... | collective-permute-start | bytes 1572872 | tf_op jit(solution)/shard_map/ppermute | solution.py:540
  897.2 10.2 %collective-permute-start.54 = (bf16[32,4096]{1,0:T(8,128)(2,1)S(1)}, bf16[32,4096]{1,0:T(8,128)(2,1)S(1)}, u32[]{:S(2)}, u32[]{:S(2)}) collective-permute-start(bf16[32,4096]{1,0:T(8,128)(2,1)S(1)} %dynamic-slice_bitcast_fusion.3), channel_id=1, source_target_pairs={{0,2},{1,3},{2,0},{3,1},{4,6},{5,7},{6,4},{7,5},{8,10},{9,11},{10,... | collective-permute-start | bytes 786440 | tf_op jit(solution)/shard_map/ppermute | solution.py:540
  905.5 9.1 collective-permute-start.64
  (144 other events, 2055.0 us)

commit v2 on v1

v2 whole, which is shorter than its diff:
```python
import functools
import math

import jax
import jax.numpy as jnp
from jax import lax
from jax.experimental import pallas as pl
from jax.experimental.pallas import tpu as pltpu
from jax.sharding import PartitionSpec as P

HEAD_DIM = 64
BUCKETS = 32
STREAMS = 3
HALO = 512
TILE = 128
PAIR = 2 * TILE
ROWS = 2 * STREAMS * TILE
NEG = -1e30
SCALE = HEAD_DIM ** (-0.5)

bucket_edges = [
    int(math.ceil(16.0 * 8.0 ** (bucket_level / 16.0))) for bucket_level in range(1, 16)
]


def bucket_of(distance):
    forward_gap = jnp.maximum(distance, 0)
    far_bucket = jnp.full_like(forward_gap, 16)
    for bucket_edge in bucket_edges:
        far_bucket = far_bucket + (forward_gap >= bucket_edge).astype(jnp.int32)
    return jnp.where(forward_gap < 16, forward_gap, far_bucket)


def iota(shape, axis):
    return lax.broadcasted_iota(jnp.int32, shape, axis)


def dot(a, b, ca, cb):
    return lax.dot_general(a, b, (((ca,), (cb,)), ((), ())), preferred_element_type=jnp.float32)


def bias_tables():
    col = iota((PAIR, PAIR), 1)
    gap = jnp.where(col < TILE, (TILE - col) % TILE, PAIR)
    row = iota((PAIR, PAIR), 0) % TILE
    back = TILE - 1 - iota((TILE, TILE), 0)
    lane = iota((TILE, TILE), 1)
    skews = [(bucket_of(gap) + BUCKETS * h == row).astype(jnp.bfloat16) for h in range(4)]
    hots = [(bucket_of(back) + BUCKETS * h == lane).astype(jnp.bfloat16) for h in range(4)]
    return jnp.concatenate(skews, axis=0), jnp.concatenate(hots, axis=0)


def head_masks():
    low = (iota((TILE, TILE), 1) < HEAD_DIM).astype(jnp.float32)
    return low.astype(jnp.bfloat16), (1.0 - low).astype(jnp.bfloat16)


def stream_rows(s, local, here):
    return pl.ds(pl.multiple_of(s * local + here, TILE), TILE)


def stack_heads(ref, local, here, lanes, masks, extra=None, scale=None):
    out = []
    for s in range(STREAMS):
        x = ref[stream_rows(s, local, here), lanes]
        if scale is not None:
            x = x * jnp.bfloat16(scale)
        for mask in masks:
            y = x * mask
            out.append(y if extra is None else jnp.concatenate([y, extra], axis=1))
    return jnp.concatenate(out, axis=0)


def part(n):
    return slice(n * TILE, (n + 1) * TILE)


def lane_max(x):
    return jnp.broadcast_to(jnp.max(x, axis=1, keepdims=True), (TILE, TILE))


def lane_sum(x):
    return jnp.broadcast_to(jnp.sum(x, axis=1, keepdims=True), (TILE, TILE))


def roll_rows(x):
    return pltpu.roll(x, 0, 1, stride=1, stride_axis=0)


WINDOWS = ((-TILE, PAIR, 0), (-3 * TILE, PAIR, PAIR), (-4 * TILE, TILE, 2 * PAIR))
REACH = 5 * TILE


def columns(rows, base):
    return pl.BlockSpec((rows, PAIR), lambda g, *_: (0, base + g))


def whole(rows, cols):
    return pl.BlockSpec((rows, cols), lambda g, *_: (0, 0))


def weights_spec(steps, reach):
    return pl.BlockSpec((1, steps, ROWS, reach), lambda g, *_: (g, 0, 0, 0))


def self_fwd_kernel(nq, need_ref, q_ref, ko_ref, vo_ref, kh_ref, vh_ref, rel_ref, doc_ref, aug_ref, skew_ref,
                    mix_ref, pr_ref, kx, vx, sc, st, bz):
    local = nq * TILE
    for p in range(2):
        kx[p, :HALO, :TILE] = kh_ref[:, part(p)]
        kx[p, HALO:, :TILE] = ko_ref[:local, part(p)]
        kx[p, :, TILE:] = aug_ref[...]
    vx[:HALO, :] = vh_ref[...]
    vx[HALO:, :] = vo_ref[:local, :]
    masks = head_masks()
    lane = iota((TILE, TILE), 1)
    row = iota((TILE, TILE), 0)

    def step(n, _):
        i, p = n // 2, n % 2
        here = pl.multiple_of(i * TILE, TILE)
        lanes = pl.ds(pl.multiple_of(p * TILE, TILE), TILE)
        qs = stack_heads(q_ref, local, here, lanes, masks, doc_ref[pl.ds(here, TILE), :], SCALE)
        table = []
        for s in range(STREAMS):
            rel = rel_ref[stream_rows(s, local, here), :]
            high = rel.astype(jnp.bfloat16)
            table.append(jnp.concatenate([high, (rel - high.astype(jnp.float32)).astype(jnp.bfloat16)], axis=1))
        table = jnp.concatenate(table, axis=0)
        for j in range(2):
            bz[j, :, :] = dot(table, skew_ref[pl.ds(pl.multiple_of((2 * p + j) * PAIR, PAIR), PAIR), :], 1, 0)

        def path(count):
            windows = []
            for off, width, at in WINDOWS[:count]:
                keys = pl.ds(pl.multiple_of(here + HALO + off, TILE), width)
                sc[:, at : at + width] = dot(qs, kx[p, keys, :], 1, 1)
                windows.append((at, width, keys))
            reach = windows[-1][0] + windows[-1][1]
            for b in range(2 * STREAMS):
                s, j = b // 2, b % 2
                rows = stream_rows(s, local, here)
                near = roll_rows(bz[j, part(s), :TILE])
                steady = bz[j, part(s), TILE:]
                left = sc[part(b), part(0)] + jnp.where(lane > row, near, steady)
                right = sc[part(b), part(1)]
                if s > 0:
                    own = lane_sum(qs[part(b), :TILE].astype(jnp.float32) * ko_ref[rows, lanes].astype(jnp.float32))
                    right = jnp.where(lane == row, own, right)
                right = right + jnp.where(lane <= row, near, NEG)
                far = [sc[part(b), part(m)] for m in range(2, reach // TILE)]
                top = jnp.maximum(left, right)
                if far:
                    most = far[0]
                    for x in far[1:]:
                        most = jnp.maximum(most, x)
                    top = jnp.maximum(top, most + steady)
                top = lane_max(top)
                base = top - steady
                weights = [jnp.exp(left - top), jnp.exp(right - top)] + [jnp.exp(x - base) for x in far]
                total = weights[0]
                for x in weights[1:]:
                    total = total + x
                inverse = 1.0 / lane_sum(total)
                for m, x in enumerate(weights):
                    x = (x * inverse).astype(jnp.bfloat16)
                    pr_ref[0, n, part(b), part(m)] = x
                    if m == 1 and s > 0:
                        st[part(b), :] = lane_sum(jnp.where(lane == row, x.astype(jnp.float32), 0.0))
            if reach < REACH:
                pr_ref[0, n, :, reach:] = jnp.zeros((ROWS, REACH - reach), jnp.bfloat16)
            acc = None
            for at, width, keys in windows:
                o = dot(pr_ref[0, n, :, at : at + width], vx[keys, lanes], 1, 0)
                acc = o if acc is None else acc + o
            main = vo_ref[stream_rows(0, local, here), lanes].astype(jnp.float32)
            for s in range(STREAMS):
                rows = stream_rows(s, local, here)
                a, b = part(2 * s), part(2 * s + 1)
                mixed = jnp.where(lane < HEAD_DIM, acc[a], acc[b])
                if s > 0:
                    own = jnp.where(lane < HEAD_DIM, st[a, :], st[b, :])
                    mixed = mixed + own * (vo_ref[rows, lanes].astype(jnp.float32) - main)
                mix_ref[rows, lanes] = mixed.astype(jnp.bfloat16)

        for count in range(1, 4):
            @pl.when(need_ref[i] == count)
            def _():
                path(count)
        return 0

    lax.fori_loop(0, 2 * nq, step, 0)


def self_forward(need, proj, halo_kv, rel, doc, aug, skew):
    tokens = proj.shape[0]
    local = tokens // STREAMS
    width = proj.shape[1] // 3
    grid = width // PAIR
    steps = 2 * local // TILE
    return pl.pallas_call(
        functools.partial(self_fwd_kernel, local // TILE),
        grid_spec=pltpu.PrefetchScalarGridSpec(
            num_scalar_prefetch=1, grid=(grid,),
            in_specs=[
                columns(tokens, 0), columns(tokens, grid), columns(tokens, 2 * grid), columns(HALO, 0), columns(HALO, grid),
                pl.BlockSpec((tokens, TILE), lambda g, *_: (0, g)),
                whole(local, TILE), whole(HALO + local, TILE), whole(4 * PAIR, PAIR),
            ],
            out_specs=[columns(tokens, 0), weights_spec(steps, REACH)],
            scratch_shapes=[
                pltpu.VMEM((2, HALO + local, PAIR), jnp.bfloat16), pltpu.VMEM((HALO + local, PAIR), jnp.bfloat16),
                pltpu.VMEM((ROWS, REACH), jnp.float32), pltpu.VMEM((ROWS, TILE), jnp.float32),
                pltpu.VMEM((2, STREAMS * TILE, PAIR), jnp.float32),
            ]),
        out_shape=[jax.ShapeDtypeStruct((tokens, width), jnp.bfloat16),
                   jax.ShapeDtypeStruct((grid, steps, ROWS, REACH), jnp.bfloat16)],
        compiler_params=pltpu.CompilerParams(vmem_limit_bytes=40 << 20),
        cost_estimate=pl.CostEstimate(flops=15_000_000_000, bytes_accessed=20_000_000, transcendentals=8_000_000),
        name="self_forward",
    )(need, proj, proj, proj, halo_kv, halo_kv, rel, doc, aug, skew)


def self_bwd_kernel(nq, plan, q_ref, ko_ref, vo_ref, kh_ref, vh_ref, hot_ref, mix_ref, up_ref, pr_ref, *refs):
    arrays, handed, refs = refs[: plan.many], refs[plan.many], refs[plan.many + 1 :]
    dproj_ref, dhalo_ref, drel_ref, sums_ref, got, kx, vx, dp, pz, ds, cb, st, dkt, dvt, dqa = refs[:15]
    g = pl.program_id(0)
    comm = Comm(plan, arrays, sums_ref, refs[15:-1])
    hand = Handing(handed.shape[0] + 1, handed.shape[0], True, handed, got, refs[-1])

    @pl.when(g == 0)
    def _():
        comm.barrier()
        hand.start()

    local = nq * TILE
    kx[:HALO, :] = kh_ref[...]
    kx[HALO:, :] = ko_ref[:local, :]
    vx[:HALO, :] = vh_ref[...]
    vx[HALO:, :] = vo_ref[:local, :]
    dkt[...] = jnp.zeros_like(dkt)
    dvt[...] = jnp.zeros_like(dvt)
    masks = head_masks()
    lane = iota((TILE, TILE), 1)
    row = iota((TILE, TILE), 0)
    flip = (row + lane == TILE - 1).astype(jnp.float32).astype(jnp.bfloat16)
    gl = pl.multiple_of(g * PAIR, PAIR)
    third = q_ref.shape[1] * pl.num_programs(0)

    def step(n, _):
        i, p = n // 2, n % 2
        here = pl.multiple_of(i * TILE, TILE)
        lanes = pl.ds(pl.multiple_of(p * TILE, TILE), TILE)
        comm.step(g * 2 * nq + n)
        qs = stack_heads(q_ref, local, here, lanes, masks, None, SCALE)
        ups = stack_heads(up_ref, local, here, lanes, masks)
        qt = qs.T
        upt = ups.T

        def window(w):
            off, width, at = WINDOWS[w]
            keys = pl.ds(pl.multiple_of(here + HALO + off, TILE), width)
            dp[:, :width] = dot(ups, vx[keys, lanes], 1, 1)
            for b in range(2 * STREAMS):
                s = b // 2
                rows = stream_rows(s, local, here)
                if w == 0:
                    upf = ups[part(b)].astype(jnp.float32)
                    centre = lane_sum(upf * mix_ref[rows, lanes].astype(jnp.float32))
                    st[0, part(b), :] = centre
                else:
                    centre = st[0, part(b), :]
                far = None
                for m in range(width // TILE):
                    x = pr_ref[0, n, part(b), slice(at + m * TILE, at + (m + 1) * TILE)]
                    xf = x.astype(jnp.float32)
                    y = (xf * (dp[part(b), part(m)] - centre)).astype(jnp.bfloat16)
                    if w > 0:
                        ds[part(b), part(m)] = y
                        far = y.astype(jnp.float32) if far is None else far + y.astype(jnp.float32)
                        continue
                    yf = y.astype(jnp.float32)
                    if m == 0:
                        ds[part(b), part(0)] = y
                        pz[part(b), part(0)] = x
                        band = jnp.where(lane > row, yf, 0.0)
                        st[3, part(b), :] = yf - band
                        continue
                    if s > 0:
                        own_weight = lane_sum(jnp.where(lane == row, xf, 0.0))
                        own_grad = own_weight * (lane_sum(upf * vo_ref[rows, lanes].astype(jnp.float32)) - centre)
                        own_grad = own_grad.astype(jnp.bfloat16).astype(jnp.float32)
                        st[1, part(b), :] = own_weight
                        st[2, part(b), :] = own_grad
                        xf = jnp.where(lane == row, 0.0, xf)
                        yf = jnp.where(lane == row, 0.0, yf)
                        band = band + jnp.where(lane == row, own_grad, yf)
                        pz[part(b), part(1)] = xf.astype(jnp.bfloat16)
                        ds[part(b), part(1)] = yf.astype(jnp.bfloat16)
                    else:
                        band = band + yf
                        pz[part(b), part(1)] = x
                        ds[part(b), part(1)] = y
                    cb[:, part(b)] = band.astype(jnp.bfloat16)
                if w > 0:
                    st[3, part(b), :] += far
            grad = ds[:, :width]
            weights = pz[...] if w == 0 else pr_ref[0, n, :, at : at + width]
            dkt[p, :, keys] += dot(qt, grad, 1, 0)
            dvt[p, :, keys] += dot(upt, weights, 1, 0)
            return dot(grad, kx[keys, lanes], 1, 0)

        dqa[...] = window(0)
        turned = dot(flip, cb[...], 1, 0)
        rolled = [roll_rows(turned[:, part(b)]).astype(jnp.bfloat16) for b in range(2 * STREAMS)]
        rolled = jnp.concatenate([jnp.concatenate(rolled[2 * s : 2 * s + 2], axis=1) for s in range(STREAMS)], axis=0)
        table = dot(rolled, hot_ref[pl.ds(pl.multiple_of(p * PAIR, PAIR), PAIR), :], 1, 0).astype(jnp.bfloat16)
        table = dot(flip, jnp.concatenate([table[part(s)] for s in range(STREAMS)], axis=1), 1, 0)

        dq = dqa[...] + window(1) + window(2)
        for s in range(STREAMS):
            rows = stream_rows(s, local, here)
            a, b = part(2 * s), part(2 * s + 1)
            dqs = jnp.where(lane < HEAD_DIM, dq[a], dq[b])
            col = pl.multiple_of(gl + p * TILE, TILE)
            if s > 0:
                own_weight = jnp.where(lane < HEAD_DIM, st[1, a, :], st[1, b, :])
                own_grad = jnp.where(lane < HEAD_DIM, st[2, a, :], st[2, b, :])
                dqs = dqs + own_grad * ko_ref[rows, lanes].astype(jnp.float32)
                dproj_ref[rows, pl.ds(pl.multiple_of(col + third, TILE), TILE)] = (
                    own_grad * (SCALE * q_ref[rows, lanes].astype(jnp.float32))
                ).astype(jnp.bfloat16)
                dproj_ref[rows, pl.ds(pl.multiple_of(col + 2 * third, TILE), TILE)] = (
                    own_weight * up_ref[rows, lanes].astype(jnp.float32)
                ).astype(jnp.bfloat16)
            dproj_ref[rows, pl.ds(col, TILE)] = (SCALE * dqs).astype(jnp.bfloat16)
            dr = table[:, part(s)]
            for j, blk in enumerate((a, b)):
                dr = dr + jnp.where(lane == BUCKETS * (2 * p + j) + BUCKETS - 1, lane_sum(st[3, blk, :]), 0.0)

            @pl.when(p == 0)
            def _():
                drel_ref[rows, :] = dr.astype(jnp.bfloat16)

            @pl.when(p == 1)
            def _():
                drel_ref[rows, :] = (drel_ref[rows, :].astype(jnp.float32) + dr).astype(jnp.bfloat16)
        return 0

    lax.fori_loop(0, 2 * nq, step, 0)
    for p in range(2):
        for j, acc in enumerate((dkt, dvt)):
            col = pl.multiple_of(gl + p * TILE + third * j, TILE)
            full = acc[p, :, :].T.astype(jnp.bfloat16)
            dhalo_ref[:, pl.ds(col, TILE)] = full[:HALO]
            dproj_ref[:local, pl.ds(pl.multiple_of(col + third, TILE), TILE)] = full[HALO:]

    @pl.when(g == pl.num_programs(0) - 1)
    def _():
        comm.rest(4 * 2 * nq)
        hand.wait()


def self_backward(plan, arrays, handed, proj, halo_kv, hot, mix, up, weights):
    tokens = proj.shape[0]
    local = tokens // STREAMS
    width = proj.shape[1] // 3
    grid = width // PAIR
    steps = 2 * local // TILE
    return pl.pallas_call(
        functools.partial(self_bwd_kernel, local // TILE, plan),
        grid=(grid,),
        in_specs=[
            columns(tokens, 0), columns(tokens, grid), columns(tokens, 2 * grid), columns(HALO, 0), columns(HALO, grid),
            whole(4 * TILE, TILE), columns(tokens, 0), columns(tokens, 0), weights_spec(steps, REACH),
        ] + plan.in_specs() + [pl.BlockSpec(memory_space=pl.ANY)],
        out_specs=[
            whole(tokens, 3 * width), whole(HALO, 2 * width), pl.BlockSpec((tokens, TILE), lambda g, *_: (0, g)), plan.out_spec(),
            pl.BlockSpec(memory_space=pl.ANY),
        ],
        scratch_shapes=[
            pltpu.VMEM((HALO + local, PAIR), jnp.bfloat16), pltpu.VMEM((HALO + local, PAIR), jnp.bfloat16),
            pltpu.VMEM((ROWS, PAIR), jnp.float32), pltpu.VMEM((ROWS, PAIR), jnp.bfloat16),
            pltpu.VMEM((ROWS, PAIR), jnp.bfloat16), pltpu.VMEM((TILE, ROWS), jnp.bfloat16),
            pltpu.VMEM((4, ROWS, TILE), jnp.float32),
            pltpu.VMEM((2, TILE, HALO + local), jnp.float32), pltpu.VMEM((2, TILE, HALO + local), jnp.float32),
            pltpu.VMEM((ROWS, TILE), jnp.float32),
        ] + plan.scratch() + handing_scratch(handed.shape[0]),
        out_shape=[
            jax.ShapeDtypeStruct((tokens, 3 * width), jnp.bfloat16), jax.ShapeDtypeStruct((HALO, 2 * width), jnp.bfloat16),
            jax.ShapeDtypeStruct((tokens, width // 2), jnp.bfloat16), plan.out_shape(),
            jax.ShapeDtypeStruct(handed.shape, handed.dtype),
        ],
        compiler_params=pltpu.CompilerParams(collective_id=plan.number, has_side_effects=True, vmem_limit_bytes=56 << 20),
        cost_estimate=pl.CostEstimate(flops=40_000_000_000, bytes_accessed=30_000_000, transcendentals=8_000_000),
        name="self_backward",
    )(proj, proj, proj, halo_kv, halo_kv, hot, mix, up, weights, *plan.views(arrays), handed)


def gather_shards(local, ref, place):
    shards = ref.shape[0] // local
    z = lax.axis_index("seq")
    for k in range(shards):
        at = pl.ds(pl.multiple_of(lax.rem(z - k + shards, shards) * local, TILE), local)
        place(at, ref[k * local : (k + 1) * local, :])


def cross_fwd_kernel(nq, lo_ref, count_ref, q_ref, k_ref, v_ref, doc_ref, aug_ref, mix_ref, pr_ref, kx, vx, sc):
    local = nq * TILE
    across = k_ref.shape[0] // PAIR

    def place_key(at, block):
        for p in range(2):
            kx[p, at, :TILE] = block[:, part(p)]

    def place_value(at, block):
        vx[at, :] = block

    gather_shards(local, k_ref, place_key)
    gather_shards(local, v_ref, place_value)
    for p in range(2):
        kx[p, :, TILE:] = aug_ref[...]
    masks = head_masks()
    lane = iota((TILE, TILE), 1)

    def step(n, _):
        i, p = n // 2, n % 2
        here = pl.multiple_of(i * TILE, TILE)
        lanes = pl.ds(pl.multiple_of(p * TILE, TILE), TILE)
        qs = stack_heads(q_ref, local, here, lanes, masks, doc_ref[pl.ds(here, TILE), :], SCALE)

        def window(w):
            return pl.ds(pl.multiple_of((lo_ref[i] + w) * PAIR, PAIR), PAIR)

        def path(count):
            for w in range(count):
                sc[:, w * PAIR : (w + 1) * PAIR] = dot(qs, kx[p, window(w), :], 1, 1)
            for b in range(2 * STREAMS):
                xs = [sc[part(b), part(m)] for m in range(2 * count)]
                top = xs[0]
                for x in xs[1:]:
                    top = jnp.maximum(top, x)
                top = lane_max(top)
                xs = [jnp.exp(x - top) for x in xs]
                total = xs[0]
                for x in xs[1:]:
                    total = total + x
                inverse = 1.0 / lane_sum(total)
                xs = [(x * inverse).astype(jnp.bfloat16) for x in xs]
                for w in range(count):
                    pr_ref[0, n, part(b), window(w)] = jnp.concatenate(xs[2 * w : 2 * w + 2], axis=1)
            total = None
            for w in range(count):
                o = dot(pr_ref[0, n, :, window(w)], vx[window(w), lanes], 1, 0)
                total = o if total is None else total + o
            for s in range(STREAMS):
                mixed = jnp.where(lane < HEAD_DIM, total[part(2 * s)], total[part(2 * s + 1)])
                mix_ref[stream_rows(s, local, here), lanes] = mixed.astype(jnp.bfloat16)

        for count in range(1, across + 1):
            @pl.when(count_ref[i] == count)
            def _():
                path(count)

        for w in range(across):
            @pl.when((w < lo_ref[i]) | (w >= lo_ref[i] + count_ref[i]))
            def _():
                pr_ref[0, n, :, w * PAIR : (w + 1) * PAIR] = jnp.zeros((ROWS, PAIR), jnp.bfloat16)
        return 0

    lax.fori_loop(0, 2 * nq, step, 0)


def cross_forward(lo, count, q, kv, doc, aug):
    tokens, width = q.shape
    local = tokens // STREAMS
    full = kv.shape[0]
    grid = width // PAIR
    steps = 2 * local // TILE
    return pl.pallas_call(
        functools.partial(cross_fwd_kernel, local // TILE),
        grid_spec=pltpu.PrefetchScalarGridSpec(
            num_scalar_prefetch=2, grid=(grid,),
            in_specs=[columns(tokens, 0), columns(full, 0), columns(full, grid), whole(local, TILE), whole(full, TILE)],
            out_specs=[columns(tokens, 0), weights_spec(steps, full)],
            scratch_shapes=[
                pltpu.VMEM((2, full, PAIR), jnp.bfloat16), pltpu.VMEM((full, PAIR), jnp.bfloat16),
                pltpu.VMEM((ROWS, full), jnp.float32),
            ]),
        out_shape=[jax.ShapeDtypeStruct((tokens, width), jnp.bfloat16), jax.ShapeDtypeStruct((grid, steps, ROWS, full), jnp.bfloat16)],
        compiler_params=pltpu.CompilerParams(vmem_limit_bytes=48 << 20),
        cost_estimate=pl.CostEstimate(flops=15_000_000_000, bytes_accessed=20_000_000, transcendentals=8_000_000),
        name="cross_forward",
    )(lo, count, q, kv, kv, doc, aug)


def cross_bwd_kernel(nq, plan, q_ref, k_ref, v_ref, mix_ref, up_ref, pr_ref, *refs):
    arrays, refs = refs[: plan.many], refs[plan.many :]
    dq_ref, dkv_ref, sums_ref, kx, vx, dp, ds, st, dkt, dvt, dqa = refs[:11]
    g = pl.program_id(0)
    comm = Comm(plan, arrays, sums_ref, refs[11:])

    @pl.when(g == 0)
    def _():
        comm.barrier()

    local = nq * TILE

    def place_key(at, block):
        kx[at, :] = block

    def place_value(at, block):
        vx[at, :] = block

    gather_shards(local, k_ref, place_key)
    gather_shards(local, v_ref, place_value)
    dkt[...] = jnp.zeros_like(dkt)
    dvt[...] = jnp.zeros_like(dvt)
    masks = head_masks()
    lane = iota((TILE, TILE), 1)

    def step(n, _):
        i, p = n // 2, n % 2
        here = pl.multiple_of(i * TILE, TILE)
        lanes = pl.ds(pl.multiple_of(p * TILE, TILE), TILE)
        comm.step(g * 2 * nq + n)
        qs = stack_heads(q_ref, local, here, lanes, masks, None, SCALE)
        ups = stack_heads(up_ref, local, here, lanes, masks)
        qt = qs.T
        upt = ups.T
        for b in range(2 * STREAMS):
            rows = stream_rows(b // 2, local, here)
            st[part(b), :] = lane_sum(ups[part(b)].astype(jnp.float32) * mix_ref[rows, lanes].astype(jnp.float32))
        dqa[...] = jnp.zeros_like(dqa)

        def window(w, _):
            at = pl.ds(pl.multiple_of(w * PAIR, PAIR), PAIR)
            dp[...] = dot(ups, vx[at, lanes], 1, 1)
            for b in range(2 * STREAMS):
                x = pr_ref[0, n, part(b), at].astype(jnp.float32)
                for m in range(2):
                    ds[part(b), part(m)] = (x[:, part(m)] * (dp[part(b), part(m)] - st[part(b), :])).astype(jnp.bfloat16)
            dkt[p, :, at] += dot(qt, ds[...], 1, 0)
            dvt[p, :, at] += dot(upt, pr_ref[0, n, :, at], 1, 0)
            dqa[...] += dot(ds[...], kx[at, lanes], 1, 0)
            return 0

        lax.fori_loop(0, k_ref.shape[0] // PAIR, window, 0)
        for s in range(STREAMS):
            dq = jnp.where(lane < HEAD_DIM, dqa[part(2 * s), :], dqa[part(2 * s + 1), :])
            dq_ref[stream_rows(s, local, here), lanes] = (SCALE * dq).astype(jnp.bfloat16)
        return 0

    lax.fori_loop(0, 2 * nq, step, 0)
    third = q_ref.shape[1] * pl.num_programs(0)
    shards = k_ref.shape[0] // local
    z = lax.axis_index("seq")
    for p in range(2):
        for j, acc in enumerate((dkt, dvt)):
            col = pl.multiple_of(g * PAIR + p * TILE + third * j, TILE)
            for k in range(shards):
                at = pl.ds(pl.multiple_of(lax.rem(z - k + shards, shards) * local, TILE), local)
                dkv_ref[k * local : (k + 1) * local, pl.ds(col, TILE)] = acc[p, :, at].T.astype(jnp.bfloat16)

    @pl.when(g == pl.num_programs(0) - 1)
    def _():
        comm.rest(4 * 2 * nq)


def cross_backward(plan, arrays, q, kv, mix, up, weights):
    tokens, width = q.shape
    local = tokens // STREAMS
    full = kv.shape[0]
    grid = width // PAIR
    steps = 2 * local // TILE
    return pl.pallas_call(
        functools.partial(cross_bwd_kernel, local // TILE, plan),
        grid=(grid,),
        in_specs=[
            columns(tokens, 0), columns(full, 0), columns(full, grid),
            columns(tokens, 0), columns(tokens, 0), weights_spec(steps, full),
        ] + plan.in_specs(),
        out_specs=[columns(tokens, 0), whole(full, 2 * width), plan.out_spec()],
        scratch_shapes=[
            pltpu.VMEM((full, PAIR), jnp.bfloat16), pltpu.VMEM((full, PAIR), jnp.bfloat16),
            pltpu.VMEM((ROWS, PAIR), jnp.float32), pltpu.VMEM((ROWS, PAIR), jnp.bfloat16),
            pltpu.VMEM((ROWS, TILE), jnp.float32),
            pltpu.VMEM((2, TILE, full), jnp.float32), pltpu.VMEM((2, TILE, full), jnp.float32),
            pltpu.VMEM((ROWS, TILE), jnp.float32),
        ] + plan.scratch(),
        out_shape=[
            jax.ShapeDtypeStruct((tokens, width), jnp.bfloat16), jax.ShapeDtypeStruct((full, 2 * width), jnp.bfloat16),
            plan.out_shape(),
        ],
        compiler_params=pltpu.CompilerParams(collective_id=plan.number, has_side_effects=True, vmem_limit_bytes=58 << 20),
        cost_estimate=pl.CostEstimate(flops=40_000_000_000, bytes_accessed=30_000_000, transcendentals=8_000_000),
        name="cross_backward",
    )(q, kv, kv, mix, up, weights, *plan.views(arrays))


CHUNK = 256
SLOTS = 8


class Route:
    def __init__(self, dp, seq):
        self.dp_bits = dp.bit_length() - 1
        self.bits = self.dp_bits + seq.bit_length() - 1
        core = self.dp_bits - 1
        rest = list(reversed(range(core)))
        tail = list(reversed(range(self.dp_bits, self.bits)))
        self.orders = ([core] + rest + tail, [core] + rest[::-1] + tail)
        steps = self.bits
        self.lags = [0, 1] + [min(1 + 2 * k, 5) + max(0, k - 2) for k in range(1, steps)]

    def place(self, bit):
        if bit < self.dp_bits:
            return "dp", self.dp_bits - 1 - bit
        return "seq", self.bits - 1 - bit

    def mine(self, bit):
        axis, k = self.place(bit)
        return lax.rem(lax.axis_index(axis) // (1 << k), 2)

    def partner(self, bit):
        axis, k = self.place(bit)
        index = lax.axis_index(axis)
        return {axis: index + (1 - 2 * self.mine(bit)) * (1 << k)}

    def left(self, kind, k):
        return sorted(set(range(self.bits)) - set(self.orders[kind][:k]))


class Plan:
    def __init__(self, route, shapes, number, chunk=CHUNK, kind=jnp.bfloat16):
        self.route, self.number, self.chunk, self.kind = route, number, chunk, kind
        rows = min(shape[0] for shape in shapes)
        self.deep = rows >> route.bits
        self.subs = [shape[0] // rows for shape in shapes]
        self.pairs = [sub * (shape[1] // (2 * chunk)) for sub, shape in zip(self.subs, shapes)]
        self.total, self.many = sum(self.pairs), len(shapes)
        self.iterations = self.total + route.lags[route.bits]

    def views(self, arrays):
        lead = lambda sub: (2,) * self.route.bits + ((sub,) if sub > 1 else ())
        return [a.reshape(lead(sub) + (self.deep, a.shape[1])) for a, sub in zip(arrays, self.subs)]

    def in_specs(self):
        return [pl.BlockSpec(memory_space=pl.ANY)] * self.many

    def out_shape(self):
        return jax.ShapeDtypeStruct((self.deep, self.total * 2 * self.chunk), jnp.float32)

    def out_spec(self):
        return pl.BlockSpec(self.out_shape().shape, lambda *_: (0, 0))

    def scratch(self):
        bits = self.route.bits
        shape = lambda lead: (SLOTS, 2) + (2,) * lead + (self.deep, self.chunk)
        own = [pltpu.VMEM(shape(bits - 1), self.kind)]
        got = [pltpu.VMEM(shape(bits - 1 - k), self.kind) for k in range(bits)]
        out = [pltpu.VMEM(shape(bits - 1 - k), self.kind) for k in range(1, bits)]
        kept = [pltpu.VMEM(shape(bits - 1 - k), jnp.float32) for k in range(1, bits)]
        sems = [pltpu.SemaphoreType.DMA((2, SLOTS))] + [pltpu.SemaphoreType.DMA((bits, 2, SLOTS))] * 2
        return own + got + out + kept + sems

    def blocks(self, sums):
        out, at = [], 0
        for sub, pairs in zip(self.subs, self.pairs):
            span = pairs * 2 * self.chunk
            block = sums[:, at : at + span]
            at += span
            if sub > 1:
                block = block.reshape(-1, sub, span // sub).transpose(1, 0, 2).reshape(-1, span // sub)
            out.append(block)
        return out


class Comm:
    def __init__(self, plan, arrays, result, scratch):
        route = plan.route
        bits = route.bits
        self.plan, self.route, self.arrays, self.result = plan, route, arrays, result
        self.pairs, self.subs, self.chunk, self.total = plan.pairs, plan.subs, plan.chunk, plan.total
        self.own = scratch[0]
        self.got = scratch[1 : 1 + bits]
        self.out = (None,) + tuple(scratch[1 + bits : 2 * bits])
        self.kept = (None,) + tuple(scratch[2 * bits : 3 * bits - 1])
        self.own_sem, self.send_sem, self.got_sem = scratch[3 * bits - 1 : 3 * bits + 2]

    def barrier(self):
        sem = pltpu.get_barrier_semaphore()
        size = 1 << (self.route.bits - self.route.dp_bits)
        others = [self.route.partner(bit) for bit in range(self.route.dp_bits)]
        others += [{"seq": lax.rem(lax.axis_index("seq") + k, size)} for k in range(1, size)]
        for other in others:
            pl.semaphore_signal(sem, inc=1, device_id=other, device_id_type=pl.DeviceIdType.MESH)
        pl.semaphore_wait(sem, len(others))

    def source(self, n, pair, kind, side):
        core = self.route.dp_bits - 1
        ref, subs = self.arrays[n], self.subs[n]
        across = ref.shape[-1] // (2 * self.chunk)
        col = pl.ds(pl.multiple_of(lax.rem(pair, across) * 2 * self.chunk + kind * self.chunk, self.chunk), self.chunk)
        index = [slice(None)] * self.route.bits
        index[core] = side
        if subs > 1:
            index.append(pair // across)
        return ref.at[tuple(index) + (slice(None), col)]

    def copy(self, k, kind, slot, src):
        return pltpu.make_async_remote_copy(
            src_ref=src,
            dst_ref=self.got[k].at[slot, kind],
            send_sem=self.send_sem.at[k, kind, slot],
            recv_sem=self.got_sem.at[k, kind, slot],
            device_id=self.route.partner(self.route.orders[kind][k]),
            device_id_type=pl.DeviceIdType.MESH,
        )

    def fetch(self, kind, slot, src):
        return pltpu.make_async_copy(src, self.own.at[slot, kind], self.own_sem.at[kind, slot])

    def begin(self, u):
        slot = lax.rem(u, SLOTS)
        side = self.route.mine(self.route.dp_bits - 1)
        first = 0
        for n, pairs in enumerate(self.pairs):
            @pl.when((u >= first) & (u < first + pairs))
            def _():
                for kind in range(2):
                    self.copy(0, kind, slot, self.source(n, u - first, kind, 1 - side)).start()
                    self.fetch(kind, slot, self.source(n, u - first, kind, side)).start()

            first += pairs

    def advance(self, k, u):
        route = self.route
        slot = lax.rem(u, SLOTS)
        for kind in range(2):
            if k == 1:
                filler = self.source(0, 0, kind, 0)
                self.fetch(kind, slot, filler).wait()
                self.copy(0, kind, slot, filler).wait()
                held = self.own
            else:
                self.copy(k - 1, kind, slot, self.out[k - 1].at[slot, kind]).wait()
                held = self.kept[k - 1]
            came = self.got[k - 1]
            if k == route.bits:
                total = held[slot, kind].astype(jnp.float32) + came[slot, kind].astype(jnp.float32)
                at = pl.multiple_of((2 * u + kind) * self.chunk, self.chunk)
                self.result[:, pl.ds(at, self.chunk)] = total
                continue
            bit = route.orders[kind][k]
            at = route.left(kind, k).index(bit)
            me = route.mine(bit)
            where = lambda side: (slot, kind) + (slice(None),) * at + (side,)
            theirs = where(1 - me)
            sent = held[theirs].astype(jnp.float32) + came[theirs].astype(jnp.float32)
            self.out[k][slot, kind] = sent.astype(self.out[k].dtype)
            self.copy(k, kind, slot, self.out[k].at[slot, kind]).start()
            ours = where(me)
            self.kept[k][slot, kind] = held[ours].astype(jnp.float32) + came[ours].astype(jnp.float32)

    def step(self, t):
        @pl.when(t < self.total)
        def _():
            self.begin(t)

        for k in range(1, self.route.bits + 1):
            u = t - self.route.lags[k]

            @pl.when((u >= 0) & (u < self.total))
            def _():
                self.advance(k, u)


    def rest(self, begin):
        def body(t, _):
            self.step(t)
            return 0

        lax.fori_loop(begin, self.plan.iterations, body, 0)


class Handing:
    def __init__(self, size, count, wraps, source, target, sems):
        self.size, self.count, self.wraps = size, count, wraps
        self.source, self.target, self.sems = source, target, sems

    def copies(self):
        z = lax.axis_index("seq")
        for k in range(1, self.count + 1):
            copy = pltpu.make_async_remote_copy(
                src_ref=self.source.at[k - 1],
                dst_ref=self.target.at[k - 1],
                send_sem=self.sems.at[0, k - 1],
                recv_sem=self.sems.at[1, k - 1],
                device_id={"seq": lax.rem(z - k + self.size, self.size)},
                device_id_type=pl.DeviceIdType.MESH,
            )
            yield copy, z >= k, z + k < self.size

    def start(self):
        for copy, sends, _ in self.copies():
            if self.wraps:
                copy.start()
            else:
                pl.when(sends)(copy.start)

    def wait(self):
        for copy, sends, gets in self.copies():
            if self.wraps:
                copy.wait()
            else:
                pl.when(sends)(copy.wait_send)
                pl.when(gets)(copy.wait_recv)


def handing_scratch(count):
    return [pltpu.SemaphoreType.DMA((2, count))]


def scatter_kernel(plan, few, size, *refs):
    many = plan.many
    arrays, small, handed = refs[:many], refs[many], refs[many + 1]
    result, small_result, got = refs[many + 2 : many + 5]
    scratch = refs[many + 5 : -1]
    half = len(scratch) // 2
    comm = Comm(plan, arrays, result, scratch[:half])
    other = Comm(few, [small], small_result, scratch[half:])
    hand = Handing(size, handed.shape[0], False, handed, got, refs[-1])
    comm.barrier()
    hand.start()

    def body(t, _):
        other.step(t)
        comm.step(t)
        return 0

    lax.fori_loop(0, plan.iterations, body, 0)
    hand.wait()


def scatter_sums(plan, few, size, arrays, small, handed):
    anywhere = pl.BlockSpec(memory_space=pl.ANY)
    return pl.pallas_call(
        functools.partial(scatter_kernel, plan, few, size),
        grid=(1,),
        in_specs=plan.in_specs() + few.in_specs() + [anywhere],
        out_specs=[plan.out_spec(), few.out_spec(), anywhere],
        out_shape=[plan.out_shape(), few.out_shape(), jax.ShapeDtypeStruct(handed.shape, handed.dtype)],
        scratch_shapes=plan.scratch() + few.scratch() + handing_scratch(handed.shape[0]),
        compiler_params=pltpu.CompilerParams(
            collective_id=plan.number, has_side_effects=True, vmem_limit_bytes=56 << 20
        ),
        cost_estimate=pl.CostEstimate(flops=20_000_000_000, bytes_accessed=60_000_000, transcendentals=0),
        name="weight_sums",
    )(*plan.views(arrays), *few.views([small]), handed)


def gelu_parts(x):
    u = jnp.abs(x) * (0.5**0.5)
    t = 1.0 / (1.0 + 0.5 * u)
    poly = jnp.float32(0.17087277)
    for coef in (-0.82215223, 1.48851587, -1.13520398, 0.27886807, -0.18628806, 0.09678418, 0.37409196, 1.00002368, -1.26551223):
        poly = poly * t + coef
    square = u * u
    half = 0.5 * t * jnp.exp(poly - square)
    below = jnp.where(x >= 0, 1.0 - half, half)
    dense = jnp.exp(-square) * (1.0 / math.sqrt(2.0 * math.pi))
    return x * below, below + x * dense


def up_kernel(x_ref, w_ref, b_ref, act_ref, slope_ref):
    rows = x_ref.shape[0]
    step = 256 if rows % 256 == 0 else TILE
    for r in range(0, rows, step):
        pre = dot(x_ref[r : r + step, :], w_ref[...], 1, 0) + b_ref[...]
        value, slope = gelu_parts(pre)
        act_ref[r : r + step, :] = value.astype(jnp.bfloat16)
        slope_ref[r : r + step, :] = slope.astype(jnp.bfloat16)


def up_gelu(x, w, b):
    tokens, width = x.shape
    hidden = w.shape[1]
    block = 512
    out = pl.BlockSpec((tokens, block), lambda j: (0, j))
    return pl.pallas_call(
        up_kernel,
        grid=(hidden // block,),
        in_specs=[
            pl.BlockSpec((tokens, width), lambda j: (0, 0)),
            pl.BlockSpec((width, block), lambda j: (0, j)),
            pl.BlockSpec((1, block), lambda j: (0, j)),
        ],
        out_specs=[out, out],
        out_shape=[jax.ShapeDtypeStruct((tokens, hidden), jnp.bfloat16)] * 2,
        compiler_params=pltpu.CompilerParams(vmem_limit_bytes=40 << 20),
        cost_estimate=pl.CostEstimate(
            flops=2 * tokens * width * hidden * 3, bytes_accessed=22_000_000, transcendentals=6_000_000
        ),
        name="up_gelu",
    )(x, w, b.reshape(1, hidden))


def normalize(hidden, gain, shift):
    centre = hidden - jnp.mean(hidden, axis=-1, keepdims=True)
    scale_inv = lax.rsqrt(jnp.mean(centre * centre, axis=-1, keepdims=True) + 1e-05)
    unit = centre * scale_inv
    return (unit * gain + shift, unit, scale_inv)


def normalize_back(upstream, unit, scale_inv, gain):
    along = upstream * gain
    inner = (
        along
        - jnp.mean(along, axis=-1, keepdims=True)
        - unit * jnp.mean(along * unit, axis=-1, keepdims=True)
    )
    return (scale_inv * inner, jnp.sum(upstream * unit, axis=0), jnp.sum(upstream, axis=0))


def gate(value, *others):
    return lax.optimization_barrier((value,) + others)[0]


def shards(
    inputs,
    encoded,
    target_lengths,
    source_lengths,
    query_key_value,
    bucket_weight,
    self_output,
    cross_query,
    cross_key_value,
    cross_output,
    up_weight,
    up_bias,
    down_weight,
    down_bias,
    norm_gain,
    norm_shift,
    cotangent,
):
    row_count, streams, local, width = inputs.shape
    parts, size = lax.axis_size("dp"), lax.axis_size("seq")
    route = Route(parts, size)
    full = local * size
    z = lax.axis_index("seq")
    begin = z * local
    bf16, f32 = jnp.bfloat16, jnp.float32
    tokens = streams * local
    up_chain = [(i, i + 1) for i in range(size - 1)]
    down_chain = [(i + 1, i) for i in range(size - 1)]

    def mm(left, right):
        return jnp.dot(left, right, preferred_element_type=f32)

    def mm_t(left, right):
        return lax.dot_general(left, right, (((1,), (1,)), ((), ())), preferred_element_type=f32)

    def wgrad(left, right):
        return dot(left, right, 0, 0).astype(bf16)

    flat = inputs.reshape(tokens, width)
    main = flat[:local]
    hops = HALO // local
    passing, pieces = main, []
    for _ in range(hops):
        passing = lax.ppermute(passing, "seq", up_chain)
        pieces.insert(0, passing)
    halo = jnp.concatenate(pieces, axis=0)
    own_source = encoded.reshape(local, width)
    waiting, halo = lax.optimization_barrier((own_source, halo))
    sources = [own_source] + [
        lax.ppermute(waiting, "seq", [(i, (i + k) % size) for i in range(size)]) for k in range(1, size)
    ]
    source = jnp.concatenate(sources, axis=0)

    here = begin + jnp.arange(local, dtype=jnp.int32)
    ends = jnp.cumsum(target_lengths[0])
    source_ends = jnp.cumsum(source_lengths[0])
    passed = here[:, None] >= ends[None, :]
    number = jnp.sum(passed.astype(jnp.int32), axis=1)
    start = jnp.max(jnp.where(passed, ends[None, :], 0), axis=1) - begin + HALO
    is_doc = number[:, None] == jnp.arange(ends.shape[0] + 1, dtype=jnp.int32)[None, :]
    zero = jnp.zeros((1,), jnp.int32)
    first = jnp.sum(jnp.where(is_doc, jnp.concatenate([zero, source_ends])[None, :], 0), axis=1)
    last = jnp.sum(jnp.where(is_doc, jnp.concatenate([source_ends, zero + full])[None, :], 0), axis=1)
    edge = start[::TILE]
    at = HALO + TILE * jnp.arange(local // TILE, dtype=jnp.int32)
    need = 1 + (edge < at - TILE).astype(jnp.int32) + (edge < at - 3 * TILE).astype(jnp.int32)
    low_key = first[::TILE] // PAIR
    count = (last[TILE - 1 :: TILE] + PAIR - 1) // PAIR - low_key

    names = jnp.arange(TILE, dtype=jnp.int32)[None, :]
    place = begin - HALO + jnp.arange(HALO + local, dtype=jnp.int32)
    key_doc = jnp.where(place >= 0, jnp.sum((place[:, None] >= ends[None, :]).astype(jnp.int32), axis=1), TILE)
    place = jnp.arange(full, dtype=jnp.int32)
    source_doc = jnp.sum((place[:, None] >= source_ends[None, :]).astype(jnp.int32), axis=1)
    doc = (number[:, None] == names).astype(bf16)
    block = lambda of: jnp.where((names < 8) & (of[:, None] != names), NEG, 0.0).astype(bf16)
    target_aug, source_aug = block(key_doc), block(source_doc)
    skew, hot = bias_tables()

    query_main = mm(flat, query_key_value).astype(bf16)
    relative = mm(flat, bucket_weight)
    proj = query_main
    halo_kv = mm(halo, query_key_value[:, width:]).astype(bf16)
    self_mix, self_weights = self_forward(need, proj, halo_kv, relative, doc, target_aug, skew)
    hidden_one, unit_one, inv_one = normalize(flat.astype(f32) + mm(self_mix, self_output), norm_gain[0], norm_shift[0])
    low_one = hidden_one.astype(bf16)
    cross_q = mm(low_one, cross_query).astype(bf16)
    source_kv = mm(source, cross_key_value).astype(bf16)
    cross_mix, cross_weights = cross_forward(low_key, count, cross_q, source_kv, doc, source_aug)
    hidden_two, unit_two, inv_two = normalize(hidden_one + mm(cross_mix, cross_output), norm_gain[1], norm_shift[1])
    low_two = hidden_two.astype(bf16)
    activated, slope = up_gelu(low_two, up_weight, up_bias)
    branch_three = mm(activated, down_weight) + down_bias
    result, unit_three, inv_three = normalize(hidden_two + branch_three, norm_gain[2], norm_shift[2])

    three_grad, gain_three, shift_three = normalize_back(
        cotangent.reshape(tokens, width).astype(f32), unit_three, inv_three, norm_gain[2]
    )
    three_low = three_grad.astype(bf16)
    down_bias_grad = jnp.sum(three_grad, axis=0)
    down_part = wgrad(activated, three_low)
    pre_grad = mm_t(three_low, down_weight).astype(bf16).astype(f32) * slope.astype(f32)
    up_bias_grad = jnp.sum(pre_grad, axis=0)
    pre_low = pre_grad.astype(bf16)
    up_part = wgrad(low_two, pre_low)
    hidden_two_grad = three_grad + mm_t(pre_low, up_weight).astype(bf16).astype(f32)
    two_grad, gain_two, shift_two = normalize_back(hidden_two_grad, unit_two, inv_two, norm_gain[1])
    two_low = two_grad.astype(bf16)
    cross_up = mm_t(two_low, cross_output).astype(bf16)
    wide = [up_part, down_part]
    wide_plan = Plan(route, [a.shape for a in wide], 0)
    query_low, source_low, wide_sums = cross_backward(
        wide_plan, wide, cross_q, source_kv, cross_mix, cross_up, cross_weights
    )
    up_grad, down_grad = wide_plan.blocks(wide_sums)
    source_back = mm_t(source_low, cross_key_value)
    back_low = source_back[local:].astype(bf16).reshape(size - 1, local, width)
    hidden_one_grad = two_grad + mm_t(query_low, cross_query).astype(bf16).astype(f32)
    one_grad, gain_one, shift_one = normalize_back(hidden_one_grad, unit_one, inv_one, norm_gain[0])
    one_low = one_grad.astype(bf16)
    self_up = mm_t(one_low, self_output).astype(bf16)
    square = [
        wgrad(source, source_low),
        wgrad(cross_mix, two_low),
        wgrad(low_one, query_low),
        wgrad(self_mix, one_low),
    ]
    square_plan = Plan(route, [a.shape for a in square], 1)
    proj_low, halo_low, table_low, square_sums, came = self_backward(
        square_plan, square, back_low, proj, halo_kv, hot, self_mix, self_up, self_weights
    )
    cross_kv_grad, cross_out_grad, cross_query_grad, self_out_grad = square_plan.blocks(square_sums)
    encoded_grad = source_back[:local] + jnp.sum(came.astype(f32), axis=0)
    halo_back = mm_t(halo_low, query_key_value[:, width:]).astype(bf16)
    handed = halo_back.reshape(hops, local, width)[::-1]
    back = mm_t(proj_low, query_key_value) + mm_t(table_low, bucket_weight)
    devices = parts * size
    gains = jnp.stack([gain_one, gain_two, gain_three]).reshape(3, devices, -1).transpose(1, 0, 2)
    shifts = jnp.stack([shift_one, shift_two, shift_three]).reshape(3, devices, -1).transpose(1, 0, 2)
    each = width // devices
    small = jnp.concatenate(
        [
            up_bias_grad.reshape(devices, -1),
            down_bias_grad.reshape(devices, -1),
            gains.reshape(devices, -1),
            shifts.reshape(devices, -1),
        ],
        axis=1,
    )
    used = small.shape[1]
    small = jnp.pad(small, ((0, 0), (0, 16 * TILE - used))).reshape(devices * 8, 2 * TILE)
    arrays = [
        wgrad(flat, proj_low[:, :width]),
        (dot(flat, proj_low[:, width:], 0, 0) + dot(halo, halo_low, 0, 0)).astype(bf16),
        wgrad(flat, table_low),
    ]
    plan = Plan(route, [a.shape for a in arrays], 2)
    few = Plan(route, [small.shape], 2, TILE, f32)
    sums, small, returned = scatter_sums(plan, few, size, arrays, small, handed)
    back = back.reshape(streams, local, width)
    behind = (jnp.arange(1, hops + 1, dtype=jnp.int32) + z < size)[:, None, None]
    passing = jnp.sum(jnp.where(behind, returned.astype(f32), 0.0), axis=0)
    back = jnp.concatenate([back[:1] + passing[None], back[1:]], axis=0).reshape(tokens, width)
    inputs_grad = one_grad + back.astype(bf16).astype(f32)
    q_grad, kv_grad, bucket_grad = plan.blocks(sums)
    small = small.reshape(-1)
    wide_each = up_bias_grad.shape[0] // devices
    cuts = [wide_each, wide_each + each, wide_each + 4 * each, used]
    up_bias_grad, down_bias_grad, gains, shifts, _ = jnp.split(small, cuts)
    return (
        result.astype(bf16).reshape(inputs.shape),
        inputs_grad.astype(bf16).reshape(inputs.shape),
        encoded_grad.astype(bf16).reshape(encoded.shape),
        jnp.concatenate([q_grad, kv_grad], axis=1),
        bucket_grad,
        self_out_grad,
        cross_query_grad,
        cross_kv_grad,
        cross_out_grad,
        up_grad,
        up_bias_grad,
        down_grad,
        down_bias_grad,
        gains.reshape(3, each),
        shifts.reshape(3, each),
    )


def solution(mesh):
    placed = (
        P("dp", None, "seq", None),
        P("dp", "seq", None),
        P("dp", None),
        P("dp", None),
        P(),
        P(),
        P(),
        P(),
        P(),
        P(),
        P(),
        P(),
        P(),
        P(),
        P(),
        P(),
        P("dp", None, "seq", None),
    )
    return jax.shard_map(
        shards,
        mesh=mesh,
        in_specs=placed,
        out_specs=(
            P("dp", None, "seq", None),
            P("dp", None, "seq", None),
            P("dp", "seq", None),
            P(("dp", "seq"), None),
            P(("dp", "seq"), None),
            P(("dp", "seq"), None),
            P(("dp", "seq"), None),
            P(("dp", "seq"), None),
            P(("dp", "seq"), None),
            P(("dp", "seq"), None),
            P(("dp", "seq")),
            P(("dp", "seq"), None),
            P(("dp", "seq")),
            P(None, ("dp", "seq")),
            P(None, ("dp", "seq")),
        ),
        check_vma=False,
    )
```

time: 926 us -> 584 us (0.63)
  waiting for transfers between devices: 209 us -> 10.7 us
  starting transfers between devices: 169 us -> 14.3 us
  Pallas kernels: 224 us -> 350 us
  local copies, waits for them, and re-layouts: 102 us -> 26.5 us
  other arithmetic: 40.8 us -> 22.4 us
  matrix products: 168 us -> 154 us
    ppermute x60 -> x0, waiting for transfers between devices: 199 us -> none  [the longest x55 188 us: swap(): return lax.ppermute(x, axis, flip_pairs(size, k))]
    ppermute x60 -> x0, starting transfers between devices: 154 us -> none  [the longest x3 86.3 us: shards(): lax.ppermute(part, 'seq', [(i, (i - k) % size) for i in range(size)])]
    pallas_call x4 -> x5, Pallas kernels: 198 us -> 324 us  [the longest x1 99.5 us: cross_backward(): pl.pallas_call(functools.partial(cross_bwd_kernel, local // TILE, plan),...]
    dynamic_slice x46 -> x0, local copies, waits for them, and re-layouts: 33.6 us -> none  [the longest x16 29.8 us: pick_columns(): x = lax.dynamic_index_in_dim(x, index, at + 1, keepdims=False)]
    reshape x6 -> x4, local copies, waits for them, and re-layouts: 26.1 us -> 0.6 us  [the longest x1 0.35 us: blocks(): block.reshape(-1, sub, span // sub).transpose(1, 0, 2)]
    dot_general x36 -> x10, matrix products: 70.3 us -> 54.1 us  [dot(): lax.dot_general(a, b, (((ca,), (cb,)), ((), ())), preferred_element_type=...]
    convert_element_type x35 -> x3, other arithmetic: 15.5 us -> 0.47 us  [the longest x2 0.37 us: shards(): jnp.where((names < 8) & (of[:, None] != names), NEG, 0.0).astype(bf16)]
    unnamed x257 -> x130, local copies, waits for them, and re-layouts: 17.9 us -> 8.55 us
  transfers between devices with their start and end apart: 65 -> 5, of which waited for: 38 -> 2; matrix products, arithmetic and copies ran while one was open for 19% -> 4% of each run, Pallas kernels for 4% -> 6%
where the time goes in v2:
time: 584 us; the launch traced here: 579 us
  Pallas kernels  350 us (60%)
  matrix products  154 us (26%)
  local copies, waits for them, and re-layouts  26.5 us (5%)
  other arithmetic  22.4 us (4%)
  starting transfers between devices  14.3 us (2%)
  waiting for transfers between devices  10.7 us (2%)
    pallas_call x1, Pallas kernels, cross_backward(): pl.pallas_call(functools.partial(cross_bwd_kernel, local // TILE, plan),...  99.5 us
    pallas_call x1, Pallas kernels, self_backward(): pl.pallas_call(functools.partial(self_bwd_kernel, local // TILE, plan), g...  90.3 us
    dot_general x9, matrix products, mm_t(): lax.dot_general(left, right, (((1,), (1,)), ((), ())), preferred_element_...  62 us
    pallas_call x1, Pallas kernels, scatter_sums(): pl.pallas_call(functools.partial(scatter_kernel, plan, few, size), grid=(...  58.9 us
    dot_general x10, matrix products, dot(): lax.dot_general(a, b, (((ca,), (cb,)), ((), ())), preferred_element_type=...  54.1 us
    pallas_call x1, Pallas kernels, cross_forward(): pl.pallas_call(functools.partial(cross_fwd_kernel, local // TILE), grid_s...  40.4 us
    dot_general x8, matrix products, mm(): return jnp.dot(left, right, preferred_element_type=f32)  37.7 us
    pallas_call x1, Pallas kernels, self_forward(): pl.pallas_call(functools.partial(self_fwd_kernel, local // TILE), grid_sp...  35 us
  transfers between devices with their start and end apart: 5, of which 2 were waited for; matrix products, arithmetic and copies ran while one was open for 4% of the time, Pallas kernels for 6%

profile of v2, /device:TPU:0, one launch (start us, length us, event | category | flops | bytes accessed | tf_op | source)
XLA Modules:
  0.0 579.1 jit_solution(11407237410911228577)
XLA Ops:
  1.9 5.0 collective-permute-start
  11.2 2.2 convert_reduce_fusion
  14.1 7.7 %convolution_convert_fusion.3.q_ref.ko_ref.vo_ref = bf16[768,3072]{1,0:T(8,128)(2,1)S(1)} fusion(bf16[768,1024]{1,0:T(8,128)(2,1)} %bitcast.121, bf16[1024,3072]{1,0:T(8,128)(2,1)} %param.21), kind=kOutput, calls=%fused_computation.8 | convolution fusion | flops 4834197504 | bytes 12582912 | tf_op jit(solution)/shard_map/dot_general | solution.py:961
  24.0 3.8 collective-permute-start.1
  28.8 9.8 %collective-permute-done.1 = bf16[256,1024]{1,0:T(8,128)(2,1)S(1)} collective-permute-done((bf16[256,1024]{1,0:T(8,128)(2,1)S(1)}, bf16[256,1024]{1,0:T(8,128)(2,1)S(1)}, u32[]{:S(2)}, u32[]{:S(2)}) %collective-permute-start.1) | collective-permute-done | bytes 524320 | tf_op jit(solution)/shard_map/ppermute | solution.py:974
  38.7 3.3 collective-permute-start.4
  42.7 1.6 collective-permute-start.2
  44.3 2.3 fusion.16.kh_ref.vh_ref
  46.6 35.0 %self_forward.1 = (bf16[768,1024]{1,0:T(8,128)(2,1)S(1)}, bf16[4,4,768,640]{3,2,1,0:T(8,128)(2,1)}) custom-call(s32[2]{0:T(128)S(1)} %fusion.71.need_ref, bf16[768,3072]{1,0:T(8,128)(2,1)S(1)} %convolution_convert_fusion.3.q_ref.ko_ref.vo_ref, bf16[768,3072]{1,0:T(8,128)(2,1)S(1)} %convolution_convert_fusion.3.q_ref.ko_ref.vo_ref, ...), custom_call_target="tpu_custom_call" | custom-call | flops 15000000512 | bytes 20000000 | tf_op jit(solution)/shard_map/self_forward/pallas_call | solution.py:201
  81.6 1.9 fusion.99
  84.0 1.9 convolution_convert_fusion.13.q_ref
  86.8 8.0 %convolution_convert_fusion.5.k_ref.v_ref = bf16[1024,2048]{1,0:T(8,128)(2,1)} fusion(bf16[1024,2048]{1,0:T(8,128)(2,1)S(1)} %copy-done.41, bf16[256,1024]{1,0:T(8,128)(2,1)S(1)} %collective-permute-done.4, bf16[256,1024]{1,0:T(8,128)(2,1)S(1)} %collective-permute-done.3, bf16[256,1024]{1,0:T(8,128)(2,1)S(1)} %collective-permute-done.2, ...), kind=kOutput, calls=%fused_computation.10 | convolution fusion | flops 4305453056 | bytes 10485760 | tf_op jit(solution)/shard_map/dot_general | solution.py:961
  94.9 40.4 %cross_forward.1 = (bf16[768,1024]{1,0:T(8,128)(2,1)S(1)}, bf16[4,4,768,1024]{3,2,1,0:T(8,128)(2,1)}) custom-call(s32[2]{0:T(128)S(1)} %get-tuple-element.72.lo_ref, s32[2]{0:T(128)S(1)} %get-tuple-element.71.count_ref, bf16[768,1024]{1,0:T(8,128)(2,1)S(1)} %convolution_convert_fusion.13.q_ref, bf16[1024,2048]{1,0:T(8,128)(2,1)} %convolution_convert_fusion.5.k_ref.v_ref, ...), custom_call_target="tpu_custom_call" | custom-call | flops 15000000512 | bytes 20000000 | tf_op jit(solution)/shard_map/cross_forward/pallas_call | solution.py:480
  135.3 2.1 fusion.100
  138.6 25.4 %up_gelu.1 = (bf16[768,4096]{1,0:T(8,128)(2,1)S(1)}, bf16[768,4096]{1,0:T(8,128)(2,1)S(1)}) custom-call(bf16[768,1024]{1,0:T(8,128)(2,1)S(1)} %fusion.21.x_ref, bf16[1024,4096]{1,0:T(8,128)(2,1)} %w_ref.1, f32[1,4096]{1,0:T(1,128)S(1)} %bitcast.110), custom_call_target="tpu_custom_call" | custom-call | flops 19327352832 | bytes 22000000 | tf_op jit(solution)/shard_map/up_gelu/pallas_call | solution.py:891
  164.1 12.8 %fusion.101 = (f32[768]{0:T(1024)S(1)}, f32[768,1024]{1,0:T(8,128)S(1)}) fusion(f32[1024]{0:T(1024)S(1)} %copy-done.55, bf16[768,4096]{1,0:T(8,128)(2,1)S(1)} %get-tuple-element.38, bf16[4096,1024]{1,0:T(8,128)(2,1)} %param.29, f32[1024]{0:T(1024)S(1)} %bitcast.142, f32[1024]{0:T(1024)S(1)} %bitcast.131, f32[768]{0:T(1024)S(1)} %add_rsqrt_fusion.1, ...), kind=kOutput, calls=%fused_computation.228 | convolution fusion | flops 6447954944 | bytes 20993024 | tf_op jit(solution)/shard_map/dot_general | solution.py:961
  178.3 1.7 fusion.14
  179.9 4.1 fusion.92
  184.0 14.0 %fusion = (f32[4096]{0:T(1024)}, bf16[768,4096]{1,0:T(8,128)(2,1)}) fusion(bf16[768,4096]{1,0:T(8,128)(2,1)} %copy-done.3, bf16[4096,1024]{1,0:T(8,128)(2,1)} %param.29, f32[768,1024]{1,0:T(8,128)} %get-tuple-element.70), kind=kOutput, calls=%fused_computation.1 | convolution fusion | flops 6458961920 | bytes 24133632 | tf_op jit(solution)/shard_map/dot_general | solution.py:964
  198.0 16.9 %multiply_reduce_fusion = (f32[1024]{0:T(1024)}, f32[768]{0:T(1024)S(1)}, f32[768]{0:T(1024)S(1)}, f32[1024]{0:T(1024)}, f32[768,1024]{1,0:T(8,128)}) fusion(f32[768,1024]{1,0:T(8,128)} %copy-done.11, f32[768]{0:T(1024)S(1)} %add_rsqrt_fusion.1, f32[768]{0:T(1024)S(1)} %broadcast_multiply_fusion.7, f32[1024]{0:T(1024)S(1)} %bitcast.132, ...), kind=kOutput, calls=%fused_computation.30 | convolution fusion | flops 6464466944 | bytes 30433280 | tf_op jit(solution)/shard_map/dot_general | solution.py:964
  214.9 13.9 %convolution_convert_fusion.1 = bf16[1024,4096]{1,0:T(8,128)(2,1)} fusion(bf16[768,1024]{1,0:T(8,128)(2,1)S(1)} %fusion.21.x_ref, bf16[768,4096]{1,0:T(8,128)(2,1)} %copy-done.3, bf16[768,4096]{1,0:T(8,128)(2,1)} %get-tuple-element.106), kind=kOutput, calls=%fused_computation.6 | convolution fusion | flops 6459228160 | bytes 22544384 | tf_op jit(solution)/shard_map/dot_general | solution.py:39
  228.8 12.0 %convolution_convert_fusion = bf16[4096,1024]{1,0:T(8,128)(2,1)} fusion(bf16[768,4096]{1,0:T(8,128)(2,1)} %copy-done.10, f32[768,1024]{1,0:T(8,128)S(1)} %copy-done.18), kind=kOutput, calls=%fused_computation.5 | convolution fusion | flops 6447431680 | bytes 17825792 | tf_op jit(solution)/shard_map/dot_general | solution.py:39
  240.9 1.5 subtract_multiply_fusion.1
  242.4 3.0 convolution_convert_fusion.12.up_ref
  245.4 3.2 convolution_convert_fusion.9
  248.7 99.5 %cross_backward.1 = (bf16[768,1024]{1,0:T(8,128)(2,1)}, bf16[1024,2048]{1,0:T(8,128)(2,1)}, f32[32,8192]{1,0:T(8,128)}) custom-call(bf16[768,1024]{1,0:T(8,128)(2,1)} %copy-done.9, bf16[1024,2048]{1,0:T(8,128)(2,1)} %convolution_convert_fusion.5.k_ref.v_ref, bf16[1024,2048]{1,0:T(8,128)(2,1)} %convolution_convert_fusion.5.k_ref.v_ref, ...), custom_call_target="tpu_custom_call" | custom-call | flops 40000000000 | bytes 30000000 | tf_op jit(solution)/shard_map/cross_backward/pallas_call | solution.py:576
  348.2 5.0 multiply_reduce_fusion.1
  353.2 3.5 convolution_convert_fusion.8
  358.3 3.0 convolution_convert_fusion.10.up_ref
  361.3 3.2 convolution_convert_fusion.7
  365.5 4.5 fusion.103
  370.1 2.0 copy-done.21
  372.1 1.4 slice.145
  374.2 6.4 %convolution_convert_fusion.4 = bf16[1024,2048]{1,0:T(8,128)(2,1)} fusion(bf16[1024,2048]{1,0:T(8,128)(2,1)S(1)} %copy-done.59, bf16[256,1024]{1,0:T(8,128)(2,1)S(1)} %copy-done.50, bf16[256,1024]{1,0:T(8,128)(2,1)S(1)} %copy-done.52, bf16[256,1024]{1,0:T(8,128)(2,1)S(1)} %copy-done.54, bf16[256,1024]{1,0:T(8,128)(2,1)S(1)} %bitcast.161), kind=kOutput, calls=%fused_computation.9 | convolution fusion | flops 4305453056 | bytes 10485760 | tf_op jit(solution)/shard_map/dot_general | solution.py:39
  380.5 90.3 %self_backward.1 = (bf16[768,3072]{1,0:T(8,128)(2,1)}, bf16[512,2048]{1,0:T(8,128)(2,1)}, bf16[768,512]{1,0:T(8,128)(2,1)}, f32[32,5120]{1,0:T(8,128)}, bf16[3,256,1024]{2,1,0:T(8,128)(2,1)}) custom-call(bf16[768,3072]{1,0:T(8,128)(2,1)} %copy-done.7, bf16[768,3072]{1,0:T(8,128)(2,1)} %copy-done.7, bf16[768,3072]{1,0:T(8,128)(2,1)} %copy-done.7, ...), custom_call_target="tpu_custom_call" | custom-call | flops 40000000000 | bytes 30000000 | tf_op jit(solution)/shard_map/self_backward/pallas_call | solution.py:370
  470.9 10.1 %fusion.104 = f32[768,1024]{1,0:T(8,128)} fusion(bf16[768,3072]{1,0:T(8,128)(2,1)} %get-tuple-element.44, bf16[1024,3072]{1,0:T(8,128)(2,1)} %param.21), kind=kOutput, calls=%fused_computation.231 | convolution fusion | flops 4831838208 | bytes 14155776 | tf_op jit(solution)/shard_map/dot_general | solution.py:964
  481.0 3.2 convolution_convert_fusion.6
  484.2 2.4 fusion.105
  486.7 2.4 fusion.31
  489.0 5.4 fusion.2
  495.5 1.3 copy.36
  499.6 58.9 %weight_sums.1 = (f32[32,3584]{1,0:T(8,128)}, f32[8,256]{1,0:T(8,128)}, bf16[2,256,1024]{2,1,0:T(8,128)(2,1)}) custom-call(bf16[2,2,2,2,2,32,1024]{6,5,4,3,2,1,0:T(8,128)(2,1)} %bitcast.169, bf16[2,2,2,2,2,32,2048]{6,5,4,3,2,1,0:T(8,128)(2,1)} %bitcast.166, bf16[2,2,2,2,2,32,512]{6,5,4,3,2,1,0:T(8,128)(2,1)} %bitcast.117, ...), custom_call_target="tpu_custom_call" | custom-call | flops 20000000000 | bytes 60000000 | tf_op jit(solution)/shard_map/weight_sums/pallas_call | solution.py:848
  558.5 1.8 concatenate.44
  560.3 1.5 slice.109
  565.8 3.0 convolution_add_fusion
  569.7 1.6 copy-done.17
  571.2 1.9 fusion.7
  573.4 2.3 fusion.44
  (217 shorter events, 29.2 us)
Async XLA Ops:
  0.6 83.4 %copy-start = (bf16[1024,1024]{1,0:T(8,128)(2,1)S(1)}, bf16[1024,1024]{1,0:T(8,128)(2,1)}, u32[]{:S(2)}) copy-start(bf16[1024,1024]{1,0:T(8,128)(2,1)} %param.24) | copy-start | bytes 6291460
  1.9 22.1 %collective-permute-start = (bf16[256,1024]{1,0:T(8,128)(2,1)S(1)}, bf16[256,1024]{1,0:T(8,128)(2,1)S(1)}, u32[]{:S(2)}, u32[]{:S(2)}) collective-permute-start(bf16[256,1024]{1,0:T(8,128)(2,1)S(1)} %slice_bitcast_fusion), channel_id=1, source_target_pairs={{0,1},{1,2},{2,3},{4,5},{5,6},{6,7},{8,9},{9,10},{10,11},{12,13},{... | collective-permute-start | bytes 1572872 | tf_op jit(solution)/shard_map/ppermute | solution.py:974
  14.1 13.6 %copy-start.27 = (bf16[1024,512]{1,0:T(8,128)(2,1)S(1)}, bf16[1024,512]{1,0:T(8,128)(2,1)}, u32[]{:S(2)}) copy-start(bf16[1024,512]{1,0:T(8,128)(2,1)} %param.22) | copy-start | bytes 3145732
  14.1 13.6 %copy-start.32 = (bf16[1,3,256,1024]{3,2,1,0:T(8,128)(2,1)S(1)}, bf16[1,3,256,1024]{3,2,1,0:T(8,128)(2,1)}, u32[]{:S(2)}) copy-start(bf16[1,3,256,1024]{3,2,1,0:T(8,128)(2,1)} %param.17) | copy-start | bytes 4718596
  21.9 24.7 %copy-start.7 = (bf16[768,3072]{1,0:T(8,128)(2,1)}, bf16[768,3072]{1,0:T(8,128)(2,1)S(1)}, u32[]{:S(2)}) copy-start(bf16[768,3072]{1,0:T(8,128)(2,1)S(1)} %convolution_convert_fusion.3.q_ref.ko_ref.vo_ref) | copy-start | bytes 14155780
  22.2 22.0 %slice-start = ((s8[6291456]{0:T(1024)(128)(4,1)}), s8[4194304]{0:T(1024)(128)(4,1)S(1)}, s32[]{:S(2)}) async-start(s8[6291456]{0:T(1024)(128)(4,1)} %bitcast.153), calls=%async_computation | async-start | bytes 8388608
  24.0 14.6 %collective-permute-start.1 = (bf16[256,1024]{1,0:T(8,128)(2,1)S(1)}, bf16[256,1024]{1,0:T(8,128)(2,1)S(1)}, u32[]{:S(2)}, u32[]{:S(2)}) collective-permute-start(bf16[256,1024]{1,0:T(8,128)(2,1)S(1)} %collective-permute-done), channel_id=1, source_target_pairs={{0,1},{1,2},{2,3},{4,5},{5,6},{6,7},{8,9},{9,10},{10,11},{12,13},{... | collective-permute-start | bytes 1572872 | tf_op jit(solution)/shard_map/ppermute | solution.py:974
  27.8 10.9 %copy-start.47 = (bf16[1,256,1024]{2,1,0:T(8,128)(2,1)S(1)}, bf16[1,256,1024]{2,1,0:T(8,128)(2,1)}, u32[]{:S(2)}) copy-start(bf16[1,256,1024]{2,1,0:T(8,128)(2,1)} %param.18) | copy-start | bytes 1572868
  27.8 16.5 %slice-start.1 = ((s8[6291456]{0:T(1024)(128)(4,1)}), s8[2097152]{0:T(1024)(128)(4,1)S(1)}, s32[]{:S(2)}) async-start(s8[6291456]{0:T(1024)(128)(4,1)} %bitcast.153), calls=%async_computation.1 | async-start | bytes 4194304
  38.6 5.6 copy-start.24
  38.7 47.3 %collective-permute-start.4 = (bf16[256,1024]{1,0:T(8,128)(2,1)S(1)}, bf16[256,1024]{1,0:T(8,128)(2,1)S(1)}, u32[]{:S(2)}, u32[]{:S(2)}) collective-permute-start(bf16[256,1024]{1,0:T(8,128)(2,1)S(1)} %bitcast.157), channel_id=1, source_target_pairs={{0,3},{1,0},{2,1},{3,2},{4,7},{5,4},{6,5},{7,6},{8,11},{9,8},{10,9... | collective-permute-start | bytes 1572872 | tf_op jit(solution)/shard_map/ppermute | solution.py:980
  41.9 44.9 %collective-permute-start.3 = (bf16[256,1024]{1,0:T(8,128)(2,1)S(1)}, bf16[256,1024]{1,0:T(8,128)(2,1)S(1)}, u32[]{:S(2)}, u32[]{:S(2)}) collective-permute-start(bf16[256,1024]{1,0:T(8,128)(2,1)S(1)} %bitcast.158), channel_id=1, source_target_pairs={{0,2},{1,3},{2,0},{3,1},{4,6},{5,7},{6,4},{7,5},{8,10},{9,11},{10,... | collective-permute-start | bytes 1572872 | tf_op jit(solution)/shard_map/ppermute | solution.py:980
  42.7 44.2 %collective-permute-start.2 = (bf16[256,1024]{1,0:T(8,128)(2,1)S(1)}, bf16[256,1024]{1,0:T(8,128)(2,1)S(1)}, u32[]{:S(2)}, u32[]{:S(2)}) collective-permute-start(bf16[256,1024]{1,0:T(8,128)(2,1)S(1)} %bitcast.159), channel_id=1, source_target_pairs={{0,1},{1,2},{2,3},{3,0},{4,5},{5,6},{6,7},{7,4},{8,9},{9,10},{10,1... | collective-permute-start | bytes 1572872 | tf_op jit(solution)/shard_map/ppermute | solution.py:980
  46.6 35.0 %copy-start.6 = (bf16[512,2048]{1,0:T(8,128)(2,1)}, bf16[512,2048]{1,0:T(8,128)(2,1)S(1)}, u32[]{:S(2)}) copy-start(bf16[512,2048]{1,0:T(8,128)(2,1)S(1)} %fusion.16.kh_ref.vh_ref) | copy-start | bytes 6291460
  46.6 35.0 %copy-start.45 = (bf16[1024,1024]{1,0:T(8,128)(2,1)S(1)}, bf16[1024,1024]{1,0:T(8,128)(2,1)}, u32[]{:S(2)}) copy-start(bf16[1024,1024]{1,0:T(8,128)(2,1)} %param.23) | copy-start | bytes 6291460
  83.5 51.8 %copy-start.14 = (f32[768,1024]{1,0:T(8,128)}, f32[768,1024]{1,0:T(8,128)S(1)}, u32[]{:S(2)}) copy-start(f32[768,1024]{1,0:T(8,128)S(1)} %get-tuple-element.98) | copy-start | bytes 9437188
  85.9 9.0 %copy-start.9 = (bf16[768,1024]{1,0:T(8,128)(2,1)}, bf16[768,1024]{1,0:T(8,128)(2,1)S(1)}, u32[]{:S(2)}) copy-start(bf16[768,1024]{1,0:T(8,128)(2,1)S(1)} %convolution_convert_fusion.13.q_ref) | copy-start | bytes 4718596
  85.9 8.9 %copy-start.49 = (bf16[256,1024]{1,0:T(8,128)(2,1)}, bf16[256,1024]{1,0:T(8,128)(2,1)S(1)}, u32[]{:S(2)}) copy-start(bf16[256,1024]{1,0:T(8,128)(2,1)S(1)} %collective-permute-done.4) | copy-start | bytes 1572868
  86.8 8.0 %copy-start.51 = (bf16[256,1024]{1,0:T(8,128)(2,1)}, bf16[256,1024]{1,0:T(8,128)(2,1)S(1)}, u32[]{:S(2)}) copy-start(bf16[256,1024]{1,0:T(8,128)(2,1)S(1)} %collective-permute-done.3) | copy-start | bytes 1572868
  86.8 8.0 %copy-start.53 = (bf16[256,1024]{1,0:T(8,128)(2,1)}, bf16[256,1024]{1,0:T(8,128)(2,1)S(1)}, u32[]{:S(2)}) copy-start(bf16[256,1024]{1,0:T(8,128)(2,1)S(1)} %collective-permute-done.2) | copy-start | bytes 1572868
  94.9 40.4 %copy-start.43 = (bf16[1024,1024]{1,0:T(8,128)(2,1)S(1)}, bf16[1024,1024]{1,0:T(8,128)(2,1)}, u32[]{:S(2)}) copy-start(bf16[1024,1024]{1,0:T(8,128)(2,1)} %param.26) | copy-start | bytes 6291460
  135.3 110.1 %copy-start.8 = (bf16[768,1024]{1,0:T(8,128)(2,1)}, bf16[768,1024]{1,0:T(8,128)(2,1)S(1)}, u32[]{:S(2)}) copy-start(bf16[768,1024]{1,0:T(8,128)(2,1)S(1)} %get-tuple-element.37.mix_ref) | copy-start | bytes 4718596
  137.4 26.7 %copy-start.11 = (f32[768,1024]{1,0:T(8,128)}, f32[768,1024]{1,0:T(8,128)S(1)}, u32[]{:S(2)}) copy-start(f32[768,1024]{1,0:T(8,128)S(1)} %get-tuple-element.100) | copy-start | bytes 9437188
  138.6 25.4 %copy-start.55 = (f32[1024]{0:T(1024)S(1)}, f32[1024]{0:T(1024)}, u32[]{:S(2)}) copy-start(f32[1024]{0:T(1024)} %param.30) | copy-start | bytes 12292
  164.0 12.8 %copy-start.3 = (bf16[768,4096]{1,0:T(8,128)(2,1)}, bf16[768,4096]{1,0:T(8,128)(2,1)S(1)}, u32[]{:S(2)}) copy-start(bf16[768,4096]{1,0:T(8,128)(2,1)S(1)} %get-tuple-element.39) | copy-start | bytes 18874372
  164.0 12.8 %copy-start.10 = (bf16[768,4096]{1,0:T(8,128)(2,1)}, bf16[768,4096]{1,0:T(8,128)(2,1)S(1)}, u32[]{:S(2)}) copy-start(bf16[768,4096]{1,0:T(8,128)(2,1)S(1)} %get-tuple-element.38) | copy-start | bytes 18874372
  214.9 13.9 %copy-start.18 = (f32[768,1024]{1,0:T(8,128)S(1)}, f32[768,1024]{1,0:T(8,128)}, u32[]{:S(2)}) copy-start(f32[768,1024]{1,0:T(8,128)} %get-tuple-element.70) | copy-start | bytes 9437188
  228.8 12.0 %copy-start.12 = (f32[768,1024]{1,0:T(8,128)S(1)}, f32[768,1024]{1,0:T(8,128)}, u32[]{:S(2)}) copy-start(f32[768,1024]{1,0:T(8,128)} %copy-done.11) | copy-start | bytes 9437188
  228.8 12.0 %copy-start.20 = (f32[768,1024]{1,0:T(8,128)S(1)}, f32[768,1024]{1,0:T(8,128)}, u32[]{:S(2)}) copy-start(f32[768,1024]{1,0:T(8,128)} %get-tuple-element.103) | copy-start | bytes 9437188
  242.4 3.0 copy-start.19
  248.6 99.5 %copy-start.15 = (f32[768,1024]{1,0:T(8,128)S(1)}, f32[768,1024]{1,0:T(8,128)}, u32[]{:S(2)}) copy-start(f32[768,1024]{1,0:T(8,128)} %copy-done.14) | copy-start | bytes 9437188
  348.2 5.1 copy-start.57
  361.3 3.2 copy-start.42
  361.3 4.2 copy-start.59
  470.9 10.1 %copy-start.33 = (bf16[1,3,256,1024]{3,2,1,0:T(8,128)(2,1)S(1)}, bf16[1,3,256,1024]{3,2,1,0:T(8,128)(2,1)}, u32[]{:S(2)}) copy-start(bf16[1,3,256,1024]{3,2,1,0:T(8,128)(2,1)} %param.17) | copy-start | bytes 4718596
  470.9 10.1 %copy-start.58 = (bf16[768,3072]{1,0:T(8,128)(2,1)S(1)}, bf16[768,3072]{1,0:T(8,128)(2,1)}, u32[]{:S(2)}) copy-start(bf16[768,3072]{1,0:T(8,128)(2,1)} %get-tuple-element.44) | copy-start | bytes 14155780
  481.0 3.2 copy-start.25
  481.0 3.2 copy-start.56
  481.0 5.6 slice-start.2
  489.0 5.4 copy-start.29
  494.4 3.2 copy-start.35
  494.5 3.2 copy-start.36
  499.6 62.2 %copy-start.31 = (f32[32,5120]{1,0:T(8,128)S(1)}, f32[32,5120]{1,0:T(8,128)}, u32[]{:S(2)}) copy-start(f32[32,5120]{1,0:T(8,128)} %get-tuple-element.50) | copy-start | bytes 1966084
  499.6 66.1 %copy-start.28 = (bf16[1024,512]{1,0:T(8,128)(2,1)S(1)}, bf16[1024,512]{1,0:T(8,128)(2,1)}, u32[]{:S(2)}) copy-start(bf16[1024,512]{1,0:T(8,128)(2,1)} %param.22) | copy-start | bytes 3145732
  499.6 66.1 %copy-start.30 = (bf16[768,512]{1,0:T(8,128)(2,1)S(1)}, bf16[768,512]{1,0:T(8,128)(2,1)}, u32[]{:S(2)}) copy-start(bf16[768,512]{1,0:T(8,128)(2,1)} %get-tuple-element.45) | copy-start | bytes 2359300
  565.8 3.2 copy-start.23
  565.8 3.2 copy-start.40
  573.1 5.5 copy-start.1
  (21 other events, 44.3 us)

commit v3 on v2

--- a/solution.py
+++ b/solution.py
@@ -48,6 +48,11 @@
     skews = [(bucket_of(gap) + BUCKETS * h == row).astype(jnp.bfloat16) for h in range(4)]
     hots = [(bucket_of(back) + BUCKETS * h == lane).astype(jnp.bfloat16) for h in range(4)]
     return jnp.concatenate(skews, axis=0), jnp.concatenate(hots, axis=0)
+
+
+def halves(a, b, ca, cb):
+    half = a.shape[0] // 2
+    return jnp.concatenate([dot(a[:half], b, ca, cb), dot(a[half:], b, ca, cb)], axis=0)
 
 
 def head_masks():
@@ -87,8 +92,8 @@
     return pltpu.roll(x, 0, 1, stride=1, stride_axis=0)
 
 
-WINDOWS = ((-TILE, PAIR, 0), (-3 * TILE, PAIR, PAIR), (-4 * TILE, TILE, 2 * PAIR))
-REACH = 5 * TILE
+REACH = HALO + TILE
+FIRST = (3 * TILE, TILE, 0)
 
 
 def columns(rows, base):
@@ -128,27 +133,24 @@
             table.append(jnp.concatenate([high, (rel - high.astype(jnp.float32)).astype(jnp.bfloat16)], axis=1))
         table = jnp.concatenate(table, axis=0)
         for j in range(2):
-            bz[j, :, :] = dot(table, skew_ref[pl.ds(pl.multiple_of((2 * p + j) * PAIR, PAIR), PAIR), :], 1, 0)
+            bz[j, :, :] = halves(table, skew_ref[pl.ds(pl.multiple_of((2 * p + j) * PAIR, PAIR), PAIR), :], 1, 0)
 
         def path(count):
-            windows = []
-            for off, width, at in WINDOWS[:count]:
-                keys = pl.ds(pl.multiple_of(here + HALO + off, TILE), width)
-                sc[:, at : at + width] = dot(qs, kx[p, keys, :], 1, 1)
-                windows.append((at, width, keys))
-            reach = windows[-1][0] + windows[-1][1]
+            first = FIRST[count - 1]
+            keys = pl.ds(pl.multiple_of(here + first, TILE), REACH - first)
+            sc[:, first:] = halves(qs, kx[p, keys, :], 1, 1)
             for b in range(2 * STREAMS):
                 s, j = b // 2, b % 2
                 rows = stream_rows(s, local, here)
                 near = roll_rows(bz[j, part(s), :TILE])
                 steady = bz[j, part(s), TILE:]
-                left = sc[part(b), part(0)] + jnp.where(lane > row, near, steady)
-                right = sc[part(b), part(1)]
+                left = sc[part(b), part(3)] + jnp.where(lane > row, near, steady)
+                right = sc[part(b), part(4)]
                 if s > 0:
                     own = lane_sum(qs[part(b), :TILE].astype(jnp.float32) * ko_ref[rows, lanes].astype(jnp.float32))
                     right = jnp.where(lane == row, own, right)
                 right = right + jnp.where(lane <= row, near, NEG)
-                far = [sc[part(b), part(m)] for m in range(2, reach // TILE)]
+                far = [sc[part(b), part(m)] for m in range(first // TILE, 3)]
                 top = jnp.maximum(left, right)
                 if far:
                     most = far[0]
@@ -157,22 +159,19 @@
                     top = jnp.maximum(top, most + steady)
                 top = lane_max(top)
                 base = top - steady
-                weights = [jnp.exp(left - top), jnp.exp(right - top)] + [jnp.exp(x - base) for x in far]
+                weights = [jnp.exp(x - base) for x in far] + [jnp.exp(left - top), jnp.exp(right - top)]
                 total = weights[0]
                 for x in weights[1:]:
                     total = total + x
                 inverse = 1.0 / lane_sum(total)
-                for m, x in enumerate(weights):
+                for m, x in enumerate(weights, first // TILE):
                     x = (x * inverse).astype(jnp.bfloat16)
                     pr_ref[0, n, part(b), part(m)] = x
-                    if m == 1 and s > 0:
+                    if m == 4 and s > 0:
                         st[part(b), :] = lane_sum(jnp.where(lane == row, x.astype(jnp.float32), 0.0))
-            if reach < REACH:
-                pr_ref[0, n, :, reach:] = jnp.zeros((ROWS, REACH - reach), jnp.bfloat16)
-            acc = None
-            for at, width, keys in windows:
-                o = dot(pr_ref[0, n, :, at : at + width], vx[keys, lanes], 1, 0)
-                acc = o if acc is None else acc + o
+            if first:
+                pr_ref[0, n, :, :first] = jnp.zeros((ROWS, first), jnp.bfloat16)
+            acc = halves(pr_ref[0, n, :, first:], vx[keys, lanes], 1, 0)
             main = vo_ref[stream_rows(0, local, here), lanes].astype(jnp.float32)
             for s in range(STREAMS):
                 rows = stream_rows(s, local, here)
@@ -221,17 +220,18 @@
     )(need, proj, proj, proj, halo_kv, halo_kv, rel, doc, aug, skew)
 
 
-def self_bwd_kernel(nq, plan, q_ref, ko_ref, vo_ref, kh_ref, vh_ref, hot_ref, mix_ref, up_ref, pr_ref, *refs):
+def self_bwd_kernel(nq, plan, shifts, q_ref, ko_ref, vo_ref, kh_ref, vh_ref, hot_ref, mix_ref, up_ref, pr_ref, *refs):
     arrays, handed, refs = refs[: plan.many], refs[plan.many], refs[plan.many + 1 :]
-    dproj_ref, dhalo_ref, drel_ref, sums_ref, got, kx, vx, dp, pz, ds, cb, st, dkt, dvt, dqa = refs[:15]
+    (dq_ref, dkv_ref, drel_ref, got), refs = refs[:4], refs[4:]
+    outs = len(plan.out_shapes())
+    results, (kx, vx, dp, ds, cb, st, dkt, dvt, cv), scratch = refs[:outs], refs[outs : outs + 9], refs[outs + 9 :]
     g = pl.program_id(0)
-    comm = Comm(plan, arrays, sums_ref, refs[15:-1])
-    hand = Handing(handed.shape[0] + 1, handed.shape[0], True, handed, got, refs[-1])
+    comm = Comm(plan, arrays, results, scratch[:-1])
+    hand = Handing(shifts, 8 * nq, handed, got, scratch[-1])
 
     @pl.when(g == 0)
     def _():
         comm.barrier()
-        hand.start()
 
     local = nq * TILE
     kx[:HALO, :] = kh_ref[...]
@@ -251,92 +251,69 @@
         i, p = n // 2, n % 2
         here = pl.multiple_of(i * TILE, TILE)
         lanes = pl.ds(pl.multiple_of(p * TILE, TILE), TILE)
+        hand.step(g * 2 * nq + n)
         comm.step(g * 2 * nq + n)
         qs = stack_heads(q_ref, local, here, lanes, masks, None, SCALE)
         ups = stack_heads(up_ref, local, here, lanes, masks)
         qt = qs.T
         upt = ups.T
 
-        def window(w):
-            off, width, at = WINDOWS[w]
-            keys = pl.ds(pl.multiple_of(here + HALO + off, TILE), width)
-            dp[:, :width] = dot(ups, vx[keys, lanes], 1, 1)
-            for b in range(2 * STREAMS):
-                s = b // 2
-                rows = stream_rows(s, local, here)
-                if w == 0:
-                    upf = ups[part(b)].astype(jnp.float32)
-                    centre = lane_sum(upf * mix_ref[rows, lanes].astype(jnp.float32))
-                    st[0, part(b), :] = centre
-                else:
-                    centre = st[0, part(b), :]
-                far = None
-                for m in range(width // TILE):
-                    x = pr_ref[0, n, part(b), slice(at + m * TILE, at + (m + 1) * TILE)]
-                    xf = x.astype(jnp.float32)
-                    y = (xf * (dp[part(b), part(m)] - centre)).astype(jnp.bfloat16)
-                    if w > 0:
-                        ds[part(b), part(m)] = y
-                        far = y.astype(jnp.float32) if far is None else far + y.astype(jnp.float32)
-                        continue
-                    yf = y.astype(jnp.float32)
-                    if m == 0:
-                        ds[part(b), part(0)] = y
-                        pz[part(b), part(0)] = x
-                        band = jnp.where(lane > row, yf, 0.0)
-                        st[3, part(b), :] = yf - band
-                        continue
-                    if s > 0:
-                        own_weight = lane_sum(jnp.where(lane == row, xf, 0.0))
-                        own_grad = own_weight * (lane_sum(upf * vo_ref[rows, lanes].astype(jnp.float32)) - centre)
-                        own_grad = own_grad.astype(jnp.bfloat16).astype(jnp.float32)
-                        st[1, part(b), :] = own_weight
-                        st[2, part(b), :] = own_grad
-                        xf = jnp.where(lane == row, 0.0, xf)
-                        yf = jnp.where(lane == row, 0.0, yf)
-                        band = band + jnp.where(lane == row, own_grad, yf)
-                        pz[part(b), part(1)] = xf.astype(jnp.bfloat16)
-                        ds[part(b), part(1)] = yf.astype(jnp.bfloat16)
-                    else:
-                        band = band + yf
-                        pz[part(b), part(1)] = x
-                        ds[part(b), part(1)] = y
-                    cb[:, part(b)] = band.astype(jnp.bfloat16)
-                if w > 0:
-                    st[3, part(b), :] += far
-            grad = ds[:, :width]
-            weights = pz[...] if w == 0 else pr_ref[0, n, :, at : at + width]
-            dkt[p, :, keys] += dot(qt, grad, 1, 0)
-            dvt[p, :, keys] += dot(upt, weights, 1, 0)
-            return dot(grad, kx[keys, lanes], 1, 0)
-
-        dqa[...] = window(0)
+        keys = pl.ds(pl.multiple_of(here, TILE), REACH)
+        dp[...] = halves(ups, vx[keys, lanes], 1, 1)
+        for b in range(2 * STREAMS):
+            s = b // 2
+            rows = stream_rows(s, local, here)
+            upf = ups[part(b)].astype(jnp.float32)
+            centre = lane_sum(upf * mix_ref[rows, lanes].astype(jnp.float32))
+            xs = [pr_ref[0, n, part(b), part(m)].astype(jnp.float32) for m in range(5)]
+            ys = [(xs[m] * (dp[part(b), part(m)] - centre)).astype(jnp.bfloat16) for m in range(5)]
+            for m in range(4):
+                ds[part(b), part(m)] = ys[m]
+            ys = [y.astype(jnp.float32) for y in ys]
+            band = jnp.where(lane > row, ys[3], 0.0)
+            st[2, part(b), :] = ys[0] + ys[1] + ys[2] + (ys[3] - band)
+            if s > 0:
+                own_weight = lane_sum(jnp.where(lane == row, xs[4], 0.0))
+                own_grad = own_weight * (lane_sum(upf * vo_ref[rows, lanes].astype(jnp.float32)) - centre)
+                own_grad = own_grad.astype(jnp.bfloat16).astype(jnp.float32)
+                st[0, part(b), :] = own_weight
+                st[1, part(b), :] = own_grad
+                band = band + jnp.where(lane == row, own_grad, ys[4])
+                ds[part(b), part(4)] = jnp.where(lane == row, 0.0, ys[4]).astype(jnp.bfloat16)
+            else:
+                band = band + ys[4]
+                ds[part(b), part(4)] = ys[4].astype(jnp.bfloat16)
+            cb[:, part(b)] = band.astype(jnp.bfloat16)
+        dkt[p, :, keys] += dot(qt, ds[...], 1, 0)
+        dvt[p, :, keys] += dot(upt, pr_ref[0, n], 1, 0)
+        dq = dot(ds[...], kx[keys, lanes], 1, 0)
         turned = dot(flip, cb[...], 1, 0)
         rolled = [roll_rows(turned[:, part(b)]).astype(jnp.bfloat16) for b in range(2 * STREAMS)]
         rolled = jnp.concatenate([jnp.concatenate(rolled[2 * s : 2 * s + 2], axis=1) for s in range(STREAMS)], axis=0)
         table = dot(rolled, hot_ref[pl.ds(pl.multiple_of(p * PAIR, PAIR), PAIR), :], 1, 0).astype(jnp.bfloat16)
         table = dot(flip, jnp.concatenate([table[part(s)] for s in range(STREAMS)], axis=1), 1, 0)
 
-        dq = dqa[...] + window(1) + window(2)
+        excess = None
         for s in range(STREAMS):
             rows = stream_rows(s, local, here)
             a, b = part(2 * s), part(2 * s + 1)
             dqs = jnp.where(lane < HEAD_DIM, dq[a], dq[b])
             col = pl.multiple_of(gl + p * TILE, TILE)
+            kept = pl.ds(pl.multiple_of(HALO + s * local + here, TILE), TILE)
             if s > 0:
-                own_weight = jnp.where(lane < HEAD_DIM, st[1, a, :], st[1, b, :])
-                own_grad = jnp.where(lane < HEAD_DIM, st[2, a, :], st[2, b, :])
+                own_weight = jnp.where(lane < HEAD_DIM, st[0, a, :], st[0, b, :])
+                own_grad = jnp.where(lane < HEAD_DIM, st[1, a, :], st[1, b, :])
                 dqs = dqs + own_grad * ko_ref[rows, lanes].astype(jnp.float32)
-                dproj_ref[rows, pl.ds(pl.multiple_of(col + third, TILE), TILE)] = (
+                own_value = own_weight * up_ref[rows, lanes].astype(jnp.float32)
+                excess = own_value if excess is None else excess + own_value
+                dkv_ref[kept, pl.ds(col, TILE)] = (
                     own_grad * (SCALE * q_ref[rows, lanes].astype(jnp.float32))
                 ).astype(jnp.bfloat16)
-                dproj_ref[rows, pl.ds(pl.multiple_of(col + 2 * third, TILE), TILE)] = (
-                    own_weight * up_ref[rows, lanes].astype(jnp.float32)
-                ).astype(jnp.bfloat16)
-            dproj_ref[rows, pl.ds(col, TILE)] = (SCALE * dqs).astype(jnp.bfloat16)
+                dkv_ref[kept, pl.ds(pl.multiple_of(col + third, TILE), TILE)] = own_value.astype(jnp.bfloat16)
+            dq_ref[rows, lanes] = (SCALE * dqs).astype(jnp.bfloat16)
             dr = table[:, part(s)]
             for j, blk in enumerate((a, b)):
-                dr = dr + jnp.where(lane == BUCKETS * (2 * p + j) + BUCKETS - 1, lane_sum(st[3, blk, :]), 0.0)
+                dr = dr + jnp.where(lane == BUCKETS * (2 * p + j) + BUCKETS - 1, lane_sum(st[2, blk, :]), 0.0)
 
             @pl.when(p == 0)
             def _():
@@ -345,52 +322,52 @@
             @pl.when(p == 1)
             def _():
                 drel_ref[rows, :] = (drel_ref[rows, :].astype(jnp.float32) + dr).astype(jnp.bfloat16)
+        cv[pl.ds(here, TILE), lanes] = excess
         return 0
 
     lax.fori_loop(0, 2 * nq, step, 0)
     for p in range(2):
         for j, acc in enumerate((dkt, dvt)):
             col = pl.multiple_of(gl + p * TILE + third * j, TILE)
-            full = acc[p, :, :].T.astype(jnp.bfloat16)
-            dhalo_ref[:, pl.ds(col, TILE)] = full[:HALO]
-            dproj_ref[:local, pl.ds(pl.multiple_of(col + third, TILE), TILE)] = full[HALO:]
+            full = acc[p, :, :].T
+            main = full[HALO:] if j == 0 else full[HALO:] - cv[:, part(p)]
+            dkv_ref[:HALO, pl.ds(col, TILE)] = full[:HALO].astype(jnp.bfloat16)
+            dkv_ref[HALO : HALO + local, pl.ds(col, TILE)] = main.astype(jnp.bfloat16)
 
     @pl.when(g == pl.num_programs(0) - 1)
     def _():
+        hand.step(4 * 2 * nq)
         comm.rest(4 * 2 * nq)
-        hand.wait()
-
-
-def self_backward(plan, arrays, handed, proj, halo_kv, hot, mix, up, weights):
+
+
+def self_backward(plan, arrays, shifts, handed, proj, halo_kv, hot, mix, up, weights):
     tokens = proj.shape[0]
     local = tokens // STREAMS
     width = proj.shape[1] // 3
     grid = width // PAIR
     steps = 2 * local // TILE
     return pl.pallas_call(
-        functools.partial(self_bwd_kernel, local // TILE, plan),
+        functools.partial(self_bwd_kernel, local // TILE, plan, shifts),
         grid=(grid,),
         in_specs=[
             columns(tokens, 0), columns(tokens, grid), columns(tokens, 2 * grid), columns(HALO, 0), columns(HALO, grid),
             whole(4 * TILE, TILE), columns(tokens, 0), columns(tokens, 0), weights_spec(steps, REACH),
         ] + plan.in_specs() + [pl.BlockSpec(memory_space=pl.ANY)],
         out_specs=[
-            whole(tokens, 3 * width), whole(HALO, 2 * width), pl.BlockSpec((tokens, TILE), lambda g, *_: (0, g)), plan.out_spec(),
+            columns(tokens, 0), whole(HALO + tokens, 2 * width), pl.BlockSpec((tokens, TILE), lambda g, *_: (0, g)),
             pl.BlockSpec(memory_space=pl.ANY),
-        ],
+        ] + plan.out_specs(),
         scratch_shapes=[
             pltpu.VMEM((HALO + local, PAIR), jnp.bfloat16), pltpu.VMEM((HALO + local, PAIR), jnp.bfloat16),
-            pltpu.VMEM((ROWS, PAIR), jnp.float32), pltpu.VMEM((ROWS, PAIR), jnp.bfloat16),
-            pltpu.VMEM((ROWS, PAIR), jnp.bfloat16), pltpu.VMEM((TILE, ROWS), jnp.bfloat16),
-            pltpu.VMEM((4, ROWS, TILE), jnp.float32),
+            pltpu.VMEM((ROWS, REACH), jnp.float32), pltpu.VMEM((ROWS, REACH), jnp.bfloat16),
+            pltpu.VMEM((TILE, ROWS), jnp.bfloat16), pltpu.VMEM((3, ROWS, TILE), jnp.float32),
             pltpu.VMEM((2, TILE, HALO + local), jnp.float32), pltpu.VMEM((2, TILE, HALO + local), jnp.float32),
-            pltpu.VMEM((ROWS, TILE), jnp.float32),
-        ] + plan.scratch() + handing_scratch(handed.shape[0]),
+            pltpu.VMEM((local, PAIR), jnp.float32),
+        ] + plan.scratch() + handing_scratch(len(shifts), 8 * local // TILE),
         out_shape=[
-            jax.ShapeDtypeStruct((tokens, 3 * width), jnp.bfloat16), jax.ShapeDtypeStruct((HALO, 2 * width), jnp.bfloat16),
-            jax.ShapeDtypeStruct((tokens, width // 2), jnp.bfloat16), plan.out_shape(),
-            jax.ShapeDtypeStruct(handed.shape, handed.dtype),
-        ],
+            jax.ShapeDtypeStruct((tokens, width), jnp.bfloat16), jax.ShapeDtypeStruct((HALO + tokens, 2 * width), jnp.bfloat16),
+            jax.ShapeDtypeStruct((tokens, width // 2), jnp.bfloat16), jax.ShapeDtypeStruct(handed.shape, handed.dtype),
+        ] + plan.out_shapes(),
         compiler_params=pltpu.CompilerParams(collective_id=plan.number, has_side_effects=True, vmem_limit_bytes=56 << 20),
         cost_estimate=pl.CostEstimate(flops=40_000_000_000, bytes_accessed=30_000_000, transcendentals=8_000_000),
         name="self_backward",
@@ -433,8 +410,8 @@
             return pl.ds(pl.multiple_of((lo_ref[i] + w) * PAIR, PAIR), PAIR)
 
         def path(count):
-            for w in range(count):
-                sc[:, w * PAIR : (w + 1) * PAIR] = dot(qs, kx[p, window(w), :], 1, 1)
+            keys = pl.ds(pl.multiple_of(lo_ref[i] * PAIR, PAIR), count * PAIR)
+            sc[:, : count * PAIR] = halves(qs, kx[p, keys, :], 1, 1)
             for b in range(2 * STREAMS):
                 xs = [sc[part(b), part(m)] for m in range(2 * count)]
                 top = xs[0]
@@ -449,10 +426,7 @@
                 xs = [(x * inverse).astype(jnp.bfloat16) for x in xs]
                 for w in range(count):
                     pr_ref[0, n, part(b), window(w)] = jnp.concatenate(xs[2 * w : 2 * w + 2], axis=1)
-            total = None
-            for w in range(count):
-                o = dot(pr_ref[0, n, :, window(w)], vx[window(w), lanes], 1, 0)
-                total = o if total is None else total + o
+            total = halves(pr_ref[0, n, :, keys], vx[keys, lanes], 1, 0)
             for s in range(STREAMS):
                 mixed = jnp.where(lane < HEAD_DIM, total[part(2 * s)], total[part(2 * s + 1)])
                 mix_ref[stream_rows(s, local, here), lanes] = mixed.astype(jnp.bfloat16)
@@ -495,10 +469,11 @@
 
 
 def cross_bwd_kernel(nq, plan, q_ref, k_ref, v_ref, mix_ref, up_ref, pr_ref, *refs):
-    arrays, refs = refs[: plan.many], refs[plan.many :]
-    dq_ref, dkv_ref, sums_ref, kx, vx, dp, ds, st, dkt, dvt, dqa = refs[:11]
+    arrays, (dq_ref, dkv_ref), refs = refs[: plan.many], refs[plan.many : plan.many + 2], refs[plan.many + 2 :]
+    outs = len(plan.out_shapes())
+    results, (kx, vx, dp, ds, st, dkt, dvt), scratch = refs[:outs], refs[outs : outs + 7], refs[outs + 7 :]
     g = pl.program_id(0)
-    comm = Comm(plan, arrays, sums_ref, refs[11:])
+    comm = Comm(plan, arrays, results, scratch)
 
     @pl.when(g == 0)
     def _():
@@ -531,23 +506,16 @@
         for b in range(2 * STREAMS):
             rows = stream_rows(b // 2, local, here)
             st[part(b), :] = lane_sum(ups[part(b)].astype(jnp.float32) * mix_ref[rows, lanes].astype(jnp.float32))
-        dqa[...] = jnp.zeros_like(dqa)
-
-        def window(w, _):
-            at = pl.ds(pl.multiple_of(w * PAIR, PAIR), PAIR)
-            dp[...] = dot(ups, vx[at, lanes], 1, 1)
-            for b in range(2 * STREAMS):
-                x = pr_ref[0, n, part(b), at].astype(jnp.float32)
-                for m in range(2):
-                    ds[part(b), part(m)] = (x[:, part(m)] * (dp[part(b), part(m)] - st[part(b), :])).astype(jnp.bfloat16)
-            dkt[p, :, at] += dot(qt, ds[...], 1, 0)
-            dvt[p, :, at] += dot(upt, pr_ref[0, n, :, at], 1, 0)
-            dqa[...] += dot(ds[...], kx[at, lanes], 1, 0)
-            return 0
-
-        lax.fori_loop(0, k_ref.shape[0] // PAIR, window, 0)
+        dp[...] = halves(ups, vx[:, lanes], 1, 1)
+        for b in range(2 * STREAMS):
+            for m in range(dp.shape[1] // TILE):
+                x = pr_ref[0, n, part(b), part(m)].astype(jnp.float32)
+                ds[part(b), part(m)] = (x * (dp[part(b), part(m)] - st[part(b), :])).astype(jnp.bfloat16)
+        dkt[p, :, :] += dot(qt, ds[...], 1, 0)
+        dvt[p, :, :] += dot(upt, pr_ref[0, n], 1, 0)
+        dqa = dot(ds[...], kx[:, lanes], 1, 0)
         for s in range(STREAMS):
-            dq = jnp.where(lane < HEAD_DIM, dqa[part(2 * s), :], dqa[part(2 * s + 1), :])
+            dq = jnp.where(lane < HEAD_DIM, dqa[part(2 * s)], dqa[part(2 * s + 1)])
             dq_ref[stream_rows(s, local, here), lanes] = (SCALE * dq).astype(jnp.bfloat16)
         return 0
 
@@ -580,18 +548,16 @@
             columns(tokens, 0), columns(full, 0), columns(full, grid),
             columns(tokens, 0), columns(tokens, 0), weights_spec(steps, full),
         ] + plan.in_specs(),
-        out_specs=[columns(tokens, 0), whole(full, 2 * width), plan.out_spec()],
+        out_specs=[columns(tokens, 0), whole(full, 2 * width)] + plan.out_specs(),
         scratch_shapes=[
             pltpu.VMEM((full, PAIR), jnp.bfloat16), pltpu.VMEM((full, PAIR), jnp.bfloat16),
-            pltpu.VMEM((ROWS, PAIR), jnp.float32), pltpu.VMEM((ROWS, PAIR), jnp.bfloat16),
+            pltpu.VMEM((ROWS, full), jnp.float32), pltpu.VMEM((ROWS, full), jnp.bfloat16),
             pltpu.VMEM((ROWS, TILE), jnp.float32),
             pltpu.VMEM((2, TILE, full), jnp.float32), pltpu.VMEM((2, TILE, full), jnp.float32),
-            pltpu.VMEM((ROWS, TILE), jnp.float32),
         ] + plan.scratch(),
         out_shape=[
             jax.ShapeDtypeStruct((tokens, width), jnp.bfloat16), jax.ShapeDtypeStruct((full, 2 * width), jnp.bfloat16),
-            plan.out_shape(),
-        ],
+        ] + plan.out_shapes(),
         compiler_params=pltpu.CompilerParams(collective_id=plan.number, has_side_effects=True, vmem_limit_bytes=58 << 20),
         cost_estimate=pl.CostEstimate(flops=40_000_000_000, bytes_accessed=30_000_000, transcendentals=8_000_000),
         name="cross_backward",
@@ -632,8 +598,9 @@
 
 
 class Plan:
-    def __init__(self, route, shapes, number, chunk=CHUNK, kind=jnp.bfloat16):
+    def __init__(self, route, shapes, number, outs=None, chunk=CHUNK, kind=jnp.bfloat16):
         self.route, self.number, self.chunk, self.kind = route, number, chunk, kind
+        self.outs = outs or [(n, 0) for n in range(len(shapes))]
         rows = min(shape[0] for shape in shapes)
         self.deep = rows >> route.bits
         self.subs = [shape[0] // rows for shape in shapes]
@@ -648,11 +615,15 @@
     def in_specs(self):
         return [pl.BlockSpec(memory_space=pl.ANY)] * self.many
 
-    def out_shape(self):
-        return jax.ShapeDtypeStruct((self.deep, self.total * 2 * self.chunk), jnp.float32)
-
-    def out_spec(self):
-        return pl.BlockSpec(self.out_shape().shape, lambda *_: (0, 0))
+    def out_shapes(self):
+        shapes = {}
+        for (out, first), sub, pairs in zip(self.outs, self.subs, self.pairs):
+            columns = first + pairs * 2 * self.chunk // sub
+            shapes[out] = (sub * self.deep, max(columns, shapes.get(out, (0, 0))[1]))
+        return [jax.ShapeDtypeStruct(shapes[out], jnp.float32) for out in sorted(shapes)]
+
+    def out_specs(self):
+        return [pl.BlockSpec(shape.shape, lambda *_: (0, 0)) for shape in self.out_shapes()]
 
     def scratch(self):
         bits = self.route.bits
@@ -664,23 +635,12 @@
         sems = [pltpu.SemaphoreType.DMA((2, SLOTS))] + [pltpu.SemaphoreType.DMA((bits, 2, SLOTS))] * 2
         return own + got + out + kept + sems
 
-    def blocks(self, sums):
-        out, at = [], 0
-        for sub, pairs in zip(self.subs, self.pairs):
-            span = pairs * 2 * self.chunk
-            block = sums[:, at : at + span]
-            at += span
-            if sub > 1:
-                block = block.reshape(-1, sub, span // sub).transpose(1, 0, 2).reshape(-1, span // sub)
-            out.append(block)
-        return out
-
 
 class Comm:
-    def __init__(self, plan, arrays, result, scratch):
+    def __init__(self, plan, arrays, results, scratch):
         route = plan.route
         bits = route.bits
-        self.plan, self.route, self.arrays, self.result = plan, route, arrays, result
+        self.plan, self.route, self.arrays, self.results = plan, route, arrays, results
         self.pairs, self.subs, self.chunk, self.total = plan.pairs, plan.subs, plan.chunk, plan.total
         self.own = scratch[0]
         self.got = scratch[1 : 1 + bits]
@@ -749,8 +709,7 @@
             came = self.got[k - 1]
             if k == route.bits:
                 total = held[slot, kind].astype(jnp.float32) + came[slot, kind].astype(jnp.float32)
-                at = pl.multiple_of((2 * u + kind) * self.chunk, self.chunk)
-                self.result[:, pl.ds(at, self.chunk)] = total
+                self.store(u, kind, total)
                 continue
             bit = route.orders[kind][k]
             at = route.left(kind, k).index(bit)
@@ -763,6 +722,21 @@
             ours = where(me)
             self.kept[k][slot, kind] = held[ours].astype(jnp.float32) + came[ours].astype(jnp.float32)
 
+    def store(self, u, kind, value):
+        first, deep = 0, self.plan.deep
+        for n, pairs in enumerate(self.pairs):
+            out, column = self.plan.outs[n]
+            across = pairs // self.subs[n]
+
+            @pl.when((u >= first) & (u < first + pairs))
+            def _():
+                pair = u - first
+                at = pl.multiple_of(column + (2 * lax.rem(pair, across) + kind) * self.chunk, self.chunk)
+                rows = pl.ds(pl.multiple_of(pair // across * deep, deep), deep)
+                self.results[out][rows, pl.ds(at, self.chunk)] = value
+
+            first += pairs
+
     def step(self, t):
         @pl.when(t < self.total)
         def _():
@@ -785,73 +759,69 @@
 
 
 class Handing:
-    def __init__(self, size, count, wraps, source, target, sems):
-        self.size, self.count, self.wraps = size, count, wraps
+    def __init__(self, shifts, pieces, source, target, sems):
+        self.shifts, self.pieces = shifts, pieces
         self.source, self.target, self.sems = source, target, sems
 
-    def copies(self):
-        z = lax.axis_index("seq")
-        for k in range(1, self.count + 1):
-            copy = pltpu.make_async_remote_copy(
-                src_ref=self.source.at[k - 1],
-                dst_ref=self.target.at[k - 1],
-                send_sem=self.sems.at[0, k - 1],
-                recv_sem=self.sems.at[1, k - 1],
-                device_id={"seq": lax.rem(z - k + self.size, self.size)},
+    def copies(self, piece):
+        z, size = lax.axis_index("seq"), lax.axis_size("seq")
+        deep = self.source.shape[1] // self.pieces
+        rows = pl.ds(pl.multiple_of(piece * deep, deep), deep)
+        for n, shift in enumerate(self.shifts):
+            yield pltpu.make_async_remote_copy(
+                src_ref=self.source.at[n, rows],
+                dst_ref=self.target.at[n, rows],
+                send_sem=self.sems.at[0, n, piece],
+                recv_sem=self.sems.at[1, n, piece],
+                device_id={"seq": lax.rem(z - shift + size, size)},
                 device_id_type=pl.DeviceIdType.MESH,
             )
-            yield copy, z >= k, z + k < self.size
-
-    def start(self):
-        for copy, sends, _ in self.copies():
-            if self.wraps:
+
+    def step(self, t):
+        @pl.when((t > 0) & (t <= self.pieces))
+        def _():
+            for copy in self.copies(t - 1):
+                copy.wait()
+
+        @pl.when(t < self.pieces)
+        def _():
+            for copy in self.copies(t):
                 copy.start()
-            else:
-                pl.when(sends)(copy.start)
-
-    def wait(self):
-        for copy, sends, gets in self.copies():
-            if self.wraps:
-                copy.wait()
-            else:
-                pl.when(sends)(copy.wait_send)
-                pl.when(gets)(copy.wait_recv)
-
-
-def handing_scratch(count):
-    return [pltpu.SemaphoreType.DMA((2, count))]
-
-
-def scatter_kernel(plan, few, size, *refs):
-    many = plan.many
+
+
+def handing_scratch(count, pieces):
+    return [pltpu.SemaphoreType.DMA((2, count, pieces))]
+
+
+def scatter_kernel(plan, few, shifts, *refs):
+    many, outs = plan.many, len(plan.out_shapes())
     arrays, small, handed = refs[:many], refs[many], refs[many + 1]
-    result, small_result, got = refs[many + 2 : many + 5]
-    scratch = refs[many + 5 : -1]
+    results, small_result, got = refs[many + 2 : many + 2 + outs], refs[many + 2 + outs], refs[many + 3 + outs]
+    scratch = refs[many + 4 + outs : -1]
     half = len(scratch) // 2
-    comm = Comm(plan, arrays, result, scratch[:half])
-    other = Comm(few, [small], small_result, scratch[half:])
-    hand = Handing(size, handed.shape[0], False, handed, got, refs[-1])
+    comm = Comm(plan, arrays, results, scratch[:half])
+    other = Comm(few, [small], [small_result], scratch[half:])
+    hand = Handing(shifts, 8, handed, got, refs[-1])
     comm.barrier()
-    hand.start()
 
     def body(t, _):
+        hand.step(t)
         other.step(t)
         comm.step(t)
         return 0
 
     lax.fori_loop(0, plan.iterations, body, 0)
-    hand.wait()
-
-
-def scatter_sums(plan, few, size, arrays, small, handed):
+
+
+def scatter_sums(plan, few, shifts, arrays, small, handed):
     anywhere = pl.BlockSpec(memory_space=pl.ANY)
     return pl.pallas_call(
-        functools.partial(scatter_kernel, plan, few, size),
+        functools.partial(scatter_kernel, plan, few, shifts),
         grid=(1,),
         in_specs=plan.in_specs() + few.in_specs() + [anywhere],
-        out_specs=[plan.out_spec(), few.out_spec(), anywhere],
-        out_shape=[plan.out_shape(), few.out_shape(), jax.ShapeDtypeStruct(handed.shape, handed.dtype)],
-        scratch_shapes=plan.scratch() + few.scratch() + handing_scratch(handed.shape[0]),
+        out_specs=plan.out_specs() + few.out_specs() + [anywhere],
+        out_shape=plan.out_shapes() + few.out_shapes() + [jax.ShapeDtypeStruct(handed.shape, handed.dtype)],
+        scratch_shapes=plan.scratch() + few.scratch() + handing_scratch(len(shifts), 8),
         compiler_params=pltpu.CompilerParams(
             collective_id=plan.number, has_side_effects=True, vmem_limit_bytes=56 << 20
         ),
@@ -861,49 +831,160 @@
 
 
 def gelu_parts(x):
-    u = jnp.abs(x) * (0.5**0.5)
-    t = 1.0 / (1.0 + 0.5 * u)
-    poly = jnp.float32(0.17087277)
-    for coef in (-0.82215223, 1.48851587, -1.13520398, 0.27886807, -0.18628806, 0.09678418, 0.37409196, 1.00002368, -1.26551223):
-        poly = poly * t + coef
-    square = u * u
-    half = 0.5 * t * jnp.exp(poly - square)
+    t = 1.0 / (1.0 + jnp.abs(x) * (0.43 * 0.5**0.5))
+    poly = jnp.float32(0.5 * 0.0709100743822703)
+    for coef in (
+        -0.2990317761502629, 0.3647352526676159, -0.06881910419857572, 0.23820862557883588,
+        0.2074695458910066, 0.24398848761768033, 0.2425387164715943,
+    ):
+        poly = poly * t + 0.5 * coef
+    bell = jnp.exp(x * x * -0.5)
+    half = poly * t * bell
     below = jnp.where(x >= 0, 1.0 - half, half)
-    dense = jnp.exp(-square) * (1.0 / math.sqrt(2.0 * math.pi))
-    return x * below, below + x * dense
-
-
-def up_kernel(x_ref, w_ref, b_ref, act_ref, slope_ref):
+    return x * below, below + x * (bell * (1.0 / math.sqrt(2.0 * math.pi)))
+
+
+def row_mean(x):
+    return jnp.mean(x, axis=1, keepdims=True)
+
+
+def column_sum(x):
+    return jnp.sum(x, axis=0, keepdims=True)
+
+
+def norm_back(upstream, unit, scale_inv, gain):
+    along = upstream * gain
+    return scale_inv * (along - row_mean(along) - unit * row_mean(along * unit))
+
+
+def row_blocks(rows):
+    return [slice(r, r + TILE) for r in range(0, rows, TILE)]
+
+
+def mlp_fwd_kernel(x_ref, wu_ref, bu_ref, wd_ref, bd_ref, hidden_ref, gain_ref, shift_ref, cot_ref,
+                   act_ref, slope_ref, result_ref, grad_ref, low_ref, sums_ref, acc):
+    j = pl.program_id(0)
     rows = x_ref.shape[0]
-    step = 256 if rows % 256 == 0 else TILE
+
+    @pl.when(j == 0)
+    def _():
+        acc[...] = jnp.zeros_like(acc)
+
+    step = 3 * TILE if rows % (3 * TILE) == 0 else TILE
     for r in range(0, rows, step):
-        pre = dot(x_ref[r : r + step, :], w_ref[...], 1, 0) + b_ref[...]
+        at = slice(r, r + step)
+        pre = halves(x_ref[at, :], wu_ref[...], 1, 0) + bu_ref[...]
         value, slope = gelu_parts(pre)
-        act_ref[r : r + step, :] = value.astype(jnp.bfloat16)
-        slope_ref[r : r + step, :] = slope.astype(jnp.bfloat16)
-
-
-def up_gelu(x, w, b):
+        value = value.astype(jnp.bfloat16)
+        act_ref[at, :] = value
+        slope_ref[at, :] = slope.astype(jnp.bfloat16)
+        acc[at, :] += halves(value, wd_ref[...], 1, 0)
+
+    @pl.when(j == pl.num_programs(0) - 1)
+    def _():
+        sums_ref[...] = jnp.zeros_like(sums_ref)
+        for at in row_blocks(rows):
+            hidden = hidden_ref[at, :] + (acc[at, :] + bd_ref[...])
+            centre = hidden - row_mean(hidden)
+            scale_inv = lax.rsqrt(row_mean(centre * centre) + 1e-05)
+            unit = centre * scale_inv
+            result_ref[at, :] = (unit * gain_ref[...] + shift_ref[...]).astype(jnp.bfloat16)
+            upstream = cot_ref[at, :].astype(jnp.float32)
+            grad = norm_back(upstream, unit, scale_inv, gain_ref[...])
+            grad_ref[at, :] = grad
+            low_ref[at, :] = grad.astype(jnp.bfloat16)
+            sums_ref[0:1, :] += column_sum(upstream * unit)
+            sums_ref[1:2, :] += column_sum(upstream)
+            sums_ref[2:3, :] += column_sum(grad)
+
+
+HIDDEN_BLOCK = 512
+
+
+def mlp_forward(x, wu, bu, wd, bd, hidden, gain, shift, cot):
     tokens, width = x.shape
-    hidden = w.shape[1]
-    block = 512
-    out = pl.BlockSpec((tokens, block), lambda j: (0, j))
+    inner = wu.shape[1]
+    block = HIDDEN_BLOCK
+    full = lambda r, c: pl.BlockSpec((r, c), lambda j: (0, 0))
+    across = pl.BlockSpec((tokens, block), lambda j: (0, j))
     return pl.pallas_call(
-        up_kernel,
-        grid=(hidden // block,),
+        mlp_fwd_kernel,
+        grid=(inner // block,),
         in_specs=[
-            pl.BlockSpec((tokens, width), lambda j: (0, 0)),
-            pl.BlockSpec((width, block), lambda j: (0, j)),
-            pl.BlockSpec((1, block), lambda j: (0, j)),
+            full(tokens, width), pl.BlockSpec((width, block), lambda j: (0, j)), pl.BlockSpec((1, block), lambda j: (0, j)),
+            pl.BlockSpec((block, width), lambda j: (j, 0)), full(1, width), full(tokens, width), full(1, width),
+            full(1, width), full(tokens, width),
         ],
-        out_specs=[out, out],
-        out_shape=[jax.ShapeDtypeStruct((tokens, hidden), jnp.bfloat16)] * 2,
-        compiler_params=pltpu.CompilerParams(vmem_limit_bytes=40 << 20),
-        cost_estimate=pl.CostEstimate(
-            flops=2 * tokens * width * hidden * 3, bytes_accessed=22_000_000, transcendentals=6_000_000
-        ),
-        name="up_gelu",
-    )(x, w, b.reshape(1, hidden))
+        out_specs=[across, across, full(tokens, width), full(tokens, width), full(tokens, width), full(8, width)],
+        out_shape=[
+            jax.ShapeDtypeStruct((tokens, inner), jnp.bfloat16), jax.ShapeDtypeStruct((tokens, inner), jnp.bfloat16),
+            jax.ShapeDtypeStruct((tokens, width), jnp.bfloat16), jax.ShapeDtypeStruct((tokens, width), jnp.float32),
+            jax.ShapeDtypeStruct((tokens, width), jnp.bfloat16), jax.ShapeDtypeStruct((8, width), jnp.float32),
+        ],
+        scratch_shapes=[pltpu.VMEM((tokens, width), jnp.float32)],
+        compiler_params=pltpu.CompilerParams(vmem_limit_bytes=56 << 20),
+        cost_estimate=pl.CostEstimate(flops=4 * tokens * width * inner, bytes_accessed=50_000_000, transcendentals=6_000_000),
+        name="mlp_forward",
+    )(x, wu, bu.reshape(1, -1), wd, bd.reshape(1, -1), hidden, gain.reshape(1, -1), shift.reshape(1, -1), cot)
+
+
+def mlp_bwd_kernel(low_ref, wd_ref, slope_ref, act_ref, x_ref, wu_ref, grad_ref, unit_ref, inv_ref, gain_ref,
+                   up_ref, down_ref, bias_ref, two_ref, two_low_ref, sums_ref, xt, acc):
+    j = pl.program_id(0)
+    rows = x_ref.shape[0]
+
+    @pl.when(j == 0)
+    def _():
+        acc[...] = jnp.zeros_like(acc)
+        for c in range(0, x_ref.shape[1], TILE):
+            xt[c : c + TILE, :] = x_ref[:, c : c + TILE].T
+
+    grad = dot(low_ref[...], wd_ref[...], 1, 1).astype(jnp.bfloat16).astype(jnp.float32)
+    grad = grad * slope_ref[...].astype(jnp.float32)
+    bias_ref[...] = column_sum(grad)
+    grad = grad.astype(jnp.bfloat16)
+    acc[...] += dot(grad, wu_ref[...], 1, 1)
+    up_ref[...] = dot(xt[...], grad, 1, 0).astype(jnp.bfloat16)
+    down_ref[...] = dot(act_ref[...].T, low_ref[...], 1, 0).astype(jnp.bfloat16)
+
+    @pl.when(j == pl.num_programs(0) - 1)
+    def _():
+        sums_ref[...] = jnp.zeros_like(sums_ref)
+        for at in row_blocks(rows):
+            upstream = grad_ref[at, :] + acc[at, :].astype(jnp.bfloat16).astype(jnp.float32)
+            unit = unit_ref[at, :]
+            two = norm_back(upstream, unit, inv_ref[at, :], gain_ref[...])
+            two_ref[at, :] = two
+            two_low_ref[at, :] = two.astype(jnp.bfloat16)
+            sums_ref[0:1, :] += column_sum(upstream * unit)
+            sums_ref[1:2, :] += column_sum(upstream)
+
+
+def mlp_backward(low, wd, slope, act, x, wu, grad, unit, inv, gain):
+    tokens, width = x.shape
+    inner = wu.shape[1]
+    block = HIDDEN_BLOCK
+    full = lambda r, c: pl.BlockSpec((r, c), lambda j: (0, 0))
+    across = lambda r: pl.BlockSpec((r, block), lambda j: (0, j))
+    down = pl.BlockSpec((block, width), lambda j: (j, 0))
+    return pl.pallas_call(
+        mlp_bwd_kernel,
+        grid=(inner // block,),
+        in_specs=[
+            full(tokens, width), down, across(tokens), across(tokens), full(tokens, width), across(width),
+            full(tokens, width), full(tokens, width), full(tokens, 1), full(1, width),
+        ],
+        out_specs=[across(width), down, across(1), full(tokens, width), full(tokens, width), full(8, width)],
+        out_shape=[
+            jax.ShapeDtypeStruct((width, inner), jnp.bfloat16), jax.ShapeDtypeStruct((inner, width), jnp.bfloat16),
+            jax.ShapeDtypeStruct((1, inner), jnp.float32), jax.ShapeDtypeStruct((tokens, width), jnp.float32),
+            jax.ShapeDtypeStruct((tokens, width), jnp.bfloat16), jax.ShapeDtypeStruct((8, width), jnp.float32),
+        ],
+        scratch_shapes=[pltpu.VMEM((width, tokens), jnp.bfloat16), pltpu.VMEM((tokens, width), jnp.float32)],
+        compiler_params=pltpu.CompilerParams(vmem_limit_bytes=58 << 20),
+        cost_estimate=pl.CostEstimate(flops=8 * tokens * width * inner, bytes_accessed=70_000_000, transcendentals=0),
+        name="mlp_backward",
+    )(low, wd, slope, act, x, wu, grad, unit, inv, gain.reshape(1, -1))
 
 
 def normalize(hidden, gain, shift):
@@ -974,6 +1055,7 @@
         passing = lax.ppermute(passing, "seq", up_chain)
         pieces.insert(0, passing)
     halo = jnp.concatenate(pieces, axis=0)
+    extended = jnp.concatenate([halo, flat], axis=0)
     own_source = encoded.reshape(local, width)
     waiting, halo = lax.optimization_barrier((own_source, halo))
     sources = [own_source] + [
@@ -1019,32 +1101,27 @@
     cross_mix, cross_weights = cross_forward(low_key, count, cross_q, source_kv, doc, source_aug)
     hidden_two, unit_two, inv_two = normalize(hidden_one + mm(cross_mix, cross_output), norm_gain[1], norm_shift[1])
     low_two = hidden_two.astype(bf16)
-    activated, slope = up_gelu(low_two, up_weight, up_bias)
-    branch_three = mm(activated, down_weight) + down_bias
-    result, unit_three, inv_three = normalize(hidden_two + branch_three, norm_gain[2], norm_shift[2])
-
-    three_grad, gain_three, shift_three = normalize_back(
-        cotangent.reshape(tokens, width).astype(f32), unit_three, inv_three, norm_gain[2]
+    activated, slope, result, three_grad, three_low, three_sums = mlp_forward(
+        low_two, up_weight, up_bias, down_weight, down_bias, hidden_two, norm_gain[2], norm_shift[2],
+        cotangent.reshape(tokens, width),
     )
-    three_low = three_grad.astype(bf16)
-    down_bias_grad = jnp.sum(three_grad, axis=0)
-    down_part = wgrad(activated, three_low)
-    pre_grad = mm_t(three_low, down_weight).astype(bf16).astype(f32) * slope.astype(f32)
-    up_bias_grad = jnp.sum(pre_grad, axis=0)
-    pre_low = pre_grad.astype(bf16)
-    up_part = wgrad(low_two, pre_low)
-    hidden_two_grad = three_grad + mm_t(pre_low, up_weight).astype(bf16).astype(f32)
-    two_grad, gain_two, shift_two = normalize_back(hidden_two_grad, unit_two, inv_two, norm_gain[1])
-    two_low = two_grad.astype(bf16)
+    gain_three, shift_three, down_bias_grad = three_sums[0], three_sums[1], three_sums[2]
+
+    up_part, down_part, up_bias_grad, two_grad, two_low, two_sums = mlp_backward(
+        three_low, down_weight, slope, activated, low_two, up_weight, three_grad, unit_two, inv_two, norm_gain[1]
+    )
+    gain_two, shift_two = two_sums[0], two_sums[1]
+    up_bias_grad = up_bias_grad.reshape(-1)
     cross_up = mm_t(two_low, cross_output).astype(bf16)
     wide = [up_part, down_part]
     wide_plan = Plan(route, [a.shape for a in wide], 0)
-    query_low, source_low, wide_sums = cross_backward(
+    query_low, source_low, up_grad, down_grad = cross_backward(
         wide_plan, wide, cross_q, source_kv, cross_mix, cross_up, cross_weights
     )
-    up_grad, down_grad = wide_plan.blocks(wide_sums)
     source_back = mm_t(source_low, cross_key_value)
-    back_low = source_back[local:].astype(bf16).reshape(size - 1, local, width)
+    far = size // 2
+    shifts = [k for k in range(1, size) if k != far]
+    block = lambda k: source_back[k * local : (k + 1) * local].astype(bf16)
     hidden_one_grad = two_grad + mm_t(query_low, cross_query).astype(bf16).astype(f32)
     one_grad, gain_one, shift_one = normalize_back(hidden_one_grad, unit_one, inv_one, norm_gain[0])
     one_low = one_grad.astype(bf16)
@@ -1056,14 +1133,21 @@
         wgrad(self_mix, one_low),
     ]
     square_plan = Plan(route, [a.shape for a in square], 1)
-    proj_low, halo_low, table_low, square_sums, came = self_backward(
-        square_plan, square, back_low, proj, halo_kv, hot, self_mix, self_up, self_weights
+    query_grad, kv_low, table_low, came, *square_sums = self_backward(
+        square_plan, square, shifts, jnp.stack([block(k) for k in shifts]), proj, halo_kv, hot, self_mix, self_up, self_weights
     )
-    cross_kv_grad, cross_out_grad, cross_query_grad, self_out_grad = square_plan.blocks(square_sums)
-    encoded_grad = source_back[:local] + jnp.sum(came.astype(f32), axis=0)
-    halo_back = mm_t(halo_low, query_key_value[:, width:]).astype(bf16)
-    handed = halo_back.reshape(hops, local, width)[::-1]
-    back = mm_t(proj_low, query_key_value) + mm_t(table_low, bucket_weight)
+    cross_kv_grad, cross_out_grad, cross_query_grad, self_out_grad = square_sums
+    halo_back = mm_t(kv_low[:HALO], query_key_value[:, width:]).astype(bf16)
+    returned = []
+    for k in range(1, hops + 1):
+        piece = halo_back[HALO - k * local : HALO - (k - 1) * local]
+        returned.append(lax.ppermute(piece, "seq", [(i, i - k) for i in range(k, size)]))
+    query_late, kv_late, table_late = lax.optimization_barrier((query_grad, kv_low, table_low, halo_back))[:3]
+    back = mm_t(query_late, query_key_value[:, :width]) + mm_t(kv_late[HALO:], query_key_value[:, width:])
+    back = (back + mm_t(table_late, bucket_weight)).reshape(streams, local, width)
+    passing = sum(got.astype(f32) for got in returned)
+    back = jnp.concatenate([back[:1] + passing[None], back[1:]], axis=0).reshape(tokens, width)
+    inputs_grad = (one_grad + back.astype(bf16).astype(f32)).astype(bf16)
     devices = parts * size
     gains = jnp.stack([gain_one, gain_two, gain_three]).reshape(3, devices, -1).transpose(1, 0, 2)
     shifts = jnp.stack([shift_one, shift_two, shift_three]).reshape(3, devices, -1).transpose(1, 0, 2)
@@ -1080,28 +1164,23 @@
     used = small.shape[1]
     small = jnp.pad(small, ((0, 0), (0, 16 * TILE - used))).reshape(devices * 8, 2 * TILE)
     arrays = [
-        wgrad(flat, proj_low[:, :width]),
-        (dot(flat, proj_low[:, width:], 0, 0) + dot(halo, halo_low, 0, 0)).astype(bf16),
-        wgrad(flat, table_low),
+        wgrad(flat, query_late),
+        wgrad(extended, kv_late),
+        wgrad(flat, gate(table_late, inputs_grad)),
     ]
-    plan = Plan(route, [a.shape for a in arrays], 2)
-    few = Plan(route, [small.shape], 2, TILE, f32)
-    sums, small, returned = scatter_sums(plan, few, size, arrays, small, handed)
-    back = back.reshape(streams, local, width)
-    behind = (jnp.arange(1, hops + 1, dtype=jnp.int32) + z < size)[:, None, None]
-    passing = jnp.sum(jnp.where(behind, returned.astype(f32), 0.0), axis=0)
-    back = jnp.concatenate([back[:1] + passing[None], back[1:]], axis=0).reshape(tokens, width)
-    inputs_grad = one_grad + back.astype(bf16).astype(f32)
-    q_grad, kv_grad, bucket_grad = plan.blocks(sums)
+    plan = Plan(route, [a.shape for a in arrays], 2, [(0, 0), (0, width), (1, 0)])
+    few = Plan(route, [small.shape], 2, chunk=TILE, kind=f32)
+    qkv_grad, bucket_grad, small, last_came = scatter_sums(plan, few, [far], arrays, small, block(far)[None])
+    encoded_grad = source_back[:local] + jnp.sum(came.astype(f32), axis=0) + last_came[0].astype(f32)
     small = small.reshape(-1)
     wide_each = up_bias_grad.shape[0] // devices
     cuts = [wide_each, wide_each + each, wide_each + 4 * each, used]
     up_bias_grad, down_bias_grad, gains, shifts, _ = jnp.split(small, cuts)
     return (
-        result.astype(bf16).reshape(inputs.shape),
-        inputs_grad.astype(bf16).reshape(inputs.shape),
+        result.reshape(inputs.shape),
+        inputs_grad.reshape(inputs.shape),
         encoded_grad.astype(bf16).reshape(encoded.shape),
-        jnp.concatenate([q_grad, kv_grad], axis=1),
+        qkv_grad,
         bucket_grad,
         self_out_grad,
         cross_query_grad,

time: 584 us -> 553 us (0.947)
  matrix products: 154 us -> 94.2 us
  Pallas kernels: 350 us -> 370 us
  waiting for transfers between devices: 10.7 us -> 24.3 us
    pallas_call x3 -> x4, Pallas kernels: 175 us -> 213 us  [the longest x1 82.4 us: self_backward(): pl.pallas_call(functools.partial(self_bwd_kernel, local // TILE, plan, sh...]
    dot_general x9 -> x8, matrix products: 62 us -> 36.4 us  [mm_t(): lax.dot_general(left, right, (((1,), (1,)), ((), ())), preferred_element_...]
    dot_general x10 -> x7, matrix products: 54.1 us -> 31.6 us  [dot(): lax.dot_general(a, b, (((ca,), (cb,)), ((), ())), preferred_element_type=...]
    pallas_call x1, Pallas kernels: 40.4 us -> 23.3 us  [cross_forward(): pl.pallas_call(functools.partial(cross_fwd_kernel, local // TILE), grid_s...]
    ppermute x0 -> x2, waiting for transfers between devices: none -> 14.5 us  [shards(): lax.ppermute(piece, 'seq', [(i, i - k) for i in range(k, size)])]
    dot_general x8 -> x7, matrix products: 37.7 us -> 26.2 us  [mm(): return jnp.dot(left, right, preferred_element_type=f32)]
    reduce_sum x5 -> x1, other arithmetic: 8.59 us -> 1.19 us  [shards(): jnp.sum(came.astype(f32), axis=0)]
    unnamed x130 -> x100, local copies, waits for them, and re-layouts: 8.55 us -> 13 us
  transfers between devices with their start and end apart: 5 -> 7, of which waited for: 2 -> 2; matrix products, arithmetic and copies ran while one was open for 4% -> 6% of each run, Pallas kernels for 6% -> 6%
where the time goes in v3:
time: 553 us; the launch traced here: 550 us
  Pallas kernels  370 us (67%)
  matrix products  94.2 us (17%)
  waiting for transfers between devices  24.3 us (4%)
  local copies, waits for them, and re-layouts  23.5 us (4%)
  starting transfers between devices  18.4 us (3%)
  other arithmetic  17.2 us (3%)
    pallas_call x1, Pallas kernels, cross_backward(): pl.pallas_call(functools.partial(cross_bwd_kernel, local // TILE, plan),...  103 us
    pallas_call x1, Pallas kernels, self_backward(): pl.pallas_call(functools.partial(self_bwd_kernel, local // TILE, plan, sh...  82.4 us
    pallas_call x1, Pallas kernels, scatter_sums(): pl.pallas_call(functools.partial(scatter_kernel, plan, few, shifts), grid...  56.1 us
    pallas_call x1, Pallas kernels, mlp_backward(): pl.pallas_call(mlp_bwd_kernel, grid=(inner // block,), in_specs=[full(tok...  39.5 us
    dot_general x8, matrix products, mm_t(): lax.dot_general(left, right, (((1,), (1,)), ((), ())), preferred_element_...  36.4 us
    pallas_call x1, Pallas kernels, mlp_forward(): pl.pallas_call(mlp_fwd_kernel, grid=(inner // block,), in_specs=[full(tok...  35.1 us
    dot_general x7, matrix products, dot(): lax.dot_general(a, b, (((ca,), (cb,)), ((), ())), preferred_element_type=...  31.6 us
    pallas_call x1, Pallas kernels, self_forward(): pl.pallas_call(functools.partial(self_fwd_kernel, local // TILE), grid_sp...  31.5 us
  transfers between devices with their start and end apart: 7, of which 2 were waited for; matrix products, arithmetic and copies ran while one was open for 6% of the time, Pallas kernels for 6%

profile of v3, /device:TPU:0, one launch (start us, length us, event | category | flops | bytes accessed | tf_op | source)
XLA Modules:
  0.0 549.7 jit_solution(9488260125111887598)
XLA Ops:
  0.7 1.2 slice_bitcast_fusion.3
  1.9 5.0 collective-permute-start
  9.5 7.7 %convolution_convert_fusion.q_ref.ko_ref.vo_ref = bf16[768,3072]{1,0:T(8,128)(2,1)S(1)} fusion(bf16[768,1024]{1,0:T(8,128)(2,1)} %bitcast.97, bf16[1024,3072]{1,0:T(8,128)(2,1)} %param.21), kind=kOutput, calls=%fused_computation | convolution fusion | flops 4834197504 | bytes 12582912 | tf_op jit(solution)/shard_map/dot_general | solution.py:1042
  19.6 3.8 collective-permute-start.1
  24.3 9.8 %collective-permute-done.1 = bf16[256,1024]{1,0:T(8,128)(2,1)S(1)} collective-permute-done((bf16[256,1024]{1,0:T(8,128)(2,1)S(1)}, bf16[256,1024]{1,0:T(8,128)(2,1)S(1)}, u32[]{:S(2)}, u32[]{:S(2)}) %collective-permute-start.1) | collective-permute-done | bytes 524320 | tf_op jit(solution)/shard_map/ppermute | solution.py:1055
  34.3 2.5 collective-permute-start.2
  36.8 1.3 collective-permute-start.3
  38.1 3.1 collective-permute-start.4
  41.2 2.4 fusion.8.kh_ref.vh_ref
  43.7 31.5 %self_forward.1 = (bf16[768,1024]{1,0:T(8,128)(2,1)S(1)}, bf16[4,4,768,640]{3,2,1,0:T(8,128)(2,1)}) custom-call(s32[2]{0:T(128)S(1)} %fusion.60.need_ref, bf16[768,3072]{1,0:T(8,128)(2,1)S(1)} %convolution_convert_fusion.q_ref.ko_ref.vo_ref, bf16[768,3072]{1,0:T(8,128)(2,1)S(1)} %convolution_convert_fusion.q_ref.ko_ref.vo_ref, ...), custom_call_target="tpu_custom_call" | custom-call | flops 15000000512 | bytes 20000000 | tf_op jit(solution)/shard_map/self_forward/pallas_call | solution.py:200
  75.2 1.9 fusion.87
  77.6 1.9 convolution_convert_fusion.11.q_ref
  80.4 7.1 %convolution_convert_fusion.3.k_ref.v_ref = bf16[1024,2048]{1,0:T(8,128)(2,1)} fusion(bf16[1024,2048]{1,0:T(8,128)(2,1)S(1)} %copy-done.28, bf16[256,1024]{1,0:T(8,128)(2,1)} %collective-permute-done.4, bf16[256,1024]{1,0:T(8,128)(2,1)S(1)} %collective-permute-done.3, bf16[256,1024]{1,0:T(8,128)(2,1)S(1)} %collective-permute-done.2, ...), kind=kOutput, calls=%fused_computation.3 | convolution fusion | flops 4305453056 | bytes 10485760 | tf_op jit(solution)/shard_map/dot_general | solution.py:1042
  87.5 23.3 %cross_forward.1 = (bf16[768,1024]{1,0:T(8,128)(2,1)S(1)}, bf16[4,4,768,1024]{3,2,1,0:T(8,128)(2,1)}) custom-call(s32[2]{0:T(128)S(1)} %get-tuple-element.108.lo_ref, s32[2]{0:T(128)S(1)} %get-tuple-element.107.count_ref, bf16[768,1024]{1,0:T(8,128)(2,1)S(1)} %convolution_convert_fusion.11.q_ref, bf16[1024,2048]{1,0:T(8,128)(2,1)} %convolution_convert_fusion.3.k_ref.v_ref, ...), custom_call_target="tpu_custom_call" | custom-call | flops 15000000512 | bytes 20000000 | tf_op jit(solution)/shard_map/cross_forward/pallas_call | solution.py:454
  110.9 4.2 fusion.88
  116.5 3.9 fusion.82
  120.4 35.1 %mlp_forward.1 = (bf16[768,4096]{1,0:T(8,128)(2,1)}, bf16[768,4096]{1,0:T(8,128)(2,1)}, bf16[768,1024]{1,0:T(8,128)(2,1)}, f32[768,1024]{1,0:T(8,128)}, bf16[768,1024]{1,0:T(8,128)(2,1)}, /*index=5*/f32[8,1024]{1,0:T(8,128)}) custom-call(bf16[768,1024]{1,0:T(8,128)(2,1)} %get-tuple-element.104.x_ref, bf16[1024,4096]{1,0:T(8,128)(2,1)} %wu_ref.3, ...), custom_call_target="tpu_custom_call" | custom-call | flops 12884901888 | bytes 50000000 | tf_op jit(solution)/shard_map/mlp_forward/pallas_call | solution.py:910
  155.4 39.5 %mlp_backward.1 = (bf16[1024,4096]{1,0:T(8,128)(2,1)}, bf16[4096,1024]{1,0:T(8,128)(2,1)}, f32[1,4096]{1,0:T(1,128)}, f32[768,1024]{1,0:T(8,128)}, bf16[768,1024]{1,0:T(8,128)(2,1)}, /*index=5*/f32[8,1024]{1,0:T(8,128)}) custom-call(bf16[768,1024]{1,0:T(8,128)(2,1)} %get-tuple-element.58.low_ref, bf16[4096,1024]{1,0:T(8,128)(2,1)} %wd_ref.3, ...), custom_call_target="tpu_custom_call" | custom-call | flops 25769803776 | bytes 70000000 | tf_op jit(solution)/shard_map/mlp_backward/pallas_call | solution.py:970
  195.0 5.2 convolution_convert_fusion.10.up_ref
  200.2 3.2 convolution_convert_fusion.7
  203.4 102.5 %cross_backward.1 = (bf16[768,1024]{1,0:T(8,128)(2,1)}, bf16[1024,2048]{1,0:T(8,128)(2,1)}, f32[32,4096]{1,0:T(8,128)}, f32[128,1024]{1,0:T(8,128)}) custom-call(bf16[768,1024]{1,0:T(8,128)(2,1)} %copy-done.7, bf16[1024,2048]{1,0:T(8,128)(2,1)} %convolution_convert_fusion.3.k_ref.v_ref, bf16[1024,2048]{1,0:T(8,128)(2,1)} %convolution_convert_fusion.3.k_ref.v_ref, ...), custom_call_target="tpu_custom_call" | custom-call | flops 40000000000 | bytes 30000000 | tf_op jit(solution)/shard_map/cross_backward/pallas_call | solution.py:544
  305.9 6.0 %convolution_convert_fusion.6 = bf16[1024,1024]{1,0:T(8,128)(2,1)} fusion(bf16[768,1024]{1,0:T(8,128)(2,1)} %get-tuple-element.67, f32[768,1024]{1,0:T(8,128)} %copy-done.8, f32[1024]{0:T(1024)S(1)} %bitcast.120, f32[1024]{0:T(1024)S(1)} %bitcast.110, f32[768]{0:T(1024)S(1)} %add_rsqrt_fusion.1, f32[768]{0:T(1024)S(1)} %broadcast_multiply_fusion.3), kind=kOutput, calls=%fused_computation.42 | convolution fusion | flops 1615593472 | bytes 6830080 | tf_op jit(solution)/shard_map/dot_general | solution.py:39
  311.9 2.7 multiply_reduce_fusion
  314.6 1.2 subtract_multiply_fusion
  315.9 3.2 convolution_convert_fusion.5
  319.1 3.0 convolution_convert_fusion.8.up_ref
  324.7 10.2 %fusion.89 = (bf16[1024,1024]{1,0:T(8,128)(2,1)S(1)}, f32[1024,1024]{1,0:T(8,128)}) fusion(bf16[1024,2048]{1,0:T(8,128)(2,1)} %get-tuple-element.69, bf16[1024,2048]{1,0:T(8,128)(2,1)} %param.25), kind=kOutput, calls=%fused_computation.204 | convolution fusion | flops 4296015872 | bytes 14680064 | tf_op jit(solution)/shard_map/dot_general | solution.py:1045
  335.8 1.1 pad_maximum_fusion.3.refs_4_
  336.9 7.3 %convolution_convert_fusion.2 = bf16[1024,2048]{1,0:T(8,128)(2,1)} fusion(bf16[1024,2048]{1,0:T(8,128)(2,1)S(1)} %copy-done.39, bf16[256,1024]{1,0:T(8,128)(2,1)} %collective-permute-done.4, bf16[256,1024]{1,0:T(8,128)(2,1)S(1)} %copy-done.36, bf16[256,1024]{1,0:T(8,128)(2,1)S(1)} %copy-done.34, bf16[256,1024]{1,0:T(8,128)(2,1)S(1)} %bitcast.132), kind=kOutput, calls=%fused_computation.2 | convolution fusion | flops 4305453056 | bytes 10485760 | tf_op jit(solution)/shard_map/dot_general | solution.py:39
  344.2 82.4 %self_backward.1 = (bf16[768,1024]{1,0:T(8,128)(2,1)}, bf16[1280,2048]{1,0:T(8,128)(2,1)}, bf16[768,512]{1,0:T(8,128)(2,1)}, bf16[2,256,1024]{2,1,0:T(8,128)(2,1...) custom-call(bf16[768,3072]{1,0:T(8,128)(2,1)} %copy-done.6, ...), custom_call_target="tpu_custom_call" | custom-call | flops 40000000000 | bytes 30000000 | tf_op jit(solution)/shard_map/self_backward/pallas_call | solution.py:349
  426.6 5.3 fusion.21
  432.0 5.4 fusion
  437.4 3.5 fusion.18
  441.0 1.3 collective-permute-start.5
  442.3 1.4 collective-permute-start.6
  445.0 7.8 %convolution_convert_fusion.1 = bf16[1024,2048]{1,0:T(8,128)(2,1)} fusion(bf16[1280,2048]{1,0:T(8,128)(2,1)S(1)} %copy-done.40, bf16[768,1024]{1,0:T(8,128)(2,1)S(1)} %bitcast.100, bf16[256,1024]{1,0:T(8,128)(2,1)S(1)} %copy-done.17, bf16[256,1024]{1,0:T(8,128)(2,1)S(1)} %copy-done.19), kind=kOutput, calls=%fused_computation.1 | convolution fusion | flops 5378670592 | bytes 12058624 | tf_op jit(solution)/shard_map/dot_general | solution.py:39
  452.8 1.2 convert_reduce_fusion
  454.9 3.2 convolution_convert_fusion.4
  458.1 14.5 %collective-permute-done.6 = bf16[256,1024]{1,0:T(8,128)(2,1)S(1)} collective-permute-done((bf16[256,1024]{1,0:T(8,128)(2,1)S(1)}, bf16[256,1024]{1,0:T(8,128)(2,1)S(1)}, u32[]{:S(2)}, u32[]{:S(2)}) %collective-permute-start.6) | collective-permute-done | bytes 524320 | tf_op jit(solution)/shard_map/ppermute | solution.py:1144
  473.0 1.8 fusion.6
  475.8 1.3 copy.42
  477.1 56.1 %weight_sums.1 = (f32[32,3072]{1,0:T(8,128)}, f32[32,512]{1,0:T(8,128)}, f32[8,256]{1,0:T(8,128)}, bf16[1,256,1024]{2,1,0:T(8,128)(2,1)}) custom-call(bf16[2,2,2,2,2,32,1024]{6,5,4,3,2,1,0:T(8,128)(2,1)} %bitcast.144, bf16[2,2,2,2,2,32,2048]{6,5,4,3,2,1,0:T(8,128)(2,1)} %bitcast.139, bf16[2,2,2,2,2,32,512]{6,5,4,3,2,1,0:T(8,128)(2,1)} %bitcast.95, ...), custom_call_target="tpu_custom_call" | custom-call | flops 20000000000 | bytes 60000000 | tf_op jit(solution)/shard_map/weight_sums/pallas_call | solution.py:818
  536.4 2.6 fusion.33
  540.3 1.6 copy.59
  541.9 1.6 copy.60
  543.5 1.7 copy.61
  545.2 1.6 copy.62
  546.7 1.9 copy.63
  (168 shorter events, 21.1 us)
Async XLA Ops:
  0.6 76.9 %copy-start = (bf16[1024,1024]{1,0:T(8,128)(2,1)S(1)}, bf16[1024,1024]{1,0:T(8,128)(2,1)}, u32[]{:S(2)}) copy-start(bf16[1024,1024]{1,0:T(8,128)(2,1)} %param.24) | copy-start | bytes 6291460
  1.9 17.6 %collective-permute-start = (bf16[256,1024]{1,0:T(8,128)(2,1)S(1)}, bf16[256,1024]{1,0:T(8,128)(2,1)S(1)}, u32[]{:S(2)}, u32[]{:S(2)}) collective-permute-start(bf16[256,1024]{1,0:T(8,128)(2,1)S(1)} %slice_bitcast_fusion.3), channel_id=1, source_target_pairs={{0,1},{1,2},{2,3},{4,5},{5,6},{6,7},{8,9},{9,10},{10,11},{12,13},{... | collective-permute-start | bytes 1572872 | tf_op jit(solution)/shard_map/ppermute | solution.py:1055
  9.5 7.8 %copy-start.26 = (f32[3,1024]{1,0:T(4,128)S(1)}, f32[3,1024]{1,0:T(4,128)}, u32[]{:S(2)}) copy-start(f32[3,1024]{1,0:T(4,128)} %param.32) | copy-start | bytes 36868
  9.5 7.8 %copy-start.27 = (f32[3,1024]{1,0:T(4,128)S(1)}, f32[3,1024]{1,0:T(4,128)}, u32[]{:S(2)}) copy-start(f32[3,1024]{1,0:T(4,128)} %param.31) | copy-start | bytes 36868
  9.5 13.8 %copy-start.12 = (bf16[1024,512]{1,0:T(8,128)(2,1)S(1)}, bf16[1024,512]{1,0:T(8,128)(2,1)}, u32[]{:S(2)}) copy-start(bf16[1024,512]{1,0:T(8,128)(2,1)} %param.22) | copy-start | bytes 3145732
  9.5 13.8 %copy-start.21 = (bf16[1,3,256,1024]{3,2,1,0:T(8,128)(2,1)S(1)}, bf16[1,3,256,1024]{3,2,1,0:T(8,128)(2,1)}, u32[]{:S(2)}) copy-start(bf16[1,3,256,1024]{3,2,1,0:T(8,128)(2,1)} %param.17) | copy-start | bytes 4718596
  17.3 26.3 %copy-start.6 = (bf16[768,3072]{1,0:T(8,128)(2,1)}, bf16[768,3072]{1,0:T(8,128)(2,1)S(1)}, u32[]{:S(2)}) copy-start(bf16[768,3072]{1,0:T(8,128)(2,1)S(1)} %convolution_convert_fusion.q_ref.ko_ref.vo_ref) | copy-start | bytes 14155780
  17.9 98.6 %copy-start.24 = (f32[1,1024]{1,0:T(1,128)}, f32[1,1024]{1,0:T(1,128)S(1)}, u32[]{:S(2)}) copy-start(f32[1,1024]{1,0:T(1,128)S(1)} %get-tuple-element.145.gain_ref) | copy-start | bytes 12292
  18.3 22.9 %slice-start = ((s8[6291456]{0:T(1024)(128)(4,1)}), s8[4194304]{0:T(1024)(128)(4,1)S(1)}, s32[]{:S(2)}) async-start(s8[6291456]{0:T(1024)(128)(4,1)} %bitcast.125), calls=%async_computation | async-start | bytes 8388608
  19.5 14.6 %copy-start.16 = (bf16[256,1024]{1,0:T(8,128)(2,1)}, bf16[256,1024]{1,0:T(8,128)(2,1)S(1)}, u32[]{:S(2)}) copy-start(bf16[256,1024]{1,0:T(8,128)(2,1)S(1)} %collective-permute-done) | copy-start | bytes 1572868
  19.6 14.6 %collective-permute-start.1 = (bf16[256,1024]{1,0:T(8,128)(2,1)S(1)}, bf16[256,1024]{1,0:T(8,128)(2,1)S(1)}, u32[]{:S(2)}, u32[]{:S(2)}) collective-permute-start(bf16[256,1024]{1,0:T(8,128)(2,1)S(1)} %collective-permute-done), channel_id=1, source_target_pairs={{0,1},{1,2},{2,3},{4,5},{5,6},{6,7},{8,9},{9,10},{10,11},{12,13},{... | collective-permute-start | bytes 1572872 | tf_op jit(solution)/shard_map/ppermute | solution.py:1055
  23.3 10.9 %copy-start.31 = (bf16[1,256,1024]{2,1,0:T(8,128)(2,1)S(1)}, bf16[1,256,1024]{2,1,0:T(8,128)(2,1)}, u32[]{:S(2)}) copy-start(bf16[1,256,1024]{2,1,0:T(8,128)(2,1)} %param.18) | copy-start | bytes 1572868
  23.4 17.9 %slice-start.1 = ((s8[6291456]{0:T(1024)(128)(4,1)}), s8[2097152]{0:T(1024)(128)(4,1)S(1)}, s32[]{:S(2)}) async-start(s8[6291456]{0:T(1024)(128)(4,1)} %bitcast.125), calls=%async_computation.1 | async-start | bytes 4194304
  34.2 9.5 %copy-start.18 = (bf16[256,1024]{1,0:T(8,128)(2,1)}, bf16[256,1024]{1,0:T(8,128)(2,1)S(1)}, u32[]{:S(2)}) copy-start(bf16[256,1024]{1,0:T(8,128)(2,1)S(1)} %collective-permute-done.1) | copy-start | bytes 1572868
  34.3 45.2 %collective-permute-start.2 = (bf16[256,1024]{1,0:T(8,128)(2,1)S(1)}, bf16[256,1024]{1,0:T(8,128)(2,1)S(1)}, u32[]{:S(2)}, u32[]{:S(2)}) collective-permute-start(bf16[256,1024]{1,0:T(8,128)(2,1)S(1)} %bitcast.128), channel_id=1, source_target_pairs={{0,1},{1,2},{2,3},{3,0},{4,5},{5,6},{6,7},{7,4},{8,9},{9,10},{10,1... | collective-permute-start | bytes 1572872 | tf_op jit(solution)/shard_map/ppermute | solution.py:1062
  36.8 42.7 %collective-permute-start.3 = (bf16[256,1024]{1,0:T(8,128)(2,1)S(1)}, bf16[256,1024]{1,0:T(8,128)(2,1)S(1)}, u32[]{:S(2)}, u32[]{:S(2)}) collective-permute-start(bf16[256,1024]{1,0:T(8,128)(2,1)S(1)} %bitcast.129), channel_id=1, source_target_pairs={{0,2},{1,3},{2,0},{3,1},{4,6},{5,7},{6,4},{7,5},{8,10},{9,11},{10,... | collective-permute-start | bytes 1572872 | tf_op jit(solution)/shard_map/ppermute | solution.py:1062
  38.1 41.4 %collective-permute-start.4 = (bf16[256,1024]{1,0:T(8,128)(2,1)S(1)}, bf16[256,1024]{1,0:T(8,128)(2,1)}, u32[]{:S(2)}, u32[]{:S(2)}) collective-permute-start(bf16[256,1024]{1,0:T(8,128)(2,1)S(1)} %bitcast.130), channel_id=1, source_target_pairs={{0,3},{1,0},{2,1},{3,2},{4,7},{5,4},{6,5},{7,6},{8,11},{9,8},{10,9... | collective-permute-start | bytes 1572872 | tf_op jit(solution)/shard_map/ppermute | solution.py:1062
  43.6 31.5 %copy-start.5 = (bf16[512,2048]{1,0:T(8,128)(2,1)}, bf16[512,2048]{1,0:T(8,128)(2,1)S(1)}, u32[]{:S(2)}) copy-start(bf16[512,2048]{1,0:T(8,128)(2,1)S(1)} %fusion.8.kh_ref.vh_ref) | copy-start | bytes 6291460
  43.6 31.5 %copy-start.29 = (bf16[1024,1024]{1,0:T(8,128)(2,1)S(1)}, bf16[1024,1024]{1,0:T(8,128)(2,1)}, u32[]{:S(2)}) copy-start(bf16[1024,1024]{1,0:T(8,128)(2,1)} %param.23) | copy-start | bytes 6291460
  75.2 240.7 %copy-start.2 = (bf16[768,1024]{1,0:T(8,128)(2,1)}, bf16[768,1024]{1,0:T(8,128)(2,1)S(1)}, u32[]{:S(2)}) copy-start(bf16[768,1024]{1,0:T(8,128)(2,1)S(1)} %get-tuple-element.54.mix_ref) | copy-start | bytes 4718596
  77.1 33.8 %copy-start.8 = (f32[768,1024]{1,0:T(8,128)}, f32[768,1024]{1,0:T(8,128)S(1)}, u32[]{:S(2)}) copy-start(f32[768,1024]{1,0:T(8,128)S(1)} %get-tuple-element.133) | copy-start | bytes 9437188
  77.6 2.8 copy-start.28
  79.5 8.1 %copy-start.7 = (bf16[768,1024]{1,0:T(8,128)(2,1)}, bf16[768,1024]{1,0:T(8,128)(2,1)S(1)}, u32[]{:S(2)}) copy-start(bf16[768,1024]{1,0:T(8,128)(2,1)S(1)} %convolution_convert_fusion.11.q_ref) | copy-start | bytes 4718596
  79.5 8.0 %copy-start.33 = (bf16[256,1024]{1,0:T(8,128)(2,1)}, bf16[256,1024]{1,0:T(8,128)(2,1)S(1)}, u32[]{:S(2)}) copy-start(bf16[256,1024]{1,0:T(8,128)(2,1)S(1)} %collective-permute-done.2) | copy-start | bytes 1572868
  79.5 8.0 %copy-start.35 = (bf16[256,1024]{1,0:T(8,128)(2,1)}, bf16[256,1024]{1,0:T(8,128)(2,1)S(1)}, u32[]{:S(2)}) copy-start(bf16[256,1024]{1,0:T(8,128)(2,1)S(1)} %collective-permute-done.3) | copy-start | bytes 1572868
  110.9 4.2 copy-start.3
  195.0 5.2 copy-start.4
  195.0 5.2 copy-start.41
  305.9 6.0 %copy-start.9 = (f32[768,1024]{1,0:T(8,128)S(1)}, f32[768,1024]{1,0:T(8,128)}, u32[]{:S(2)}) copy-start(f32[768,1024]{1,0:T(8,128)} %copy-done.8) | copy-start | bytes 9437188
  305.9 6.0 %copy-start.37 = (f32[768,1024]{1,0:T(8,128)S(1)}, f32[768,1024]{1,0:T(8,128)}, u32[]{:S(2)}) copy-start(f32[768,1024]{1,0:T(8,128)} %get-tuple-element.62) | copy-start | bytes 9437188
  305.9 6.0 %copy-start.38 = (bf16[768,1024]{1,0:T(8,128)(2,1)S(1)}, bf16[768,1024]{1,0:T(8,128)(2,1)}, u32[]{:S(2)}) copy-start(bf16[768,1024]{1,0:T(8,128)(2,1)} %get-tuple-element.67) | copy-start | bytes 4718596
  315.9 3.2 copy-start.30
  324.7 12.2 %copy-start.39 = (bf16[1024,2048]{1,0:T(8,128)(2,1)S(1)}, bf16[1024,2048]{1,0:T(8,128)(2,1)}, u32[]{:S(2)}) copy-start(bf16[1024,2048]{1,0:T(8,128)(2,1)} %get-tuple-element.69) | copy-start | bytes 12582916
  426.6 5.4 copy-start.40
  432.0 5.4 copy-start.42
  437.4 6.4 %copy-start.13 = (bf16[1024,512]{1,0:T(8,128)(2,1)S(1)}, bf16[1024,512]{1,0:T(8,128)(2,1)}, u32[]{:S(2)}) copy-start(bf16[1024,512]{1,0:T(8,128)(2,1)} %param.22) | copy-start | bytes 3145732
  437.4 6.4 %copy-start.14 = (bf16[768,512]{1,0:T(8,128)(2,1)S(1)}, bf16[768,512]{1,0:T(8,128)(2,1)}, u32[]{:S(2)}) copy-start(bf16[768,512]{1,0:T(8,128)(2,1)} %get-tuple-element.77) | copy-start | bytes 2359300
  441.0 17.1 %collective-permute-start.5 = (bf16[256,1024]{1,0:T(8,128)(2,1)S(1)}, bf16[256,1024]{1,0:T(8,128)(2,1)S(1)}, u32[]{:S(2)}, u32[]{:S(2)}) collective-permute-start(bf16[256,1024]{1,0:T(8,128)(2,1)S(1)} %get-tuple-element.112), channel_id=1, source_target_pairs={{1,0},{2,1},{3,2},{5,4},{6,5},{7,6},{9,8},{10,9},{11,10},{13,12},{... | collective-permute-start | bytes 1572872 | tf_op jit(solution)/shard_map/ppermute | solution.py:1144
  442.3 2.7 copy-start.17
  442.3 2.7 copy-start.19
  442.3 2.7 copy-start.22
  442.3 30.2 %collective-permute-start.6 = (bf16[256,1024]{1,0:T(8,128)(2,1)S(1)}, bf16[256,1024]{1,0:T(8,128)(2,1)S(1)}, u32[]{:S(2)}, u32[]{:S(2)}) collective-permute-start(bf16[256,1024]{1,0:T(8,128)(2,1)S(1)} %get-tuple-element.113), channel_id=1, source_target_pairs={{2,0},{3,1},{6,4},{7,5},{10,8},{11,9},{14,12},{15,13},{18,16},{19,... | collective-permute-start | bytes 1572872 | tf_op jit(solution)/shard_map/ppermute | solution.py:1144
  445.0 7.8 %copy-start.11 = (bf16[2,256,1024]{2,1,0:T(8,128)(2,1)S(1)}, bf16[2,256,1024]{2,1,0:T(8,128)(2,1)}, u32[]{:S(2)}) copy-start(bf16[2,256,1024]{2,1,0:T(8,128)(2,1)} %get-tuple-element.76) | copy-start | bytes 3145732
  477.1 59.3 %copy-start.10 = (f32[256,1024]{1,0:T(8,128)S(1)}, f32[256,1024]{1,0:T(8,128)}, u32[]{:S(2)}) copy-start(f32[256,1024]{1,0:T(8,128)} %convert_reduce_fusion) | copy-start | bytes 3145732
  533.2 5.8 %copy-start.20 = (f32[32,3072]{1,0:T(8,128)S(1)}, f32[32,3072]{1,0:T(8,128)}, u32[]{:S(2)}) copy-start(f32[32,3072]{1,0:T(8,128)} %get-tuple-element.168) | copy-start | bytes 1179652
  534.0 5.7 %copy-start.23 = (f32[32,512]{1,0:T(8,128)S(1)}, f32[32,512]{1,0:T(8,128)}, u32[]{:S(2)}) copy-start(f32[32,512]{1,0:T(8,128)} %get-tuple-element.169) | copy-start | bytes 196612
  536.4 13.0 %copy-start.1 = (bf16[1024,1024]{1,0:T(8,128)(2,1)S(1)}, bf16[1024,1024]{1,0:T(8,128)(2,1)}, u32[]{:S(2)}) copy-start(bf16[1024,1024]{1,0:T(8,128)(2,1)} %param.24) | copy-start | bytes 6291460
  536.4 12.2 %copy-start.15 = (f32[128,1024]{1,0:T(8,128)S(1)}, f32[128,1024]{1,0:T(8,128)}, u32[]{:S(2)}) copy-start(f32[128,1024]{1,0:T(8,128)} %get-tuple-element.176) | copy-start | bytes 1572868
  (4 other events, 8.6 us)
